TPU v7x, 512 devices: a whole 4x8x8 slice. The times are simulated.
512 devices in a mesh: curve: 512 (over x, y, z, core).
Axes of the slice: x: 4, y: 8, z: 8, core: 2. Of those that a mesh axis runs over, the one named last changes fastest.
Arguments:
- vectors: bfloat16 [524288, 128], P('curve'), may hold values from -6 to 6
- near_self: bfloat16 [524288, 512], P('curve'), may hold values from -0.15625 to 0.15625
- near_next: bfloat16 [524288, 512], P('curve'), may hold values from -0.15625 to 0.15625
- leaf_basis: bfloat16 [524288, 256], P('curve'), may hold values from -0.25 to 0.25
- transfer_one: bfloat16 [262144, 256], P('curve'), may hold values from -0.25 to 0.25
- transfer_two: bfloat16 [65536, 256], P('curve'), may hold values from -0.25 to 0.25
- coupling_zero: bfloat16 [262144, 3, 256], P('curve'), may hold values from -0.21875 to 0.21875
- coupling_one: bfloat16 [65536, 3, 256], P('curve'), may hold values from -0.21875 to 0.21875
- coupling_two: bfloat16 [16384, 3, 256], P('curve'), may hold values from -0.21875 to 0.21875
- list_zero: int32 [1024, 3], P('curve'), may hold values from 0 to 1023, as said below
- list_one: int32 [256, 3], replicated, may hold values from 0 to 255, as said below
- list_two: int32 [64, 3], replicated, may hold values from 0 to 63, as said below
Outputs:
- product: bfloat16 [524288, 128], P('curve')
Inputs may be any that keep to these rules, and one draw needn't show every extreme that they name: `list_zero`: row c holds 3 different entries (c + d) mod 1024, each d one of -3, -2, 2, 3. `list_one`: row p holds 3 entries (p + d) mod 256 for different d among -3, -2, 2, 3. `list_two`: row q holds 3 entries (q + d) mod 64 for different d among -3, -2, 2, 3.
All inputs are finite; a program needn't handle non-finite values.
Results may differ from a plain program's by a relative error of at most 0.014.
Values may be sent and summed in bfloat16 or wider, within the bound.
No kernel may reach another device: no remote copies, remote signals or barrier semaphores. Data moves between devices by JAX's collectives and lax.ppermute only.
A program may use at most 64 MiB of HBM per device.

v0:
```python
import jax
import jax.numpy as jnp
from jax import lax
from jax.sharding import PartitionSpec as P


def swapped(value, axis, stride):
    return lax.ppermute(value, axis, [(i, i ^ 1 << stride) for i in range(lax.axis_size(axis))])


def passed_along(block, axis, distance):
    devices = range(lax.axis_size(axis))
    route = [((i - distance) % len(devices), i) for i in devices]
    return lax.ppermute(block, axis, route)


def total_pair_count(partial_value, level_bits):
    running = partial_value
    for bit_number in range(level_bits):
        running = running + swapped(running.astype(jnp.bfloat16), "curve", bit_number).astype(
            running.dtype
        )
    return running


def own_rows(totals, level_bits):
    row_count = totals.shape[0] >> level_bits
    position = lax.axis_index("curve") & (1 << level_bits) - 1
    return lax.dynamic_slice_in_dim(totals, position * row_count, row_count, 0)


def group_total(partial_value, level_bits):
    return total_pair_count(partial_value, level_bits)


def split_sum(partial_value, level_bits):
    return own_rows(group_total(partial_value, level_bits), level_bits)


def spread_rows(row_block, level_bits):
    row_count = row_block.shape[0]
    position = lax.axis_index("curve") & (1 << level_bits) - 1
    zeros_full = jnp.zeros((row_count << level_bits, row_block.shape[1]), jnp.float32)
    placed = lax.dynamic_update_slice_in_dim(
        zeros_full, row_block.astype(jnp.float32), position * row_count, 0
    )
    return group_total(placed, level_bits).astype(jnp.bfloat16)


def select_partners(stacked, distance, clusters):
    candidates = jnp.array([-3, -2, 2, 3], jnp.int32) % clusters
    matching_pairs = (distance[:, None] == candidates[None, :]).astype(jnp.int32)
    chosen_slot = jnp.argmax(matching_pairs, axis=1)
    return stacked[chosen_slot]


def upper_partners(coefficients, interaction_rows, level_bits):
    devices = lax.axis_size("curve")
    group_size = 1 << level_bits
    clusters = devices // group_size
    cluster = lax.axis_index("curve") // group_size
    received = []
    for offset in (-3, -2, 2, 3):
        received.append(passed_along(coefficients, "curve", -offset * group_size % devices))
    stacked = jnp.stack(received, 0)
    partner_row = lax.dynamic_slice_in_dim(interaction_rows, cluster, 1, 0)[0]
    return select_partners(stacked, (partner_row - cluster) % clusters, clusters)


def per_device(
    vectors,
    near_self,
    near_next,
    leaf_basis,
    transfer_one,
    transfer_two,
    coupling_zero,
    coupling_one,
    coupling_two,
    list_zero,
    list_one,
    list_two,
):
    devices = lax.axis_size("curve")
    points = near_self.shape[1]
    rank_size = leaf_basis.shape[1]
    columns = vectors.shape[1]
    leaf_points = vectors.reshape(2, points, columns)
    basis = leaf_basis.reshape(2, points, rank_size)
    leaf_coefficients = jnp.einsum(
        "imk,imr->ikr", basis, leaf_points, preferred_element_type=jnp.float32
    ).astype(jnp.bfloat16)
    lifting_step = transfer_one.reshape(2, rank_size, rank_size)
    upward_first_pass = jnp.einsum(
        "vlg,vly->gy", lifting_step, leaf_coefficients, preferred_element_type=jnp.float32
    )
    coef_one = split_sum(upward_first_pass, 1).astype(jnp.bfloat16)
    upward_two = jnp.einsum("ab,ar->br", transfer_two, coef_one, preferred_element_type=jnp.float32)
    coef_two = split_sum(upward_two, 3).astype(jnp.bfloat16)
    neighbours = []
    for shift_by in (2, 1, -1, -2):
        neighbours.append(passed_along(leaf_coefficients, "curve", shift_by))
    window = jnp.concatenate(
        [neighbours[0], neighbours[1], leaf_coefficients, neighbours[2], neighbours[3]], 0
    )
    leaf_clusters = 2 * devices
    local_leaves = jnp.arange(2, dtype=jnp.int32)
    own_leaves = 2 * lax.axis_index("curve") + local_leaves
    distance = (list_zero - own_leaves[:, None]) % leaf_clusters
    signed = jnp.where(distance > leaf_clusters // 2, distance - leaf_clusters, distance)
    chosen_leaf = window[4 + local_leaves[:, None] + signed]
    far_zero = jnp.einsum(
        "iasb,isar->ibr",
        coupling_zero.reshape(2, rank_size, -1, rank_size),
        chosen_leaf,
        preferred_element_type=jnp.float32,
    )
    far_one = jnp.einsum(
        "asb,sar->br",
        coupling_one,
        upper_partners(coef_one, list_one, 1),
        preferred_element_type=jnp.float32,
    )
    far_two = jnp.einsum(
        "asb,sar->br",
        coupling_two,
        upper_partners(coef_two, list_two, 3),
        preferred_element_type=jnp.float32,
    )
    expansion_two = group_total(far_two, 3).astype(jnp.bfloat16)
    rows_one = split_sum(far_one, 1) + jnp.einsum(
        "ab,br->ar", transfer_two, expansion_two, preferred_element_type=jnp.float32
    )
    expansion_first_level = spread_rows(rows_one.astype(jnp.bfloat16), 1)
    expansion_zero = (
        far_zero
        + jnp.einsum(
            "wou,uq->woq", lifting_step, expansion_first_level, preferred_element_type=jnp.float32
        )
    ).astype(jnp.bfloat16)
    far_field = jnp.einsum(
        "imk,ikr->imr", basis, expansion_zero, preferred_element_type=jnp.float32
    )
    self_blocks = near_self.reshape(2, points, points)
    next_blocks = near_next.reshape(2, points, points)
    following = passed_along(leaf_points[0], "curve", -1)
    ahead = jnp.stack([leaf_points[1], following], 0)
    near_field = jnp.einsum(
        "imn,inr->imr", self_blocks, leaf_points, preferred_element_type=jnp.float32
    )
    near_field = near_field + jnp.einsum(
        "imn,inr->imr", next_blocks, ahead, preferred_element_type=jnp.float32
    )
    inner_term = jnp.einsum(
        "mn,mr->nr", next_blocks[0], leaf_points[0], preferred_element_type=jnp.float32
    )
    outgoing_terms = jnp.einsum(
        "mn,mr->nr", next_blocks[1], leaf_points[1], preferred_element_type=jnp.float32
    )
    incoming = passed_along(outgoing_terms.astype(jnp.bfloat16), "curve", 1).astype(
        outgoing_terms.dtype
    )
    near_field = near_field + jnp.stack([incoming, inner_term], 0)
    return (near_field + far_field).astype(jnp.bfloat16).reshape(2 * points, columns)


def solution(mesh):
    return jax.shard_map(
        per_device,
        mesh=mesh,
        in_specs=(
            P("curve", None),
            P("curve", None),
            P("curve", None),
            P("curve", None),
            P("curve", None),
            P("curve", None),
            P("curve", None, None),
            P("curve", None, None),
            P("curve", None, None),
            P("curve", None),
            P(),
            P(),
        ),
        out_specs=P("curve", None),
        check_vma=False,
    )
```

profile of v0, /device:TPU:1, one launch (start us, length us, event | category | flops | bytes accessed | tf_op | source)
XLA Modules:
  0.0 127.7 jit_solution(16164033360380034652)
XLA Ops:
  0.0 1.6 %convolution_convert_fusion = bf16[2,256,128]{2,1,0:T(8,128)(2,1)S(1)} fusion(bf16[2,512,256]{2,1,0:T(8,128)(2,1)} %bitcast.89, bf16[2,512,128]{2,1,0:T(8,128)(2,1)} %bitcast.87), kind=kOutput, calls=%fused_computation.13 | convolution fusion | flops 67174400 | bytes 917504 | tf_op jit(solution)/shard_map/imk,imr->ikr/dot_general | solution.py:90
  1.6 4.8 %collective-permute-start.2 = (bf16[2,256,128]{2,1,0:T(8,128)(2,1)S(1)}, bf16[2,256,128]{2,1,0:T(8,128)(2,1)S(1)}, u32[]{:S(2)}, u32[]{:S(2)}) collective-permute-start(bf16[2,256,128]{2,1,0:T(8,128)(2,1)S(1)} %convolution_convert_fusion), channel_id=1, source_target_pairs={{510,0},{511,1},{0,2},{1,3},{2,4},{3,5},{4,6},{5,7},{6,8},{7,9},{8... | collective-permute-start | bytes 393224 | tf_op jit(solution)/shard_map/ppermute | solution.py:14
  6.4 1.9 %fusion.36 = (bf16[256,128]{0,1:T(8,128)(2,1)}, f32[256,128]{0,1:T(8,128)S(1)}) fusion(bf16[2,256,128]{2,1,0:T(8,128)(2,1)S(1)} %convolution_convert_fusion, bf16[2,256,256]{2,1,0:T(8,128)(2,1)} %bitcast.93), kind=kOutput, calls=%fused_computation.90 | convolution fusion | flops 33587200 | bytes 589824 | tf_op jit(solution)/shard_map/vlg,vly->gy/dot_general | solution.py:94
  8.3 5.8 %collective-permute-start.6 = (bf16[256,128]{0,1:T(8,128)(2,1)}, bf16[256,128]{0,1:T(8,128)(2,1)}, u32[]{:S(2)}, u32[]{:S(2)}) collective-permute-start(bf16[256,128]{0,1:T(8,128)(2,1)} %get-tuple-element.13), channel_id=1, source_target_pairs={{0,1},{1,0},{2,3},{3,2},{4,5},{5,4},{6,7},{7,6},{8,9},{9,8},{10,11... | collective-permute-start | bytes 196616 | tf_op jit(solution)/shard_map/ppermute | solution.py:8
  14.2 1.0 convolution_convert_fusion.1
  15.2 1.0 convolution_bitcast_fusion.2
  16.3 0.7 copy-done.9
  17.0 0.2 fusion.24
  17.2 0.6 copy-done.12
  17.8 0.7 iota_reduce_fusion.1
  18.6 0.6 copy-done.11
  19.2 0.7 iota_reduce_fusion
  19.9 0.7 copy-done.10
  20.6 0.1 compare_select_fusion
  20.7 0.1 reshape.86
  20.8 0.8 copy.51
  21.6 0.4 fusion.40
  22.0 0.1 copy.50
  22.2 0.8 fusion.19
  23.0 6.0 %collective-permute-start.7 = (bf16[128,128]{0,1:T(8,128)(2,1)S(1)}, bf16[128,128]{0,1:T(8,128)(2,1)S(1)}, u32[]{:S(2)}, u32[]{:S(2)}) collective-permute-start(bf16[128,128]{0,1:T(8,128)(2,1)S(1)} %fusion.19), channel_id=1, source_target_pairs={{506,0},{507,1},{508,2},{509,3},{510,4},{511,5},{0,6},{1,7},{2,8},... | collective-permute-start | bytes 98312 | tf_op jit(solution)/shard_map/ppermute | solution.py:14
  29.0 4.0 %collective-permute-start.8 = (bf16[128,128]{0,1:T(8,128)(2,1)S(1)}, bf16[128,128]{0,1:T(8,128)(2,1)S(1)}, u32[]{:S(2)}, u32[]{:S(2)}) collective-permute-start(bf16[128,128]{0,1:T(8,128)(2,1)S(1)} %fusion.19), channel_id=1, source_target_pairs={{508,0},{509,1},{510,2},{511,3},{0,4},{1,5},{2,6},{3,7},{4,8},{5,9... | collective-permute-start | bytes 98312 | tf_op jit(solution)/shard_map/ppermute | solution.py:14
  33.0 7.6 %collective-permute-start.9 = (bf16[128,128]{0,1:T(8,128)(2,1)S(1)}, bf16[128,128]{0,1:T(8,128)(2,1)S(1)}, u32[]{:S(2)}, u32[]{:S(2)}) collective-permute-start(bf16[128,128]{0,1:T(8,128)(2,1)S(1)} %fusion.19), channel_id=1, source_target_pairs={{4,0},{5,1},{6,2},{7,3},{8,4},{9,5},{10,6},{11,7},{12,8},{13,9},{1... | collective-permute-start | bytes 98312 | tf_op jit(solution)/shard_map/ppermute | solution.py:14
  40.6 4.6 %collective-permute-start.10 = (bf16[128,128]{0,1:T(8,128)(2,1)S(1)}, bf16[128,128]{0,1:T(8,128)(2,1)S(1)}, u32[]{:S(2)}, u32[]{:S(2)}) collective-permute-start(bf16[128,128]{0,1:T(8,128)(2,1)S(1)} %fusion.19), channel_id=1, source_target_pairs={{6,0},{7,1},{8,2},{9,3},{10,4},{11,5},{12,6},{13,7},{14,8},{15,9},... | collective-permute-start | bytes 98312 | tf_op jit(solution)/shard_map/ppermute | solution.py:14
  45.2 0.2 fusion.37
  45.4 1.9 %collective-permute-start.3 = (bf16[2,256,128]{2,1,0:T(8,128)(2,1)S(1)}, bf16[2,256,128]{2,1,0:T(8,128)(2,1)S(1)}, u32[]{:S(2)}, u32[]{:S(2)}) collective-permute-start(bf16[2,256,128]{2,1,0:T(8,128)(2,1)S(1)} %convolution_convert_fusion), channel_id=1, source_target_pairs={{511,0},{0,1},{1,2},{2,3},{3,4},{4,5},{5,6},{6,7},{7,8},{8,9},{9,1... | collective-permute-start | bytes 393224 | tf_op jit(solution)/shard_map/ppermute | solution.py:14
  47.3 1.9 %collective-permute-start.1 = (bf16[512,128]{1,0:T(8,128)(2,1)S(1)}, bf16[512,128]{1,0:T(8,128)(2,1)S(1)}, u32[]{:S(2)}, u32[]{:S(2)}) collective-permute-start(bf16[512,128]{1,0:T(8,128)(2,1)S(1)} %copy-done.13), channel_id=1, source_target_pairs={{511,0},{0,1},{1,2},{2,3},{3,4},{4,5},{5,6},{6,7},{7,8},{8,9},{9,1... | collective-permute-start | bytes 393224 | tf_op jit(solution)/shard_map/ppermute | solution.py:14
  49.3 2.8 %collective-permute-start.12 = (bf16[256,128]{0,1:T(8,128)(2,1)S(1)}, bf16[256,128]{0,1:T(8,128)(2,1)S(1)}, u32[]{:S(2)}, u32[]{:S(2)}) collective-permute-start(bf16[256,128]{0,1:T(8,128)(2,1)S(1)} %get-tuple-element.15), channel_id=1, source_target_pairs={{0,1},{1,0},{2,3},{3,2},{4,5},{5,4},{6,7},{7,6},{8,9},{9,8},{10,11... | collective-permute-start | bytes 196616 | tf_op jit(solution)/shard_map/ppermute | solution.py:8
  52.1 0.6 gather_fusion.1
  52.7 0.3 collective-permute-done.12
  52.9 1.9 %collective-permute-start.13 = (bf16[256,128]{0,1:T(8,128)(2,1)S(1)}, bf16[256,128]{0,1:T(8,128)(2,1)S(1)}, u32[]{:S(2)}, u32[]{:S(2)}) collective-permute-start(bf16[256,128]{0,1:T(8,128)(2,1)S(1)} %fusion.13), channel_id=1, source_target_pairs={{0,2},{1,3},{2,0},{3,1},{4,6},{5,7},{6,4},{7,5},{8,10},{9,11},{10,... | collective-permute-start | bytes 196616 | tf_op jit(solution)/shard_map/ppermute | solution.py:8
  54.9 0.2 fusion.39
  55.1 3.2 %collective-permute-done.13 = bf16[256,128]{0,1:T(8,128)(2,1)S(1)} collective-permute-done((bf16[256,128]{0,1:T(8,128)(2,1)S(1)}, bf16[256,128]{0,1:T(8,128)(2,1)S(1)}, u32[]{:S(2)}, u32[]{:S(2)}) %collective-permute-start.13) | collective-permute-done | bytes 65568 | tf_op jit(solution)/shard_map/ppermute | solution.py:8
  58.3 4.5 %collective-permute-start.14 = (bf16[256,128]{0,1:T(8,128)(2,1)S(1)}, bf16[256,128]{0,1:T(8,128)(2,1)S(1)}, u32[]{:S(2)}, u32[]{:S(2)}) collective-permute-start(bf16[256,128]{0,1:T(8,128)(2,1)S(1)} %get-tuple-element.9), channel_id=1, source_target_pairs={{0,4},{1,5},{2,6},{3,7},{4,0},{5,1},{6,2},{7,3},{8,12},{9,13},{10,... | collective-permute-start | bytes 196616 | tf_op jit(solution)/shard_map/ppermute | solution.py:8
  62.8 1.6 %collective-permute-done.14 = bf16[256,128]{0,1:T(8,128)(2,1)S(1)} collective-permute-done((bf16[256,128]{0,1:T(8,128)(2,1)S(1)}, bf16[256,128]{0,1:T(8,128)(2,1)S(1)}, u32[]{:S(2)}, u32[]{:S(2)}) %collective-permute-start.14) | collective-permute-done | bytes 65568 | tf_op jit(solution)/shard_map/ppermute | solution.py:8
  64.4 0.1 fusion.16
  64.5 2.7 %collective-permute-start.15 = (bf16[32,128]{0,1:T(8,128)(2,1)S(1)}, bf16[32,128]{0,1:T(8,128)(2,1)S(1)}, u32[]{:S(2)}, u32[]{:S(2)}) collective-permute-start(bf16[32,128]{0,1:T(8,128)(2,1)S(1)} %fusion.16), channel_id=1, source_target_pairs={{488,0},{489,1},{490,2},{491,3},{492,4},{493,5},{494,6},{495,7},{4... | collective-permute-start | bytes 24584 | tf_op jit(solution)/shard_map/ppermute | solution.py:14
  67.2 3.2 %collective-permute-start.16 = (bf16[32,128]{0,1:T(8,128)(2,1)S(1)}, bf16[32,128]{0,1:T(8,128)(2,1)S(1)}, u32[]{:S(2)}, u32[]{:S(2)}) collective-permute-start(bf16[32,128]{0,1:T(8,128)(2,1)S(1)} %fusion.16), channel_id=1, source_target_pairs={{496,0},{497,1},{498,2},{499,3},{500,4},{501,5},{502,6},{503,7},{5... | collective-permute-start | bytes 24584 | tf_op jit(solution)/shard_map/ppermute | solution.py:14
  70.5 7.4 %collective-permute-start.17 = (bf16[32,128]{0,1:T(8,128)(2,1)S(1)}, bf16[32,128]{0,1:T(8,128)(2,1)S(1)}, u32[]{:S(2)}, u32[]{:S(2)}) collective-permute-start(bf16[32,128]{0,1:T(8,128)(2,1)S(1)} %fusion.16), channel_id=1, source_target_pairs={{16,0},{17,1},{18,2},{19,3},{20,4},{21,5},{22,6},{23,7},{24,8},{25... | collective-permute-start | bytes 24584 | tf_op jit(solution)/shard_map/ppermute | solution.py:14
  77.9 6.2 %collective-permute-start.18 = (bf16[32,128]{0,1:T(8,128)(2,1)S(1)}, bf16[32,128]{0,1:T(8,128)(2,1)S(1)}, u32[]{:S(2)}, u32[]{:S(2)}) collective-permute-start(bf16[32,128]{0,1:T(8,128)(2,1)S(1)} %fusion.16), channel_id=1, source_target_pairs={{24,0},{25,1},{26,2},{27,3},{28,4},{29,5},{30,6},{31,7},{32,8},{33... | collective-permute-start | bytes 24584 | tf_op jit(solution)/shard_map/ppermute | solution.py:14
  84.2 0.7 constant_dynamic-update-slice_fusion.4
  84.8 5.1 %collective-permute-start.4 = (bf16[2,256,128]{2,1,0:T(8,128)(2,1)S(1)}, bf16[2,256,128]{2,1,0:T(8,128)(2,1)S(1)}, u32[]{:S(2)}, u32[]{:S(2)}) collective-permute-start(bf16[2,256,128]{2,1,0:T(8,128)(2,1)S(1)} %convolution_convert_fusion), channel_id=1, source_target_pairs={{1,0},{2,1},{3,2},{4,3},{5,4},{6,5},{7,6},{8,7},{9,8},{10,9},{11,1... | collective-permute-start | bytes 393224 | tf_op jit(solution)/shard_map/ppermute | solution.py:14
  90.0 0.1 copy.39
  90.1 5.3 %collective-permute-start.5 = (bf16[2,256,128]{2,1,0:T(8,128)(2,1)S(1)}, bf16[2,256,128]{2,1,0:T(8,128)(2,1)S(1)}, u32[]{:S(2)}, u32[]{:S(2)}) collective-permute-start(bf16[2,256,128]{2,1,0:T(8,128)(2,1)S(1)} %convolution_convert_fusion), channel_id=1, source_target_pairs={{2,0},{3,1},{4,2},{5,3},{6,4},{7,5},{8,6},{9,7},{10,8},{11,9},{12,... | collective-permute-start | bytes 393224 | tf_op jit(solution)/shard_map/ppermute | solution.py:14
  95.4 2.2 %collective-permute-start = (bf16[512,128]{0,1:T(8,128)(2,1)}, bf16[512,128]{0,1:T(8,128)(2,1)}, u32[]{:S(2)}, u32[]{:S(2)}) collective-permute-start(bf16[512,128]{0,1:T(8,128)(2,1)} %copy.51), channel_id=1, source_target_pairs={{1,0},{2,1},{3,2},{4,3},{5,4},{6,5},{7,6},{8,7},{9,8},{10,9},{11,1... | collective-permute-start | bytes 393224 | tf_op jit(solution)/shard_map/ppermute | solution.py:14
  97.7 2.0 %collective-permute-start.11 = (bf16[256,128]{0,1:T(8,128)(2,1)S(1)}, bf16[256,128]{0,1:T(8,128)(2,1)S(1)}, u32[]{:S(2)}, u32[]{:S(2)}) collective-permute-start(bf16[256,128]{0,1:T(8,128)(2,1)S(1)} %get-tuple-element.19), channel_id=1, source_target_pairs={{0,1},{1,0},{2,3},{3,2},{4,5},{5,4},{6,7},{7,6},{8,9},{9,8},{10,11... | collective-permute-start | bytes 196616 | tf_op jit(solution)/shard_map/ppermute | solution.py:8
  99.9 0.6 gather_fusion.2
  100.4 0.2 copy-done.7
  100.7 0.2 fusion.38
  100.9 2.3 %collective-permute-start.19 = (bf16[256,128]{0,1:T(8,128)(2,1)S(1)}, bf16[256,128]{0,1:T(8,128)(2,1)S(1)}, u32[]{:S(2)}, u32[]{:S(2)}) collective-permute-start(bf16[256,128]{0,1:T(8,128)(2,1)S(1)} %get-tuple-element.17), channel_id=1, source_target_pairs={{0,1},{1,0},{2,3},{3,2},{4,5},{5,4},{6,7},{7,6},{8,9},{9,8},{10,11... | collective-permute-start | bytes 196616 | tf_op jit(solution)/shard_map/ppermute | solution.py:8
  103.2 0.7 constant_dynamic-update-slice_fusion.3
  103.8 0.2 collective-permute-done.19
  104.1 3.3 %collective-permute-start.20 = (bf16[256,128]{0,1:T(8,128)(2,1)S(1)}, bf16[256,128]{0,1:T(8,128)(2,1)S(1)}, u32[]{:S(2)}, u32[]{:S(2)}) collective-permute-start(bf16[256,128]{0,1:T(8,128)(2,1)S(1)} %fusion.14), channel_id=1, source_target_pairs={{0,2},{1,3},{2,0},{3,1},{4,6},{5,7},{6,4},{7,5},{8,10},{9,11},{10,... | collective-permute-start | bytes 196616 | tf_op jit(solution)/shard_map/ppermute | solution.py:8
  107.4 0.7 constant_dynamic-update-slice_fusion.2
  108.1 1.0 collective-permute-done.20
  109.1 1.9 %collective-permute-start.21 = (bf16[256,128]{0,1:T(8,128)(2,1)S(1)}, bf16[256,128]{0,1:T(8,128)(2,1)S(1)}, u32[]{:S(2)}, u32[]{:S(2)}) collective-permute-start(bf16[256,128]{0,1:T(8,128)(2,1)S(1)} %fusion.22), channel_id=1, source_target_pairs={{0,4},{1,5},{2,6},{3,7},{4,0},{5,1},{6,2},{7,3},{8,12},{9,13},{10,... | collective-permute-start | bytes 196616 | tf_op jit(solution)/shard_map/ppermute | solution.py:8
  111.0 0.7 constant_dynamic-update-slice_fusion.1
  111.7 3.3 %collective-permute-done.21 = bf16[256,128]{0,1:T(8,128)(2,1)S(1)} collective-permute-done((bf16[256,128]{0,1:T(8,128)(2,1)S(1)}, bf16[256,128]{0,1:T(8,128)(2,1)S(1)}, u32[]{:S(2)}, u32[]{:S(2)}) %collective-permute-start.21) | collective-permute-done | bytes 65568 | tf_op jit(solution)/shard_map/ppermute | solution.py:8
  115.0 0.2 convert_dynamic-update-slice_fusion
  115.2 4.8 %collective-permute-start.22 = (bf16[256,128]{0,1:T(8,128)(2,1)S(1)}, bf16[256,128]{0,1:T(8,128)(2,1)S(1)}, u32[]{:S(2)}, u32[]{:S(2)}) collective-permute-start(bf16[256,128]{0,1:T(8,128)(2,1)S(1)} %get-tuple-element.21), channel_id=1, source_target_pairs={{0,1},{1,0},{2,3},{3,2},{4,5},{5,4},{6,7},{7,6},{8,9},{9,8},{10,11... | collective-permute-start | bytes 196616 | tf_op jit(solution)/shard_map/ppermute | solution.py:8
  120.0 0.7 constant_dynamic-update-slice_fusion
  120.7 1.8 %gather_fusion = bf16[6,256,128]{2,1,0:T(8,128)(2,1)S(1)} fusion(bf16[10,256,128]{2,1,0:T(8,128)(2,1)} %constant_dynamic-update-slice_fusion, s32[1024]{0:T(1024)S(1)} %pad_clamp_fusion.2), kind=kCustom, calls=%fused_computation | custom fusion | bytes 786456 | tf_op jit(solution)/shard_map/gather | solution.py:111
  122.5 0.9 convolution_bitcast_fusion.3
  123.5 1.8 %convolution_bitcast_fusion = f32[2,512,128]{2,1,0:T(8,128)S(1)} fusion(bf16[2,512,256]{2,1,0:T(8,128)(2,1)S(1)} %bitcast.90, f32[2,256,128]{1,2,0:T(8,128)} %convolution_bitcast_fusion.3, bf16[2,3,256,128]{3,2,1,0:T(8,128)(2,1)S(1)} %bitcast.91, bf16[2,256,3,256]{3,1,0,2:T(8,128)(2,1)} %bitcast.95), kind=kOutput, calls=%fused_computation.3 | convolution fusion | flops 167903232 | bytes 2490368 | tf_op jit(solution)/shard_map/imk,ikr->imr/dot_general | solution.py:141
  125.3 2.5 %fusion.3 = bf16[2,512,128]{2,1,0:T(8,128)(2,1)} fusion(f32[2,512,128]{2,1,0:T(8,128)S(1)} %convolution_bitcast_fusion, f32[2,512,128]{2,1,0:T(8,128)S(1)} %fusion.40, bf16[2,512,512]{2,1,0:T(8,128)(2,1)} %bitcast.92, f32[1,512,128]{2,1,0:T(8,128)} %convolution_bitcast_fusion.2, f32[1,512,128]{2,1,0:T(8,128)S(1)} %bitcast_convert_fusion, ...), kind=kOutput, calls=%fused_computation.8 | convolution fusion | flops 135004160 | bytes 3145728 | tf_op jit(solution)/shard_map/imn,inr->imr/dot_general | solution.py:151
  (62 shorter events, 0.6 us)
Async XLA Ops:
  0.0 21.6 %copy-start = (bf16[1024,512]{1,0:T(8,128)(2,1)S(1)}, bf16[1024,512]{1,0:T(8,128)(2,1)}, u32[]{:S(2)}) copy-start(bf16[1024,512]{1,0:T(8,128)(2,1)} %param.15) | copy-start | bytes 3145732
  0.0 14.2 %copy-start.3 = (bf16[1024,512]{1,0:T(8,128)(2,1)S(1)}, bf16[1024,512]{1,0:T(8,128)(2,1)}, u32[]{:S(2)}) copy-start(bf16[1024,512]{1,0:T(8,128)(2,1)} %param.16) | copy-start | bytes 3145732
  1.6 76.3 %collective-permute-start.2 = (bf16[2,256,128]{2,1,0:T(8,128)(2,1)S(1)}, bf16[2,256,128]{2,1,0:T(8,128)(2,1)S(1)}, u32[]{:S(2)}, u32[]{:S(2)}) collective-permute-start(bf16[2,256,128]{2,1,0:T(8,128)(2,1)S(1)} %convolution_convert_fusion), channel_id=1, source_target_pairs={{510,0},{511,1},{0,2},{1,3},{2,4},{3,5},{4,6},{5,7},{6,8},{7,9},{8... | collective-permute-start | bytes 393224 | tf_op jit(solution)/shard_map/ppermute | solution.py:14
  6.4 7.7 %copy-start.1 = (bf16[1024,128]{1,0:T(8,128)(2,1)S(1)}, bf16[1024,128]{1,0:T(8,128)(2,1)}, u32[]{:S(2)}) copy-start(bf16[1024,128]{1,0:T(8,128)(2,1)} %param.14) | copy-start | bytes 786436
  8.3 13.8 %collective-permute-start.6 = (bf16[256,128]{0,1:T(8,128)(2,1)}, bf16[256,128]{0,1:T(8,128)(2,1)}, u32[]{:S(2)}, u32[]{:S(2)}) collective-permute-start(bf16[256,128]{0,1:T(8,128)(2,1)} %get-tuple-element.13), channel_id=1, source_target_pairs={{0,1},{1,0},{2,3},{3,2},{4,5},{5,4},{6,7},{7,6},{8,9},{9,8},{10,11... | collective-permute-start | bytes 196616 | tf_op jit(solution)/shard_map/ppermute | solution.py:8
  16.3 0.7 copy-start.9
  16.3 0.7 copy-start.8
  17.2 0.7 copy-start.12
  18.6 0.7 copy-start.11
  19.9 0.7 copy-start.10
  22.1 23.1 %copy-start.5 = (bf16[128,256]{1,0:T(8,128)(2,1)S(1)}, bf16[128,256]{1,0:T(8,128)(2,1)}, u32[]{:S(2)}) copy-start(bf16[128,256]{1,0:T(8,128)(2,1)} %param.19) | copy-start | bytes 196612
  23.0 24.4 %copy-start.13 = (bf16[512,128]{1,0:T(8,128)(2,1)S(1)}, bf16[512,128]{1,0:T(8,128)(2,1)}, u32[]{:S(2)}) copy-start(bf16[512,128]{1,0:T(8,128)(2,1)} %convolution_convert_fusion.1) | copy-start | bytes 393220
  23.0 22.4 %collective-permute-start.7 = (bf16[128,128]{0,1:T(8,128)(2,1)S(1)}, bf16[128,128]{0,1:T(8,128)(2,1)S(1)}, u32[]{:S(2)}, u32[]{:S(2)}) collective-permute-start(bf16[128,128]{0,1:T(8,128)(2,1)S(1)} %fusion.19), channel_id=1, source_target_pairs={{506,0},{507,1},{508,2},{509,3},{510,4},{511,5},{0,6},{1,7},{2,8},... | collective-permute-start | bytes 98312 | tf_op jit(solution)/shard_map/ppermute | solution.py:14
  29.0 18.4 %collective-permute-start.8 = (bf16[128,128]{0,1:T(8,128)(2,1)S(1)}, bf16[128,128]{0,1:T(8,128)(2,1)S(1)}, u32[]{:S(2)}, u32[]{:S(2)}) collective-permute-start(bf16[128,128]{0,1:T(8,128)(2,1)S(1)} %fusion.19), channel_id=1, source_target_pairs={{508,0},{509,1},{510,2},{511,3},{0,4},{1,5},{2,6},{3,7},{4,8},{5,9... | collective-permute-start | bytes 98312 | tf_op jit(solution)/shard_map/ppermute | solution.py:14
  33.0 16.3 %collective-permute-start.9 = (bf16[128,128]{0,1:T(8,128)(2,1)S(1)}, bf16[128,128]{0,1:T(8,128)(2,1)S(1)}, u32[]{:S(2)}, u32[]{:S(2)}) collective-permute-start(bf16[128,128]{0,1:T(8,128)(2,1)S(1)} %fusion.19), channel_id=1, source_target_pairs={{4,0},{5,1},{6,2},{7,3},{8,4},{9,5},{10,6},{11,7},{12,8},{13,9},{1... | collective-permute-start | bytes 98312 | tf_op jit(solution)/shard_map/ppermute | solution.py:14
  40.6 11.5 %collective-permute-start.10 = (bf16[128,128]{0,1:T(8,128)(2,1)S(1)}, bf16[128,128]{0,1:T(8,128)(2,1)S(1)}, u32[]{:S(2)}, u32[]{:S(2)}) collective-permute-start(bf16[128,128]{0,1:T(8,128)(2,1)S(1)} %fusion.19), channel_id=1, source_target_pairs={{6,0},{7,1},{8,2},{9,3},{10,4},{11,5},{12,6},{13,7},{14,8},{15,9},... | collective-permute-start | bytes 98312 | tf_op jit(solution)/shard_map/ppermute | solution.py:14
  45.4 55.5 %collective-permute-start.3 = (bf16[2,256,128]{2,1,0:T(8,128)(2,1)S(1)}, bf16[2,256,128]{2,1,0:T(8,128)(2,1)S(1)}, u32[]{:S(2)}, u32[]{:S(2)}) collective-permute-start(bf16[2,256,128]{2,1,0:T(8,128)(2,1)S(1)} %convolution_convert_fusion), channel_id=1, source_target_pairs={{511,0},{0,1},{1,2},{2,3},{3,4},{4,5},{5,6},{6,7},{7,8},{8,9},{9,1... | collective-permute-start | bytes 393224 | tf_op jit(solution)/shard_map/ppermute | solution.py:14
  47.3 15.4 %collective-permute-start.1 = (bf16[512,128]{1,0:T(8,128)(2,1)S(1)}, bf16[512,128]{1,0:T(8,128)(2,1)S(1)}, u32[]{:S(2)}, u32[]{:S(2)}) collective-permute-start(bf16[512,128]{1,0:T(8,128)(2,1)S(1)} %copy-done.13), channel_id=1, source_target_pairs={{511,0},{0,1},{1,2},{2,3},{3,4},{4,5},{5,6},{6,7},{7,8},{8,9},{9,1... | collective-permute-start | bytes 393224 | tf_op jit(solution)/shard_map/ppermute | solution.py:14
  49.3 3.6 %collective-permute-start.12 = (bf16[256,128]{0,1:T(8,128)(2,1)S(1)}, bf16[256,128]{0,1:T(8,128)(2,1)S(1)}, u32[]{:S(2)}, u32[]{:S(2)}) collective-permute-start(bf16[256,128]{0,1:T(8,128)(2,1)S(1)} %get-tuple-element.15), channel_id=1, source_target_pairs={{0,1},{1,0},{2,3},{3,2},{4,5},{5,4},{6,7},{7,6},{8,9},{9,8},{10,11... | collective-permute-start | bytes 196616 | tf_op jit(solution)/shard_map/ppermute | solution.py:8
  52.1 2.8 %copy-start.6 = (bf16[128,3,256]{2,0,1:T(8,128)(2,1)S(1)}, bf16[128,3,256]{2,0,1:T(8,128)(2,1)}, u32[]{:S(2)}) copy-start(bf16[128,3,256]{2,0,1:T(8,128)(2,1)} %param.21) | copy-start | bytes 589828
  52.9 5.3 %collective-permute-start.13 = (bf16[256,128]{0,1:T(8,128)(2,1)S(1)}, bf16[256,128]{0,1:T(8,128)(2,1)S(1)}, u32[]{:S(2)}, u32[]{:S(2)}) collective-permute-start(bf16[256,128]{0,1:T(8,128)(2,1)S(1)} %fusion.13), channel_id=1, source_target_pairs={{0,2},{1,3},{2,0},{3,1},{4,6},{5,7},{6,4},{7,5},{8,10},{9,11},{10,... | collective-permute-start | bytes 196616 | tf_op jit(solution)/shard_map/ppermute | solution.py:8
  58.3 6.1 %collective-permute-start.14 = (bf16[256,128]{0,1:T(8,128)(2,1)S(1)}, bf16[256,128]{0,1:T(8,128)(2,1)S(1)}, u32[]{:S(2)}, u32[]{:S(2)}) collective-permute-start(bf16[256,128]{0,1:T(8,128)(2,1)S(1)} %get-tuple-element.9), channel_id=1, source_target_pairs={{0,4},{1,5},{2,6},{3,7},{4,0},{5,1},{6,2},{7,3},{8,12},{9,13},{10,... | collective-permute-start | bytes 196616 | tf_op jit(solution)/shard_map/ppermute | solution.py:8
  64.5 20.3 %collective-permute-start.15 = (bf16[32,128]{0,1:T(8,128)(2,1)S(1)}, bf16[32,128]{0,1:T(8,128)(2,1)S(1)}, u32[]{:S(2)}, u32[]{:S(2)}) collective-permute-start(bf16[32,128]{0,1:T(8,128)(2,1)S(1)} %fusion.16), channel_id=1, source_target_pairs={{488,0},{489,1},{490,2},{491,3},{492,4},{493,5},{494,6},{495,7},{4... | collective-permute-start | bytes 24584 | tf_op jit(solution)/shard_map/ppermute | solution.py:14
  67.2 22.8 %collective-permute-start.16 = (bf16[32,128]{0,1:T(8,128)(2,1)S(1)}, bf16[32,128]{0,1:T(8,128)(2,1)S(1)}, u32[]{:S(2)}, u32[]{:S(2)}) collective-permute-start(bf16[32,128]{0,1:T(8,128)(2,1)S(1)} %fusion.16), channel_id=1, source_target_pairs={{496,0},{497,1},{498,2},{499,3},{500,4},{501,5},{502,6},{503,7},{5... | collective-permute-start | bytes 24584 | tf_op jit(solution)/shard_map/ppermute | solution.py:14
  70.5 25.0 %collective-permute-start.17 = (bf16[32,128]{0,1:T(8,128)(2,1)S(1)}, bf16[32,128]{0,1:T(8,128)(2,1)S(1)}, u32[]{:S(2)}, u32[]{:S(2)}) collective-permute-start(bf16[32,128]{0,1:T(8,128)(2,1)S(1)} %fusion.16), channel_id=1, source_target_pairs={{16,0},{17,1},{18,2},{19,3},{20,4},{21,5},{22,6},{23,7},{24,8},{25... | collective-permute-start | bytes 24584 | tf_op jit(solution)/shard_map/ppermute | solution.py:14
  77.9 19.8 %collective-permute-start.18 = (bf16[32,128]{0,1:T(8,128)(2,1)S(1)}, bf16[32,128]{0,1:T(8,128)(2,1)S(1)}, u32[]{:S(2)}, u32[]{:S(2)}) collective-permute-start(bf16[32,128]{0,1:T(8,128)(2,1)S(1)} %fusion.16), channel_id=1, source_target_pairs={{24,0},{25,1},{26,2},{27,3},{28,4},{29,5},{30,6},{31,7},{32,8},{33... | collective-permute-start | bytes 24584 | tf_op jit(solution)/shard_map/ppermute | solution.py:14
  84.8 26.2 %collective-permute-start.4 = (bf16[2,256,128]{2,1,0:T(8,128)(2,1)S(1)}, bf16[2,256,128]{2,1,0:T(8,128)(2,1)S(1)}, u32[]{:S(2)}, u32[]{:S(2)}) collective-permute-start(bf16[2,256,128]{2,1,0:T(8,128)(2,1)S(1)} %convolution_convert_fusion), channel_id=1, source_target_pairs={{1,0},{2,1},{3,2},{4,3},{5,4},{6,5},{7,6},{8,7},{9,8},{10,9},{11,1... | collective-permute-start | bytes 393224 | tf_op jit(solution)/shard_map/ppermute | solution.py:14
  90.1 30.0 %collective-permute-start.5 = (bf16[2,256,128]{2,1,0:T(8,128)(2,1)S(1)}, bf16[2,256,128]{2,1,0:T(8,128)(2,1)S(1)}, u32[]{:S(2)}, u32[]{:S(2)}) collective-permute-start(bf16[2,256,128]{2,1,0:T(8,128)(2,1)S(1)} %convolution_convert_fusion), channel_id=1, source_target_pairs={{2,0},{3,1},{4,2},{5,3},{6,4},{7,5},{8,6},{9,7},{10,8},{11,9},{12,... | collective-permute-start | bytes 393224 | tf_op jit(solution)/shard_map/ppermute | solution.py:14
  95.4 29.8 %collective-permute-start = (bf16[512,128]{0,1:T(8,128)(2,1)}, bf16[512,128]{0,1:T(8,128)(2,1)}, u32[]{:S(2)}, u32[]{:S(2)}) collective-permute-start(bf16[512,128]{0,1:T(8,128)(2,1)} %copy.51), channel_id=1, source_target_pairs={{1,0},{2,1},{3,2},{4,3},{5,4},{6,5},{7,6},{8,7},{9,8},{10,9},{11,1... | collective-permute-start | bytes 393224 | tf_op jit(solution)/shard_map/ppermute | solution.py:14
  97.7 14.0 %collective-permute-start.11 = (bf16[256,128]{0,1:T(8,128)(2,1)S(1)}, bf16[256,128]{0,1:T(8,128)(2,1)S(1)}, u32[]{:S(2)}, u32[]{:S(2)}) collective-permute-start(bf16[256,128]{0,1:T(8,128)(2,1)S(1)} %get-tuple-element.19), channel_id=1, source_target_pairs={{0,1},{1,0},{2,3},{3,2},{4,5},{5,4},{6,7},{7,6},{8,9},{9,8},{10,11... | collective-permute-start | bytes 196616 | tf_op jit(solution)/shard_map/ppermute | solution.py:8
  99.8 0.8 copy-start.7
  100.9 3.2 %collective-permute-start.19 = (bf16[256,128]{0,1:T(8,128)(2,1)S(1)}, bf16[256,128]{0,1:T(8,128)(2,1)S(1)}, u32[]{:S(2)}, u32[]{:S(2)}) collective-permute-start(bf16[256,128]{0,1:T(8,128)(2,1)S(1)} %get-tuple-element.17), channel_id=1, source_target_pairs={{0,1},{1,0},{2,3},{3,2},{4,5},{5,4},{6,7},{7,6},{8,9},{9,8},{10,11... | collective-permute-start | bytes 196616 | tf_op jit(solution)/shard_map/ppermute | solution.py:8
  104.1 5.0 %collective-permute-start.20 = (bf16[256,128]{0,1:T(8,128)(2,1)S(1)}, bf16[256,128]{0,1:T(8,128)(2,1)S(1)}, u32[]{:S(2)}, u32[]{:S(2)}) collective-permute-start(bf16[256,128]{0,1:T(8,128)(2,1)S(1)} %fusion.14), channel_id=1, source_target_pairs={{0,2},{1,3},{2,0},{3,1},{4,6},{5,7},{6,4},{7,5},{8,10},{9,11},{10,... | collective-permute-start | bytes 196616 | tf_op jit(solution)/shard_map/ppermute | solution.py:8
  109.1 5.9 %collective-permute-start.21 = (bf16[256,128]{0,1:T(8,128)(2,1)S(1)}, bf16[256,128]{0,1:T(8,128)(2,1)S(1)}, u32[]{:S(2)}, u32[]{:S(2)}) collective-permute-start(bf16[256,128]{0,1:T(8,128)(2,1)S(1)} %fusion.22), channel_id=1, source_target_pairs={{0,4},{1,5},{2,6},{3,7},{4,0},{5,1},{6,2},{7,3},{8,12},{9,13},{10,... | collective-permute-start | bytes 196616 | tf_op jit(solution)/shard_map/ppermute | solution.py:8
  115.2 7.3 %collective-permute-start.22 = (bf16[256,128]{0,1:T(8,128)(2,1)S(1)}, bf16[256,128]{0,1:T(8,128)(2,1)S(1)}, u32[]{:S(2)}, u32[]{:S(2)}) collective-permute-start(bf16[256,128]{0,1:T(8,128)(2,1)S(1)} %get-tuple-element.21), channel_id=1, source_target_pairs={{0,1},{1,0},{2,3},{3,2},{4,5},{5,4},{6,7},{7,6},{8,9},{9,8},{10,11... | collective-permute-start | bytes 196616 | tf_op jit(solution)/shard_map/ppermute | solution.py:8
  120.7 1.8 %copy-start.4 = (bf16[512,256]{1,0:T(8,128)(2,1)S(1)}, bf16[512,256]{1,0:T(8,128)(2,1)}, u32[]{:S(2)}) copy-start(bf16[512,256]{1,0:T(8,128)(2,1)} %param.18) | copy-start | bytes 786436
  122.4 1.0 copy-start.2
where the time goes:
time: 129 us; the launch traced here: 128 us
  starting transfers between devices  92.5 us (72%)
  matrix products  11.8 us (9%)
  local copies, waits for them, and re-layouts  10.4 us (8%)
  waiting for transfers between devices  9.61 us (7%)
  other arithmetic  2.81 us (2%)
    ppermute x14, starting transfers between devices, passed_along(): return lax.ppermute(block, axis, route)  63.1 us
    ppermute x9, starting transfers between devices, swapped(): lax.ppermute(value, axis, [(i, i ^ 1 << stride) for i in range(lax.axis_s...  29.4 us
    ppermute x9, waiting for transfers between devices, swapped(): lax.ppermute(value, axis, [(i, i ^ 1 << stride) for i in range(lax.axis_s...  9.58 us
    unnamed x35, local copies, waits for them, and re-layouts  6.51 us
  transfers between devices with their start and end apart: 23, of which 6 were waited for; matrix products, arithmetic and copies ran while one was open for 14% of the time, Pallas kernels for 0%

commit v1 on v0

v1 whole, which is shorter than its diff:
```python
import jax
import jax.numpy as jnp
from jax import lax
from jax.sharding import PartitionSpec as P

F32 = jnp.float32
BF16 = jnp.bfloat16


def route(value, source_of):
    size = lax.axis_size("curve")
    return lax.ppermute(value, "curve", [(source_of(i) % size, i) for i in range(size)])


def core_swap(value):
    return route(value, lambda i: i ^ 1)


def chip_swap(value):
    return route(value, lambda i: i + 1 if i & 1 else i - 1)


def far_route(value, chips):
    return route(value, lambda i: i + 2 * chips if i & 1 else i - 2 * chips)


def chip_groups(size):
    return [[8 * g + 2 * i + j for i in range(4)] for g in range(size // 8) for j in range(2)]


def dot_tn(a, b):
    return lax.dot_general(a, b, (((0,), (0,)), ((), ())), preferred_element_type=F32)


def dot_nn(a, b):
    return lax.dot_general(a, b, (((1,), (0,)), ((), ())), preferred_element_type=F32)


def slots_of(row, own, clusters, core):
    distance = (row - own) % clusters
    near = jnp.where(core == 0, -2, 2) % clusters
    far = jnp.where(core == 0, -3, 3) % clusters
    return distance == near, distance == far


def pick(masks, near, far):
    m, n = masks
    zero = jnp.zeros((), near.dtype)
    return jnp.where(
        m[:, None, None], near[None], jnp.where(n[:, None, None], far[None], zero)
    )


def couple(weights, chosen):
    total = dot_tn(weights[0], chosen[0])
    for s in range(1, weights.shape[0]):
        total = total + dot_tn(weights[s], chosen[s])
    return total


def per_device(
    vectors,
    near_self,
    near_next,
    leaf_basis,
    transfer_one,
    transfer_two,
    coupling_zero,
    coupling_one,
    coupling_two,
    list_zero,
    list_one,
    list_two,
):
    size = lax.axis_size("curve")
    device = lax.axis_index("curve")
    core = device & 1
    rank = leaf_basis.shape[1]
    columns = vectors.shape[1]
    points = near_self.shape[1]
    x = vectors.reshape(2, points, columns)
    basis = leaf_basis.reshape(2, points, rank)
    e1 = transfer_one.reshape(2, rank, rank)
    c0 = jnp.transpose(coupling_zero, (1, 0, 2))
    c1 = jnp.transpose(coupling_one, (1, 0, 2))
    c2 = jnp.transpose(coupling_two, (1, 0, 2))

    def columns_of(w):
        return jnp.concatenate([w[..., :128].reshape(-1, 128), w[..., 128:].reshape(-1, 128)], 0)

    def back(rows, shape):
        half = rows.shape[0] // 2
        return jnp.concatenate(
            [rows[:half].reshape(shape[:-1] + (128,)), rows[half:].reshape(shape[:-1] + (128,))], -1
        )

    coef = jnp.stack([dot_tn(basis[i], x[i]).astype(BF16) for i in range(2)], 0)
    part_one = (dot_tn(e1[0], coef[0]) + dot_tn(e1[1], coef[1])).astype(BF16)

    pieces = [coef.reshape(-1, columns), part_one, columns_of(transfer_two), columns_of(c1), columns_of(c2)]
    sizes = [p.shape[0] for p in pieces]
    got = core_swap(jnp.concatenate(pieces, 0))
    cuts = []
    at = 0
    for n in sizes:
        cuts.append(got[at : at + n])
        at += n
    partner_coef = cuts[0].reshape(coef.shape)
    first = core == 0

    def in_order(mine, other, axis):
        return jnp.concatenate(
            [jnp.where(first, mine, other), jnp.where(first, other, mine)], axis
        )

    coef_one = (part_one.astype(F32) + cuts[1].astype(F32)).astype(BF16)
    e2 = in_order(transfer_two, back(cuts[2], transfer_two.shape), 0)
    c1 = in_order(c1, back(cuts[3], c1.shape), 1)
    c2 = in_order(c2, back(cuts[4], c2.shape), 1)

    part_two = dot_tn(e2, coef_one).astype(BF16)
    shares = lax.all_to_all(
        part_two.reshape(4, rank // 4, columns), "curve", 0, 0, axis_index_groups=chip_groups(size)
    )
    coef_two = shares.astype(F32).sum(0).astype(BF16)

    two_far = far_route(coef_two, 12)
    two_near = far_route(coef_two, 8)
    one_near = far_route(coef_one, 2)
    one_far = far_route(coef_one, 3)

    outgoing = dot_tn(near_next[points:], x[1]).astype(BF16)
    ahead = x[0]
    leaves = jnp.concatenate(
        [
            jnp.where(first, coef[0], partner_coef[1]),
            jnp.where(first, coef[1], coef[0]),
            jnp.where(first, partner_coef[0], coef[1]),
            jnp.where(first, ahead, outgoing),
        ],
        0,
    )
    crossed = chip_swap(leaves)
    b = crossed[: 3 * rank].reshape(3, rank, columns)
    cross_near = crossed[3 * rank :]

    clusters_two = size // 8
    row_two = lax.dynamic_slice_in_dim(list_two, device // 8, 1, 0)[0]
    masks_two = slots_of(row_two, device // 8, clusters_two, core)
    far_two = couple(c2, pick(masks_two, two_near, two_far)).astype(BF16)
    gathered = lax.all_to_all(
        jnp.broadcast_to(far_two[None], (4,) + far_two.shape),
        "curve",
        0,
        0,
        axis_index_groups=chip_groups(size),
    )
    expansion_two = gathered.astype(F32).sum(0).astype(BF16)

    clusters_one = size // 2
    row_one = lax.dynamic_slice_in_dim(list_one, device // 2, 1, 0)[0]
    masks_one = slots_of(row_one, device // 2, clusters_one, core)
    far_one = couple(c1, pick(masks_one, one_near, one_far))
    share_one = (far_one + dot_nn(e2, expansion_two)).astype(BF16)

    last = core_swap(
        jnp.concatenate(
            [share_one, jnp.where(first, b[2], b[0]), jnp.where(first, outgoing, ahead)], 0
        )
    )
    expansion_one = (share_one.astype(F32) + last[:rank].astype(F32)).astype(BF16)
    window = jnp.concatenate([b, partner_coef, last[None, rank : 2 * rank]], 0)
    pair_near = last[2 * rank :]

    leaf = 2 * device + jnp.arange(2, dtype=jnp.int32)
    distance = (list_zero - leaf[:, None]) % (2 * size)
    code = jnp.where(distance == 2, 2, jnp.where(distance == 3, 3, jnp.where(distance == 2 * size - 2, 1, 0)))
    table = jnp.array(
        [[[0, 1, 3, 4], [1, 2, 4, 5]], [[5, 3, 0, 1], [3, 4, 1, 2]]], jnp.int32
    )
    places = table[core]
    index = jnp.take_along_axis(places, code, axis=1)
    chosen = window[index]

    incoming = jnp.where(first, cross_near, pair_near)
    following = jnp.where(first, pair_near, cross_near)
    out = []
    for i in range(2):
        far_zero = couple(c0[:, i * rank : (i + 1) * rank], chosen[i])
        expansion_zero = (far_zero + dot_nn(e1[i], expansion_one)).astype(BF16)
        near = dot_nn(near_self[i * points : (i + 1) * points], x[i])
        near = near + dot_nn(near_next[i * points : (i + 1) * points], x[1] if i == 0 else following)
        if i == 0:
            near = near + incoming.astype(F32)
        else:
            near = near + dot_tn(near_next[:points], x[0])
        out.append((near + dot_nn(basis[i], expansion_zero)).astype(BF16))
    return jnp.concatenate(out, 0)


def solution(mesh):
    rows = P("curve", None)
    cube = P("curve", None, None)
    return jax.shard_map(
        per_device,
        mesh=mesh,
        in_specs=(rows, rows, rows, rows, rows, rows, cube, cube, cube, rows, P(), P()),
        out_specs=rows,
        check_vma=False,
    )
```

time: 129 us -> 97.4 us (0.76)
  starting transfers between devices: 92.5 us -> 53.3 us
  matrix products: 11.8 us -> 17.5 us
    ppermute x23 -> x7, starting transfers between devices: 92.5 us -> 45.4 us  [route(): lax.ppermute(value, 'curve', [(source_of(i) % size, i) for i in range(siz...]
    all_to_all x0 -> x2, starting transfers between devices: none -> 7.93 us  [the longest x1 4.52 us: per_device(): lax.all_to_all(part_two.reshape(4, rank // 4, columns), 'curve', 0, 0, ax...]
    ppermute x23 -> x7, waiting for transfers between devices: 9.61 us -> 3.58 us  [route(): lax.ppermute(value, 'curve', [(source_of(i) % size, i) for i in range(siz...]
    all_to_all x0 -> x2, waiting for transfers between devices: none -> 5.86 us  [the longest x1 5.33 us: per_device(): lax.all_to_all(jnp.broadcast_to(far_two[None], (4,) + far_two.shape), 'cu...]
    dot_general x12 -> x26, matrix products: 11.8 us -> 17.5 us  [the longest x19 9.73 us: dot_tn(): lax.dot_general(a, b, (((0,), (0,)), ((), ())), preferred_element_type=F32)]
    unnamed x35 -> x46, local copies, waits for them, and re-layouts: 6.51 us -> 8.52 us
    concatenate x0 -> x4, other arithmetic: none -> 1.54 us  [the longest x1 0.75 us: per_device(): jnp.concatenate([jnp.where(first, coef[0], partner_coef[1]), jnp.where(fi...]
    another operation x5 -> x1, other arithmetic: 1.46 us -> 0.02 us  [per_device(): coef = jnp.stack([dot_tn(basis[i], x[i]).astype(BF16) for i in range(2)], 0)]
  transfers between devices with their start and end apart: 23 -> 9, of which waited for: 6 -> 4; matrix products, arithmetic and copies ran while one was open for 14% -> 14% of each run, Pallas kernels for 0% -> 0%
where the time goes in v1:
time: 97.4 us; the launch traced here: 96.4 us
  starting transfers between devices  53.3 us (55%)
  matrix products  17.5 us (18%)
  local copies, waits for them, and re-layouts  11.5 us (12%)
  waiting for transfers between devices  9.44 us (10%)
  other arithmetic  4.03 us (4%)
    ppermute x7, starting transfers between devices, route(): lax.ppermute(value, 'curve', [(source_of(i) % size, i) for i in range(siz...  45.4 us
    dot_general x19, matrix products, dot_tn(): lax.dot_general(a, b, (((0,), (0,)), ((), ())), preferred_element_type=F32)  9.73 us
    unnamed x46, local copies, waits for them, and re-layouts  8.52 us
    dot_general x7, matrix products, dot_nn(): lax.dot_general(a, b, (((1,), (0,)), ((), ())), preferred_element_type=F32)  7.81 us
    all_to_all x1, waiting for transfers between devices, per_device(): lax.all_to_all(jnp.broadcast_to(far_two[None], (4,) + far_two.shape), 'cu...  5.33 us
    all_to_all x1, starting transfers between devices, per_device(): lax.all_to_all(part_two.reshape(4, rank // 4, columns), 'curve', 0, 0, ax...  4.52 us
    ppermute x7, waiting for transfers between devices, route(): lax.ppermute(value, 'curve', [(source_of(i) % size, i) for i in range(siz...  3.58 us
    all_to_all x1, starting transfers between devices, per_device(): lax.all_to_all(jnp.broadcast_to(far_two[None], (4,) + far_two.shape), 'cu...  3.41 us
  transfers between devices with their start and end apart: 9, of which 4 were waited for; matrix products, arithmetic and copies ran while one was open for 14% of the time, Pallas kernels for 0%

profile of v1, /device:TPU:1, one launch (start us, length us, event | category | flops | bytes accessed | tf_op | source)
XLA Modules:
  0.0 96.4 jit_solution(7622079571367923491)
XLA Ops:
  0.0 1.3 %convolution_convert_fusion.2 = bf16[256,128]{1,0:T(8,128)(2,1)S(1)} fusion(bf16[1024,256]{1,0:T(8,128)(2,1)} %param.16, bf16[1024,128]{1,0:T(8,128)(2,1)} %param.13), kind=kOutput, calls=%fused_computation.24 | convolution fusion | flops 33587200 | bytes 458752 | tf_op jit(solution)/shard_map/dot_general | solution.py:32
  1.3 1.2 %convolution_convert_fusion.1 = bf16[256,128]{1,0:T(8,128)(2,1)S(1)} fusion(bf16[1024,256]{1,0:T(8,128)(2,1)S(1)} %copy-done.5, bf16[1024,128]{1,0:T(8,128)(2,1)} %param.13), kind=kOutput, calls=%fused_computation.23 | convolution fusion | flops 33587200 | bytes 458752 | tf_op jit(solution)/shard_map/dot_general | solution.py:32
  2.6 0.6 constant_dynamic-update-slice_fusion.5
  3.2 0.3 copy-done
  3.5 0.2 fusion.46
  3.8 0.8 constant_dynamic-update-slice_fusion.4
  4.6 0.6 slice_dynamic-update-slice_fusion.1
  5.2 0.6 slice_dynamic-update-slice_fusion
  5.9 0.8 copy-done.12
  6.6 0.6 constant_dynamic-update-slice_fusion.3
  7.3 0.7 constant_dynamic-update-slice_fusion.2
  7.9 0.6 constant_dynamic-update-slice_fusion.1
  8.5 0.6 constant_dynamic-update-slice_fusion
  9.1 8.7 %collective-permute-start = (bf16[1984,128]{1,0:T(8,128)(2,1)}, bf16[1984,128]{1,0:T(8,128)(2,1)S(1)}, u32[]{:S(2)}, u32[]{:S(2)}) collective-permute-start(bf16[1984,128]{1,0:T(8,128)(2,1)} %constant_dynamic-update-slice_fusion), channel_id=1, source_target_pairs={{1,0},{0,1},{3,2},{2,3},{5,4},{4,5},{7,6},{6,7},{9,8},{8,9},{11,10... | collective-permute-start | bytes 1523720 | tf_op jit(solution)/shard_map/ppermute | solution.py:12
  18.0 2.0 %fusion.12 = f32[512,128]{1,0:T(8,128)} fusion(bf16[1024,512]{1,0:T(8,128)(2,1)} %param.14, bf16[1024,128]{1,0:T(8,128)(2,1)S(1)} %copy-done.14), kind=kOutput, calls=%fused_computation.34 | convolution fusion | flops 67108864 | bytes 917504 | tf_op jit(solution)/shard_map/dot_general | solution.py:36
  20.0 2.1 %fusion.10 = f32[512,128]{1,0:T(8,128)} fusion(bf16[1024,512]{1,0:T(8,128)(2,1)} %param.14, bf16[1024,128]{1,0:T(8,128)(2,1)S(1)} %copy-done.14), kind=kOutput, calls=%fused_computation.32 | convolution fusion | flops 67108864 | bytes 917504 | tf_op jit(solution)/shard_map/dot_general | solution.py:36
  22.2 0.1 bitcast_or_fusion
  22.4 0.7 gather_fusion.1
  23.1 0.6 copy-done.16
  23.7 0.2 subtract_reduce_fusion
  24.0 0.7 copy-done.18
  24.6 0.2 subtract_reduce_fusion.1
  24.9 1.0 %broadcast_select_fusion.3 = (bf16[512,128]{1,0:T(8,128)(2,1)S(1)}, bf16[512,128]{1,0:T(8,128)(2,1)}) fusion(pred[]{:T(512)S(6)} %eq.66, bf16[1024,128]{1,0:T(8,128)(2,1)S(1)} %copy-done.14, bf16[1024,512]{1,0:T(8,128)(2,1)S(1)} %copy-done.1), kind=kOutput, calls=%fused_computation.81 | convolution fusion | flops 67305472 | bytes 1048577 | tf_op jit(solution)/shard_map/dot_general | solution.py:32
  26.0 1.0 %fusion.16 = f32[512,128]{1,0:T(8,128)} fusion(bf16[1024,512]{1,0:T(8,128)(2,1)S(1)} %copy-done.1, bf16[1024,128]{1,0:T(8,128)(2,1)S(1)} %copy-done.14), kind=kOutput, calls=%fused_computation.38 | convolution fusion | flops 67108864 | bytes 917504 | tf_op jit(solution)/shard_map/dot_general | solution.py:32
  27.0 0.7 add_convert_fusion.2
  27.7 10.4 %collective-permute-start.2 = (bf16[256,128]{1,0:T(8,128)(2,1)}, bf16[256,128]{1,0:T(8,128)(2,1)}, u32[]{:S(2)}, u32[]{:S(2)}) collective-permute-start(bf16[256,128]{1,0:T(8,128)(2,1)} %add_convert_fusion.2), channel_id=1, source_target_pairs={{508,0},{5,1},{510,2},{7,3},{0,4},{9,5},{2,6},{11,7},{4,8},{13,9},... | collective-permute-start | bytes 196616 | tf_op jit(solution)/shard_map/ppermute | solution.py:12
  38.1 1.9 %collective-permute-start.3 = (bf16[256,128]{1,0:T(8,128)(2,1)}, bf16[256,128]{1,0:T(8,128)(2,1)}, u32[]{:S(2)}, u32[]{:S(2)}) collective-permute-start(bf16[256,128]{1,0:T(8,128)(2,1)} %add_convert_fusion.2), channel_id=1, source_target_pairs={{506,0},{7,1},{508,2},{9,3},{510,4},{11,5},{0,6},{13,7},{2,8},{15,... | collective-permute-start | bytes 196616 | tf_op jit(solution)/shard_map/ppermute | solution.py:12
  40.1 1.7 %convolution_convert_fusion.3 = bf16[256,128]{1,0:T(8,128)(2,1)} fusion(bf16[256,128]{1,0:T(8,128)(2,1)} %add_convert_fusion.2, bf16[128,256]{1,0:T(8,128)(2,1)S(1)} %get-tuple-element.27, bf16[128,256]{1,0:T(8,128)(2,1)S(1)} %get-tuple-element.26), kind=kOutput, calls=%fused_computation.30 | convolution fusion | flops 17072128 | bytes 262144 | tf_op jit(solution)/shard_map/dot_general | solution.py:32
  41.8 4.5 %all-to-all-start = ((bf16[4,64,128]{2,1,0:T(8,128)(2,1)}), bf16[4,64,128]{2,1,0:T(8,128)(2,1)S(1)}, u32[]{:S(2)}, u32[]{:S(2)}) async-start(bf16[4,64,128]{2,1,0:T(8,128)(2,1)} %bitcast.21), calls=%async_computation | async-start | bytes 131072 | tf_op jit(solution)/shard_map/all_to_all | solution.py:122
  46.3 0.7 pad_maximum_fusion.1
  47.1 1.9 %collective-permute-start.1 = (bf16[1280,128]{1,0:T(8,128)(2,1)}, bf16[1280,128]{1,0:T(8,128)(2,1)S(1)}, u32[]{:S(2)}, u32[]{:S(2)}) collective-permute-start(bf16[1280,128]{1,0:T(8,128)(2,1)} %pad_maximum_fusion.1), channel_id=1, source_target_pairs={{511,0},{2,1},{1,2},{4,3},{3,4},{6,5},{5,6},{8,7},{7,8},{10,9},{9,... | collective-permute-start | bytes 983048 | tf_op jit(solution)/shard_map/ppermute | solution.py:12
  49.2 1.0 select_select_fusion
  50.1 0.2 fusion.27
  50.4 0.5 all-to-all-done
  50.9 4.2 %collective-permute-start.4 = (bf16[64,128]{1,0:T(8,128)(2,1)S(1)}, bf16[64,128]{1,0:T(8,128)(2,1)S(1)}, u32[]{:S(2)}, u32[]{:S(2)}) collective-permute-start(bf16[64,128]{1,0:T(8,128)(2,1)S(1)} %reduce_sum.24), channel_id=1, source_target_pairs={{496,0},{17,1},{498,2},{19,3},{500,4},{21,5},{502,6},{23,7},{504,8... | collective-permute-start | bytes 49160 | tf_op jit(solution)/shard_map/ppermute | solution.py:12
  55.1 6.4 %collective-permute-start.5 = (bf16[64,128]{1,0:T(8,128)(2,1)S(1)}, bf16[64,128]{1,0:T(8,128)(2,1)S(1)}, u32[]{:S(2)}, u32[]{:S(2)}) collective-permute-start(bf16[64,128]{1,0:T(8,128)(2,1)S(1)} %reduce_sum.24), channel_id=1, source_target_pairs={{488,0},{25,1},{490,2},{27,3},{492,4},{29,5},{494,6},{31,7},{496,8... | collective-permute-start | bytes 49160 | tf_op jit(solution)/shard_map/ppermute | solution.py:12
  61.5 0.2 convolution_add_fusion.9
  61.7 2.8 %collective-permute-done.5 = bf16[64,128]{1,0:T(8,128)(2,1)S(1)} collective-permute-done((bf16[64,128]{1,0:T(8,128)(2,1)S(1)}, bf16[64,128]{1,0:T(8,128)(2,1)S(1)}, u32[]{:S(2)}, u32[]{:S(2)}) %collective-permute-start.5) | collective-permute-done | bytes 16416 | tf_op jit(solution)/shard_map/ppermute | solution.py:12
  64.6 0.2 fusion.57
  64.8 0.2 convolution_add_fusion.12
  65.0 0.2 fusion.4
  65.2 0.7 broadcast_in_dim.110
  65.9 3.4 %all-to-all-start.1 = ((bf16[4,256,128]{2,1,0:T(8,128)(2,1)}), bf16[4,256,128]{2,1,0:T(8,128)(2,1)S(1)}, u32[]{:S(2)}, u32[]{:S(2)}) async-start(bf16[4,256,128]{2,1,0:T(8,128)(2,1)} %broadcast_in_dim.110), calls=%async_computation.1 | async-start | bytes 524288 | tf_op jit(solution)/shard_map/all_to_all | solution.py:151
  69.4 0.2 convolution_add_fusion.8
  69.6 5.3 %all-to-all-done.1 = bf16[4,256,128]{2,1,0:T(8,128)(2,1)S(1)} async-done(((bf16[4,256,128]{2,1,0:T(8,128)(2,1)}), bf16[4,256,128]{2,1,0:T(8,128)(2,1)S(1)}, u32[]{:S(2)}, u32[]{:S(2)}) %all-to-all-start.1) | async-done | bytes 262176 | tf_op jit(solution)/shard_map/all_to_all | solution.py:151
  75.0 0.2 fusion.6
  75.2 0.7 copy-done.13
  75.9 11.9 %collective-permute-start.6 = (bf16[1024,128]{1,0:T(8,128)(2,1)S(1)}, bf16[1024,128]{1,0:T(8,128)(2,1)S(1)}, u32[]{:S(2)}, u32[]{:S(2)}) collective-permute-start(bf16[1024,128]{1,0:T(8,128)(2,1)S(1)} %pad_maximum_fusion.2), channel_id=1, source_target_pairs={{1,0},{0,1},{3,2},{2,3},{5,4},{4,5},{7,6},{6,7},{9,8},{8,9},{11,10... | collective-permute-start | bytes 786440 | tf_op jit(solution)/shard_map/ppermute | solution.py:12
  87.8 0.3 convolution_add_fusion
  88.2 0.8 collective-permute-done.6
  88.9 0.7 copy-done.7
  89.7 0.6 gather_fusion
  90.3 0.4 copy-done.3
  90.8 0.2 fusion.33
  91.0 0.2 fusion.32
  91.2 0.2 convolution_add_fusion.6
  91.4 0.2 convolution_add_fusion.5
  91.6 0.2 convolution_add_fusion.3
  91.8 0.2 convolution_add_fusion.2
  92.0 1.5 %convolution_bitcast_fusion.1 = f32[512,128]{1,0:T(8,128)S(1)} fusion(f32[128,256]{1,0:T(8,128)S(1)} %convolution_add_fusion.2, bf16[1024,256]{1,0:T(8,128)(2,1)} %param.16, bf16[512,256]{1,0:T(8,128)(2,1)S(1)} %copy-done, bf16[256,128]{1,0:T(8,128)(2,1)S(1)} %fusion.6, bf16[1024,128]{1,0:T(8,128)(2,1)} %copy-done.7), kind=kOutput, calls=%fused_computation.6 | convolution fusion | flops 50528256 | bytes 917504 | tf_op jit(solution)/shard_map/dot_general | solution.py:36
  93.5 0.4 add_convert_fusion
  94.0 0.5 copy-done.9
  94.5 1.2 %fusion.3 = bf16[512,128]{1,0:T(8,128)(2,1)S(1)} fusion(f32[512,128]{1,0:T(8,128)S(1)} %convolution_bitcast_fusion.1, f32[512,128]{1,0:T(8,128)} %fusion.16, f32[512,128]{1,0:T(8,128)S(1)} %copy-done.9, bf16[1024,512]{1,0:T(8,128)(2,1)S(1)} %copy-done.1, pred[]{:T(512)S(6)} %eq.66, bf16[1024,128]{1,0:T(8,128)(2,1)S(1)} %copy-done.8, ...), kind=kOutput, calls=%fused_computation.10 | convolution fusion | flops 67436544 | bytes 1703937 | tf_op jit(solution)/shard_map/dot_general | solution.py:36
  95.7 0.7 pad_maximum_fusion.3
  (68 shorter events, 0.9 us)
Async XLA Ops:
  0.0 1.3 %copy-start.5 = (bf16[1024,256]{1,0:T(8,128)(2,1)S(1)}, bf16[1024,256]{1,0:T(8,128)(2,1)}, u32[]{:S(2)}) copy-start(bf16[1024,256]{1,0:T(8,128)(2,1)} %param.16) | copy-start | bytes 1572868
  2.5 1.0 %copy-start = (bf16[512,256]{1,0:T(8,128)(2,1)S(1)}, bf16[512,256]{1,0:T(8,128)(2,1)}, u32[]{:S(2)}) copy-start(bf16[512,256]{1,0:T(8,128)(2,1)} %param.17) | copy-start | bytes 786436
  3.7 0.9 copy-start.10
  3.7 2.1 %copy-start.4 = (bf16[128,3,256]{2,0,1:T(8,128)(2,1)S(1)}, bf16[128,3,256]{2,0,1:T(8,128)(2,1)}, u32[]{:S(2)}) copy-start(bf16[128,3,256]{2,0,1:T(8,128)(2,1)} %param.20) | copy-start | bytes 589828
  5.8 0.8 copy-start.12
  7.3 10.7 %copy-start.14 = (bf16[1024,128]{1,0:T(8,128)(2,1)S(1)}, bf16[1024,128]{1,0:T(8,128)(2,1)}, u32[]{:S(2)}) copy-start(bf16[1024,128]{1,0:T(8,128)(2,1)} %param.13) | copy-start | bytes 786436
  9.1 17.9 %collective-permute-start = (bf16[1984,128]{1,0:T(8,128)(2,1)}, bf16[1984,128]{1,0:T(8,128)(2,1)S(1)}, u32[]{:S(2)}, u32[]{:S(2)}) collective-permute-start(bf16[1984,128]{1,0:T(8,128)(2,1)} %constant_dynamic-update-slice_fusion), channel_id=1, source_target_pairs={{1,0},{0,1},{3,2},{2,3},{5,4},{4,5},{7,6},{6,7},{9,8},{8,9},{11,10... | collective-permute-start | bytes 1523720 | tf_op jit(solution)/shard_map/ppermute | solution.py:12
  18.0 4.2 %copy-start.17 = (s32[2,3]{1,0:T(2,128)S(1)}, s32[2,3]{1,0:T(2,128)}, u32[]{:S(2)}) copy-start(s32[2,3]{1,0:T(2,128)} %param.22) | copy-start | bytes 76
  18.0 4.4 %copy-start.19 = (s32[2,2,4]{2,1,0:T(2,128)S(1)}, s32[2,2,4]{2,1,0:T(2,128)}, u32[]{:S(2)}) copy-start(s32[2,2,4]{2,1,0:T(2,128)} %constant.127.clone) | copy-start | bytes 196
  20.0 4.9 %copy-start.1 = (bf16[1024,512]{1,0:T(8,128)(2,1)S(1)}, bf16[1024,512]{1,0:T(8,128)(2,1)}, u32[]{:S(2)}) copy-start(bf16[1024,512]{1,0:T(8,128)(2,1)} %param.15) | copy-start | bytes 3145732
  23.0 0.7 copy-start.16
  23.9 0.7 copy-start.18
  27.0 61.1 %copy-start.2 = (bf16[1984,128]{1,0:T(8,128)(2,1)}, bf16[1984,128]{1,0:T(8,128)(2,1)S(1)}, u32[]{:S(2)}) copy-start(bf16[1984,128]{1,0:T(8,128)(2,1)S(1)} %collective-permute-done) | copy-start | bytes 1523716
  27.7 21.4 %collective-permute-start.2 = (bf16[256,128]{1,0:T(8,128)(2,1)}, bf16[256,128]{1,0:T(8,128)(2,1)}, u32[]{:S(2)}, u32[]{:S(2)}) collective-permute-start(bf16[256,128]{1,0:T(8,128)(2,1)} %add_convert_fusion.2), channel_id=1, source_target_pairs={{508,0},{5,1},{510,2},{7,3},{0,4},{9,5},{2,6},{11,7},{4,8},{13,9},... | collective-permute-start | bytes 196616 | tf_op jit(solution)/shard_map/ppermute | solution.py:12
  38.1 11.0 %collective-permute-start.3 = (bf16[256,128]{1,0:T(8,128)(2,1)}, bf16[256,128]{1,0:T(8,128)(2,1)}, u32[]{:S(2)}, u32[]{:S(2)}) collective-permute-start(bf16[256,128]{1,0:T(8,128)(2,1)} %add_convert_fusion.2), channel_id=1, source_target_pairs={{506,0},{7,1},{508,2},{9,3},{510,4},{11,5},{0,6},{13,7},{2,8},{15,... | collective-permute-start | bytes 196616 | tf_op jit(solution)/shard_map/ppermute | solution.py:12
  41.8 9.1 %all-to-all-start = ((bf16[4,64,128]{2,1,0:T(8,128)(2,1)}), bf16[4,64,128]{2,1,0:T(8,128)(2,1)S(1)}, u32[]{:S(2)}, u32[]{:S(2)}) async-start(bf16[4,64,128]{2,1,0:T(8,128)(2,1)} %bitcast.21), calls=%async_computation | async-start | bytes 131072 | tf_op jit(solution)/shard_map/all_to_all | solution.py:122
  47.1 22.5 %collective-permute-start.1 = (bf16[1280,128]{1,0:T(8,128)(2,1)}, bf16[1280,128]{1,0:T(8,128)(2,1)S(1)}, u32[]{:S(2)}, u32[]{:S(2)}) collective-permute-start(bf16[1280,128]{1,0:T(8,128)(2,1)} %pad_maximum_fusion.1), channel_id=1, source_target_pairs={{511,0},{2,1},{1,2},{4,3},{3,4},{6,5},{5,6},{8,7},{7,8},{10,9},{9,... | collective-permute-start | bytes 983048 | tf_op jit(solution)/shard_map/ppermute | solution.py:12
  50.9 10.8 %collective-permute-start.4 = (bf16[64,128]{1,0:T(8,128)(2,1)S(1)}, bf16[64,128]{1,0:T(8,128)(2,1)S(1)}, u32[]{:S(2)}, u32[]{:S(2)}) collective-permute-start(bf16[64,128]{1,0:T(8,128)(2,1)S(1)} %reduce_sum.24), channel_id=1, source_target_pairs={{496,0},{17,1},{498,2},{19,3},{500,4},{21,5},{502,6},{23,7},{504,8... | collective-permute-start | bytes 49160 | tf_op jit(solution)/shard_map/ppermute | solution.py:12
  55.1 9.5 %collective-permute-start.5 = (bf16[64,128]{1,0:T(8,128)(2,1)S(1)}, bf16[64,128]{1,0:T(8,128)(2,1)S(1)}, u32[]{:S(2)}, u32[]{:S(2)}) collective-permute-start(bf16[64,128]{1,0:T(8,128)(2,1)S(1)} %reduce_sum.24), channel_id=1, source_target_pairs={{488,0},{25,1},{490,2},{27,3},{492,4},{29,5},{494,6},{31,7},{496,8... | collective-permute-start | bytes 49160 | tf_op jit(solution)/shard_map/ppermute | solution.py:12
  65.9 9.0 %all-to-all-start.1 = ((bf16[4,256,128]{2,1,0:T(8,128)(2,1)}), bf16[4,256,128]{2,1,0:T(8,128)(2,1)S(1)}, u32[]{:S(2)}, u32[]{:S(2)}) async-start(bf16[4,256,128]{2,1,0:T(8,128)(2,1)} %broadcast_in_dim.110), calls=%async_computation.1 | async-start | bytes 524288 | tf_op jit(solution)/shard_map/all_to_all | solution.py:151
  75.0 0.9 copy-start.13
  75.9 11.9 %copy-start.11 = (f32[512,128]{1,0:T(8,128)S(1)}, f32[512,128]{1,0:T(8,128)}, u32[]{:S(2)}) copy-start(f32[512,128]{1,0:T(8,128)} %fusion.12) | copy-start | bytes 786436
  75.9 11.9 %copy-start.15 = (bf16[1024,128]{1,0:T(8,128)(2,1)S(1)}, bf16[1024,128]{1,0:T(8,128)(2,1)}, u32[]{:S(2)}) copy-start(bf16[1024,128]{1,0:T(8,128)(2,1)} %param.13) | copy-start | bytes 786436
  75.9 13.0 %collective-permute-start.6 = (bf16[1024,128]{1,0:T(8,128)(2,1)S(1)}, bf16[1024,128]{1,0:T(8,128)(2,1)S(1)}, u32[]{:S(2)}, u32[]{:S(2)}) collective-permute-start(bf16[1024,128]{1,0:T(8,128)(2,1)S(1)} %pad_maximum_fusion.2), channel_id=1, source_target_pairs={{1,0},{0,1},{3,2},{2,3},{5,4},{4,5},{7,6},{6,7},{9,8},{8,9},{11,10... | collective-permute-start | bytes 786440 | tf_op jit(solution)/shard_map/ppermute | solution.py:12
  88.2 1.5 %slice-start = ((bf16[1984,128]{1,0:T(8,128)(2,1)}), bf16[512,128]{1,0:T(8,128)(2,1)S(1)}, s32[]{:S(2)}) async-start(bf16[1984,128]{1,0:T(8,128)(2,1)} %copy-done.2), calls=%async_computation.2 | async-start | bytes 262144 | tf_op jit(solution)/shard_map/slice | solution.py:106
  88.9 0.7 copy-start.7
  89.6 1.1 %copy-start.3 = (bf16[512,3,256]{2,0,1:T(8,128)(2,1)S(1)}, bf16[512,3,256]{2,0,1:T(8,128)(2,1)}, u32[]{:S(2)}) copy-start(bf16[512,3,256]{2,0,1:T(8,128)(2,1)} %param.19) | copy-start | bytes 2359300
  92.0 1.5 %copy-start.6 = (bf16[1024,256]{1,0:T(8,128)(2,1)S(1)}, bf16[1024,256]{1,0:T(8,128)(2,1)}, u32[]{:S(2)}) copy-start(bf16[1024,256]{1,0:T(8,128)(2,1)} %param.16) | copy-start | bytes 1572868
  92.0 1.5 %copy-start.8 = (bf16[1024,128]{1,0:T(8,128)(2,1)S(1)}, bf16[1024,128]{1,0:T(8,128)(2,1)}, u32[]{:S(2)}) copy-start(bf16[1024,128]{1,0:T(8,128)(2,1)} %copy-done.7) | copy-start | bytes 786436
  93.5 1.0 copy-start.9

commit v2 on v1

v2 whole, which is shorter than its diff:
```python
import functools

import jax
import jax.numpy as jnp
from jax import lax
from jax.experimental import pallas as pl
from jax.experimental.pallas import tpu as pltpu
from jax.sharding import PartitionSpec as P


F32 = jnp.float32
BF16 = jnp.bfloat16
I32 = jnp.int32


def route(value, source_of):
    size = lax.axis_size("curve")
    return lax.ppermute(value, "curve", [(source_of(i) % size, i) for i in range(size)])


def core_swap(value):
    return route(value, lambda i: i ^ 1)


def chip_swap(value):
    return route(value, lambda i: i + 1 if i & 1 else i - 1)


def far_route(value, chips):
    return route(value, lambda i: i + 2 * chips if i & 1 else i - 2 * chips)


def third_cluster(value):
    def source_of(i):
        turned = i ^ 4
        return turned + 24 if i & 1 else turned - 24

    return route(value, source_of)


def chip_groups(size):
    return [[8 * g + 2 * i + j for i in range(4)] for g in range(size // 8) for j in range(2)]


def cluster_groups(size):
    return [[8 * g + i for i in range(8)] for g in range(size // 8)]


def nn(a, b):
    return lax.dot_general(a, b, (((1,), (0,)), ((), ())), preferred_element_type=F32)


def nt(a, b):
    return lax.dot_general(a, b, (((1,), (1,)), ((), ())), preferred_element_type=F32)


def call(body, outs, flops, *args, far=False, scratch=(), grant=8):
    spec = pl.BlockSpec(memory_space=pltpu.VMEM)
    moved = sum(a.size * a.dtype.itemsize for a in args)
    if far:
        args = [pltpu.with_memory_space_constraint(a, pltpu.HBM) for a in args]
    return pl.pallas_call(
        body,
        out_shape=[jax.ShapeDtypeStruct(s, t) for s, t in outs],
        in_specs=[pl.BlockSpec(memory_space=pltpu.HBM) if far else spec] * len(args),
        out_specs=[spec] * len(outs),
        scratch_shapes=list(scratch),
        compiler_params=pltpu.CompilerParams(vmem_limit_bytes=grant << 20),
        cost_estimate=pl.CostEstimate(flops=flops, bytes_accessed=moved, transcendentals=0),
    )(*args)


def picked_row(table, row):
    lanes = lax.broadcasted_iota(I32, table.shape, 1)
    return jnp.sum(jnp.where(lanes == row, table, 0), axis=1, keepdims=True)


def offset_mask(entry, own, offset, clusters):
    wanted = lax.rem(own + offset + clusters, clusters)
    return jnp.where(entry == wanted, 1.0, 0.0).astype(F32)


def spread_body(table_ref, coupling_ref, out_ref):
    device = lax.axis_index("curve")
    clusters = table_ref.shape[1]
    own = device // 8
    row = picked_row(table_ref[...], own)
    for core, offsets in enumerate(((-2, -3), (2, 3))):
        for n, offset in enumerate(offsets):
            total = None
            for s in range(3):
                mask = offset_mask(row[s : s + 1], own, offset, clusters)
                term = coupling_ref[s].astype(F32) * mask
                total = term if total is None else total + term
            value = total.astype(BF16)
            for chip in range(4):
                out_ref[2 * chip + core, n] = value


def first_body(
    points, rank, basis_hbm, x_hbm, e1_hbm, next_hbm, e2_hbm, c1_hbm, pack_ref, cross_ref,
    basis_ref, x_ref, e1_ref, next_ref, sems,
):
    core = lax.axis_index("curve") & 1
    copies = []
    for i in range(2):
        rows = pl.ds(i * points, points)
        copies.append((x_hbm.at[rows], x_ref.at[rows]))
        copies.append((basis_hbm.at[rows], basis_ref.at[rows]))
    copies.append((e1_hbm, e1_ref))
    copies.append((next_hbm.at[pl.ds(points, points)], next_ref))
    copies.append((e2_hbm, pack_ref.at[pl.ds(640, 128)]))
    for s in range(3):
        copies.append((c1_hbm.at[s], pack_ref.at[pl.ds(768 + 128 * s, 128)]))
    moves = [pltpu.make_async_copy(a, b, sems.at[n]) for n, (a, b) in enumerate(copies)]
    for move in moves:
        move.start()
    coefs = []
    for i in range(2):
        moves[2 * i].wait()
        turned = x_ref[i * points : (i + 1) * points].T
        moves[2 * i + 1].wait()
        coef = nn(turned, basis_ref[i * points : (i + 1) * points]).astype(BF16)
        pack_ref[128 * i : 128 * (i + 1)] = coef
        coefs.append(coef)
    moves[4].wait()
    part = nn(coefs[0], e1_ref[0:rank]) + nn(coefs[1], e1_ref[rank : 2 * rank])
    pack_ref[256:384] = part.astype(BF16)
    moves[5].wait()
    outgoing = nn(turned, next_ref[...]).astype(BF16)
    first = core == 0
    for h in range(2):
        sent = outgoing[:, 256 * h : 256 * (h + 1)]
        low = x_ref[128 * h : 128 * (h + 1)]
        high = x_ref[256 + 128 * h : 256 + 128 * (h + 1)]
        ahead = jnp.concatenate([low, high], 1)
        pack_ref[384 + 128 * h : 512 + 128 * h] = jnp.where(first, sent, ahead)
        cross_ref[128 * h : 128 * (h + 1)] = jnp.where(first, ahead, sent)
    for move in moves[6:]:
        move.wait()


def second_body(pack_ref, got_ref, one_ref, two_ref):
    first = (lax.axis_index("curve") & 1) == 0
    one = (pack_ref[256:384].astype(F32) + got_ref[256:384].astype(F32)).astype(BF16)
    one_ref[...] = one
    mine = pack_ref[640:768]
    other = got_ref[640:768]
    top = jnp.where(first, mine, other)
    bottom = jnp.where(first, other, mine)
    two_ref[...] = (nn(one[:, 0:128], top) + nn(one[:, 128:256], bottom)).astype(BF16)


def cross_body(pack_ref, got_ref, near_ref, out_ref):
    first = (lax.axis_index("curve") & 1) == 0
    out_ref[0:128] = jnp.where(first, pack_ref[0:128], got_ref[128:256])
    out_ref[128:256] = jnp.where(first, pack_ref[128:256], pack_ref[0:128])
    out_ref[256:384] = jnp.where(first, got_ref[0:128], pack_ref[128:256])
    out_ref[384:640] = near_ref[...]


def near_body(points, self_ref, next_ref, x_ref, out_ref):
    x0 = x_ref[0:points]
    x1 = x_ref[points : 2 * points]
    out_ref[0:points] = nn(self_ref[0:points], x0) + nn(next_ref[0:points], x1)
    inner = nn(x0.T, next_ref[0:points])
    out_ref[points : 2 * points] = nn(self_ref[points : 2 * points], x1) + inner.T


def couple_two_body(near_ref, far_ref, weights_ref, out_ref):
    near = near_ref[...]
    far = far_ref[...]
    total = None
    for m in range(8):
        piece = nn(near[:, 32 * m : 32 * (m + 1)], weights_ref[m, 0])
        piece = piece + nn(far[:, 32 * m : 32 * (m + 1)], weights_ref[m, 1])
        total = piece if total is None else total + piece
    value = total.astype(BF16)
    for i in range(4):
        out_ref[i] = value


def gather_body(
    points,
    rank,
    table_ref,
    leaf_ref,
    pack_ref,
    got_ref,
    near_ref,
    far_ref,
    cross_ref,
    c0_ref,
    part_ref,
    next_ref,
    one_ref,
    zero_ref,
    weight_ref,
    field_ref,
    send_ref,
):
    device = lax.axis_index("curve")
    core = device & 1
    first = core == 0
    clusters = table_ref.shape[1]
    own = device // 2
    sign = jnp.where(first, -1, 1)
    row = picked_row(table_ref[...], own)
    near = near_ref[...].astype(F32)
    far = far_ref[...].astype(F32)
    total = None
    for s in range(3):
        entry = row[s : s + 1]
        chosen = near * offset_mask(entry, own, 2 * sign, clusters)
        chosen = chosen + far * offset_mask(entry, own, 3 * sign, clusters)
        chosen = chosen.astype(BF16)
        mine = pack_ref[768 + 128 * s : 896 + 128 * s]
        other = got_ref[768 + 128 * s : 896 + 128 * s]
        term = nn(chosen[:, 0:128], jnp.where(first, mine, other))
        term = term + nn(chosen[:, 128:256], jnp.where(first, other, mine))
        total = term if total is None else total + term
    one_ref[...] = total

    leaves = clusters * 4
    cross = [cross_ref[128 * n : 128 * (n + 1)].astype(F32) for n in range(3)]
    partner = [got_ref[128 * n : 128 * (n + 1)].astype(F32) for n in range(2)]
    send_ref[...] = jnp.where(first, cross_ref[256:384], cross_ref[0:128])

    def either(a, b):
        return jnp.where(first, a, b)

    nothing = jnp.zeros_like(cross[0])
    tables = (
        (
            (-3, either(cross[0], nothing)),
            (-2, either(cross[1], partner[0])),
            (2, either(partner[0], cross[0])),
            (3, either(partner[1], cross[1])),
        ),
        (
            (-3, either(cross[1], partner[0])),
            (-2, either(cross[2], partner[1])),
            (2, either(partner[1], cross[1])),
            (3, either(nothing, cross[2])),
        ),
    )
    weight = None
    for i in range(2):
        leaf = 2 * device + i
        total = None
        for s in range(3):
            entry = leaf_ref[i : i + 1, s : s + 1]
            chosen = None
            for offset, value in tables[i]:
                term = value * offset_mask(entry, leaf, offset, leaves)
                chosen = term if chosen is None else chosen + term
            block = c0_ref[s, i * rank : (i + 1) * rank]
            term = nn(chosen.astype(BF16), block)
            total = term if total is None else total + term
            edge = offset_mask(entry, leaf, 3 if i else -3, leaves)
            edge = edge * jnp.where(core == (1 - i), 1.0, 0.0)
            term = block.astype(F32) * edge
            weight = term if weight is None else weight + term
        zero_ref[128 * i : 128 * (i + 1)] = total
    weight_ref[...] = weight.astype(BF16)

    pieces = []
    ahead = []
    for h in range(2):
        paired = got_ref[384 + 128 * h : 512 + 128 * h]
        crossed = cross_ref[384 + 128 * h : 512 + 128 * h]
        pieces.append(jnp.where(first, crossed, paired))
        ahead.append(jnp.where(first, paired, crossed))
    incoming = jnp.concatenate(pieces, 1).astype(F32).T
    following = jnp.concatenate(
        [ahead[0][:, 0:128], ahead[1][:, 0:128], ahead[0][:, 128:256], ahead[1][:, 128:256]], 0
    )
    field_ref[0:points] = part_ref[0:points] + incoming
    field_ref[points : 2 * points] = part_ref[points : 2 * points] + nn(
        next_ref[points : 2 * points], following
    )


def share_body(gathered_ref, one_ref, pack_ref, got_ref, send_ref, out_ref):
    first = (lax.axis_index("curve") & 1) == 0
    mine = pack_ref[640:768]
    other = got_ref[640:768]
    total = gathered_ref[0].astype(F32)
    for i in range(1, 4):
        total = total + gathered_ref[i].astype(F32)
    total = total.astype(BF16)
    top = nt(total, jnp.where(first, mine, other))
    bottom = nt(total, jnp.where(first, other, mine))
    out_ref[0:128] = (one_ref[...] + jnp.concatenate([top, bottom], 1)).astype(BF16)
    out_ref[128:256] = send_ref[...]


def last_body(points, rank, mine_ref, got_ref, zero_ref, weight_ref, e1_ref, basis_ref, field_ref, out_ref):
    core = lax.axis_index("curve") & 1
    one = (mine_ref[0:128].astype(F32) + got_ref[0:128].astype(F32)).astype(BF16)
    extra = nn(got_ref[128:256], weight_ref[...])
    for i in range(2):
        used = jnp.where(core == (1 - i), 1.0, 0.0)
        zero = zero_ref[128 * i : 128 * (i + 1)] + extra * used
        zero = zero + nt(one, e1_ref[i * rank : (i + 1) * rank])
        field = nt(basis_ref[i * points : (i + 1) * points], zero.astype(BF16))
        out_ref[i * points : (i + 1) * points] = (
            field_ref[i * points : (i + 1) * points] + field
        ).astype(BF16)


def local_part(
    vectors,
    near_self,
    near_next,
    leaf_basis,
    transfer_one,
    transfer_two,
    coupling_zero,
    coupling_one,
    coupling_two,
    list_zero,
    list_one,
    list_two,
):
    size = lax.axis_size("curve")
    rank = leaf_basis.shape[1]
    points = near_self.shape[1]
    c0 = jnp.transpose(coupling_zero, (1, 0, 2))
    c1 = jnp.transpose(coupling_one, (1, 0, 2))
    c2 = jnp.transpose(coupling_two, (1, 0, 2))
    table_one = list_one.T
    table_two = list_two.T

    (spread,) = call(spread_body, [((8, 2, 32, 256), BF16)], 1 << 18, table_two, c2)
    weights_two = lax.all_to_all(
        spread, "curve", 0, 0, axis_index_groups=cluster_groups(size)
    )
    pack, near_cross = call(
        functools.partial(first_body, points, rank),
        [((1152, 256), BF16), ((256, 256), BF16)],
        160 << 20,
        leaf_basis,
        vectors,
        transfer_one,
        near_next,
        transfer_two,
        c1,
        far=True,
        scratch=[
            pltpu.VMEM((2 * points, rank), BF16),
            pltpu.VMEM((2 * points, 128), BF16),
            pltpu.VMEM((2 * rank, rank), BF16),
            pltpu.VMEM((points, points), BF16),
            pltpu.SemaphoreType.DMA((10,)),
        ],
    )
    got = core_swap(pack)
    one, two = call(second_body, [((128, 256), BF16), ((128, 256), BF16)], 16 << 20, pack, got)
    two_far = third_cluster(two)
    two_near = far_route(two, 8)
    (leaves,) = call(cross_body, [((640, 256), BF16)], 1 << 18, pack, got, near_cross)
    crossed = chip_swap(leaves)
    one_near = far_route(one, 2)
    one_far = far_route(one, 3)
    (near_part,) = call(
        functools.partial(near_body, points),
        [((2 * points, 128), F32)],
        320 << 20,
        near_self,
        near_next,
        vectors,
    )
    (coupled,) = call(
        couple_two_body, [((4, 128, 256), BF16)], 32 << 20, two_near, two_far, weights_two
    )
    gathered = lax.all_to_all(coupled, "curve", 0, 0, axis_index_groups=chip_groups(size))
    far_one, far_zero, weight, field, send = call(
        functools.partial(gather_body, points, rank),
        [
            ((128, 256), F32),
            ((256, 256), F32),
            ((256, 256), BF16),
            ((2 * points, 128), F32),
            ((128, 256), BF16),
        ],
        220 << 20,
        table_one,
        list_zero,
        pack,
        got,
        one_near,
        one_far,
        crossed,
        c0,
        near_part,
        near_next,
    )
    (share,) = call(share_body, [((256, 256), BF16)], 16 << 20, gathered, far_one, pack, got, send)
    last = core_swap(share)
    (out,) = call(
        functools.partial(last_body, points, rank),
        [((2 * points, 128), BF16)],
        120 << 20,
        share,
        last,
        far_zero,
        weight,
        transfer_one,
        leaf_basis,
        field,
    )
    return out


def solution(mesh):
    rows = P("curve", None)
    cube = P("curve", None, None)
    return jax.shard_map(
        local_part,
        mesh=mesh,
        in_specs=(rows, rows, rows, rows, rows, rows, cube, cube, cube, rows, P(), P()),
        out_specs=rows,
        check_vma=False,
    )
```

time: 97.4 us -> 75.2 us (0.77)
  matrix products: 17.5 us -> 0 us
  Pallas kernels: 0 us -> 7.4 us
  local copies, waits for them, and re-layouts: 11.5 us -> 5.24 us
  other arithmetic: 4.03 us -> 0 us
  waiting for transfers between devices: 9.44 us -> 5.61 us
  starting transfers between devices: 53.3 us -> 56.1 us
    dot_general x26 -> x0, matrix products: 17.5 us -> none  [the longest x19 9.73 us: dot_tn(): lax.dot_general(a, b, (((0,), (0,)), ((), ())), preferred_element_type=F32)]
    pallas_call x0 -> x9, Pallas kernels: none -> 7.4 us  [call(): pl.pallas_call(body, out_shape=[jax.ShapeDtypeStruct(s, t) for s, t in ou...]
    all_to_all x2, waiting for transfers between devices: 5.86 us -> 0.01 us  [the longest x1 0.01 us: local_part(): lax.all_to_all(spread, 'curve', 0, 0, axis_index_groups=cluster_groups(si...]
    ppermute x7, starting transfers between devices: 45.4 us -> 49.2 us  [route(): lax.ppermute(value, 'curve', [(source_of(i) % size, i) for i in range(siz...]
    unnamed x46 -> x32, local copies, waits for them, and re-layouts: 8.52 us -> 5.24 us
    ppermute x7, waiting for transfers between devices: 3.58 us -> 5.6 us  [route(): lax.ppermute(value, 'curve', [(source_of(i) % size, i) for i in range(siz...]
    concatenate x4 -> x0, other arithmetic: 1.54 us -> none  [the longest x1 0.75 us: per_device(): jnp.concatenate([jnp.where(first, coef[0], partner_coef[1]), jnp.where(fi...]
    gather x4 -> x0, local copies, waits for them, and re-layouts: 1.46 us -> none  [the longest x3 0.83 us: per_device(): index = jnp.take_along_axis(places, code, axis=1)]
  transfers between devices with their start and end apart: 9 -> 9, of which waited for: 4 -> 3; matrix products, arithmetic and copies ran while one was open for 14% -> 0% of each run, Pallas kernels for 0% -> 3%
where the time goes in v2:
time: 75.2 us; the launch traced here: 74.6 us
  starting transfers between devices  56.1 us (75%)
  Pallas kernels  7.4 us (10%)
  waiting for transfers between devices  5.61 us (7%)
  local copies, waits for them, and re-layouts  5.24 us (7%)
    ppermute x7, starting transfers between devices, route(): lax.ppermute(value, 'curve', [(source_of(i) % size, i) for i in range(siz...  49.2 us
    pallas_call x9, Pallas kernels, call(): pl.pallas_call(body, out_shape=[jax.ShapeDtypeStruct(s, t) for s, t in ou...  7.4 us
    ppermute x7, waiting for transfers between devices, route(): lax.ppermute(value, 'curve', [(source_of(i) % size, i) for i in range(siz...  5.6 us
    unnamed x32, local copies, waits for them, and re-layouts  5.24 us
    all_to_all x1, starting transfers between devices, local_part(): lax.all_to_all(coupled, 'curve', 0, 0, axis_index_groups=chip_groups(size))  3.54 us
    all_to_all x1, starting transfers between devices, local_part(): lax.all_to_all(spread, 'curve', 0, 0, axis_index_groups=cluster_groups(si...  3.36 us
  transfers between devices with their start and end apart: 9, of which 3 were waited for; matrix products, arithmetic and copies ran while one was open for 0% of the time, Pallas kernels for 3%

profile of v2, /device:TPU:1, one launch (start us, length us, event | category | flops | bytes accessed | tf_op | source)
XLA Modules:
  0.0 74.6 jit_solution(13815600136713017465)
XLA Ops:
  0.0 0.0 copy-start.10
  0.0 2.1 %shard_map.118 = (bf16[1152,256]{1,0:T(8,128)(2,1)S(1)}, bf16[256,256]{1,0:T(8,128)(2,1)S(1)}) custom-call(bf16[1024,256]{1,0:T(8,128)(2,1)} %basis_ref.1, bf16[1024,128]{1,0:T(8,128)(2,1)} %x_ref.1, bf16[512,256]{1,0:T(8,128)(2,1)} %e1_ref.1, bf16[1024,512]{1,0:T(8,128)(2,1)} %next_ref.3, bf16[128,256]{1,0:T(8,128)(2,1)} %e2_hbm.1, bf16[3,128,256]{2,1,0:T(8,128)(2,1)} %bitcast.9), custom_call_target="tpu_custom_call" | custom-call | flops 167772160 | bytes 2359296 | tf_op jit(solution)/shard_map/pallas_call | solution.py:62
  2.1 0.0 copy-start.6
  2.1 0.6 copy-done.6
  2.7 0.0 copy-start.12
  2.7 8.9 %collective-permute-start = (bf16[1152,256]{1,0:T(8,128)(2,1)S(1)}, bf16[1152,256]{1,0:T(8,128)(2,1)S(1)}, u32[]{:S(2)}, u32[]{:S(2)}) collective-permute-start(bf16[1152,256]{1,0:T(8,128)(2,1)S(1)} %get-tuple-element.14.pack_ref), channel_id=1, source_target_pairs={{1,0},{0,1},{3,2},{2,3},{5,4},{4,5},{7,6},{6,7},{9,8},{8,9},{11,10... | collective-permute-start | bytes 1769480 | tf_op jit(solution)/shard_map/ppermute | solution.py:18
  11.6 0.0 copy-done.10
  11.6 0.0 copy-done.12
  11.6 0.8 %shard_map.120 = bf16[8,2,32,256]{3,2,1,0:T(8,128)(2,1)} custom-call(s32[3,64]{1,0:T(4,128)S(1)} %bitcast.8, bf16[3,32,256]{2,1,0:T(8,128)(2,1)S(1)} %bitcast.6), custom_call_target="tpu_custom_call" | custom-call | flops 262144 | bytes 49920 | tf_op jit(solution)/shard_map/pallas_call | solution.py:62
  12.5 3.4 %all-to-all-start = ((bf16[8,2,32,256]{3,2,1,0:T(8,128)(2,1)}), bf16[8,2,32,256]{3,2,1,0:T(8,128)(2,1)S(1)}, u32[]{:S(2)}, u32[]{:S(2)}) async-start(bf16[8,2,32,256]{3,2,1,0:T(8,128)(2,1)} %shard_map.120), calls=%async_computation | async-start | bytes 524288 | tf_op jit(solution)/shard_map/all_to_all | solution.py:336
  15.8 0.0 collective-permute-done.got_ref
  15.8 0.2 shard_map.119
  16.0 0.0 copy-start.14
  16.0 0.6 copy-done.14
  16.6 5.9 %collective-permute-start.1 = (bf16[128,256]{1,0:T(8,128)(2,1)S(1)}, bf16[128,256]{1,0:T(8,128)(2,1)S(1)}, u32[]{:S(2)}, u32[]{:S(2)}) collective-permute-start(bf16[128,256]{1,0:T(8,128)(2,1)S(1)} %get-tuple-element.15), channel_id=1, source_target_pairs={{496,0},{17,1},{498,2},{19,3},{500,4},{21,5},{502,6},{23,7},{504,8... | collective-permute-start | bytes 196616 | tf_op jit(solution)/shard_map/ppermute | solution.py:18
  22.6 9.7 %collective-permute-start.2 = (bf16[128,256]{1,0:T(8,128)(2,1)S(1)}, bf16[128,256]{1,0:T(8,128)(2,1)S(1)}, u32[]{:S(2)}, u32[]{:S(2)}) collective-permute-start(bf16[128,256]{1,0:T(8,128)(2,1)S(1)} %get-tuple-element.15), channel_id=1, source_target_pairs={{492,0},{29,1},{494,2},{31,3},{488,4},{25,5},{490,6},{27,7},{500,8... | collective-permute-start | bytes 196616 | tf_op jit(solution)/shard_map/ppermute | solution.py:18
  32.3 0.0 all-to-all-done.weights_ref
  32.3 0.0 collective-permute-done.1.near_ref
  32.3 1.4 %collective-permute-done.2.far_ref = bf16[128,256]{1,0:T(8,128)(2,1)S(1)} collective-permute-done((bf16[128,256]{1,0:T(8,128)(2,1)S(1)}, bf16[128,256]{1,0:T(8,128)(2,1)S(1)}, u32[]{:S(2)}, u32[]{:S(2)}) %collective-permute-start.2) | collective-permute-done | bytes 65568 | tf_op jit(solution)/shard_map/ppermute | solution.py:18
  33.7 1.1 %shard_map.121 = bf16[4,128,256]{2,1,0:T(8,128)(2,1)} custom-call(bf16[128,256]{1,0:T(8,128)(2,1)S(1)} %collective-permute-done.1.near_ref, bf16[128,256]{1,0:T(8,128)(2,1)S(1)} %collective-permute-done.2.far_ref, bf16[8,2,32,256]{3,2,1,0:T(8,128)(2,1)S(1)} %all-to-all-done.weights_ref), custom_call_target="tpu_custom_call" | custom-call | flops 33554432 | bytes 393216 | tf_op jit(solution)/shard_map/pallas_call | solution.py:62
  34.8 0.0 copy-start
  34.8 0.0 copy-start.3
  34.8 3.5 %all-to-all-start.1 = ((bf16[4,128,256]{2,1,0:T(8,128)(2,1)}), bf16[4,128,256]{2,1,0:T(8,128)(2,1)S(1)}, u32[]{:S(2)}, u32[]{:S(2)}) async-start(bf16[4,128,256]{2,1,0:T(8,128)(2,1)} %shard_map.121), calls=%async_computation.1 | async-start | bytes 524288 | tf_op jit(solution)/shard_map/all_to_all | solution.py:377
  38.3 0.0 copy-start.7
  38.4 0.9 %copy-done.7 = bf16[256,256]{1,0:T(8,128)(2,1)S(1)} copy-done((bf16[256,256]{1,0:T(8,128)(2,1)S(1)}, bf16[256,256]{1,0:T(8,128)(2,1)}, u32[]{:S(2)}) %copy-start.7) | copy-done | bytes 131096
  39.2 0.0 copy-start.15
  39.3 5.3 %collective-permute-start.5 = (bf16[640,256]{1,0:T(8,128)(2,1)S(1)}, bf16[640,256]{1,0:T(8,128)(2,1)S(1)}, u32[]{:S(2)}, u32[]{:S(2)}) collective-permute-start(bf16[640,256]{1,0:T(8,128)(2,1)S(1)} %shard_map.122), channel_id=1, source_target_pairs={{511,0},{2,1},{1,2},{4,3},{3,4},{6,5},{5,6},{8,7},{7,8},{10,9},{9,... | collective-permute-start | bytes 983048 | tf_op jit(solution)/shard_map/ppermute | solution.py:18
  44.6 0.0 copy-done.15
  44.6 8.5 %collective-permute-start.3 = (bf16[128,256]{1,0:T(8,128)(2,1)S(1)}, bf16[128,256]{1,0:T(8,128)(2,1)S(1)}, u32[]{:S(2)}, u32[]{:S(2)}) collective-permute-start(bf16[128,256]{1,0:T(8,128)(2,1)S(1)} %copy-done.15), channel_id=1, source_target_pairs={{508,0},{5,1},{510,2},{7,3},{0,4},{9,5},{2,6},{11,7},{4,8},{13,9},... | collective-permute-start | bytes 196616 | tf_op jit(solution)/shard_map/ppermute | solution.py:18
  53.1 1.9 %collective-permute-start.4 = (bf16[128,256]{1,0:T(8,128)(2,1)S(1)}, bf16[128,256]{1,0:T(8,128)(2,1)S(1)}, u32[]{:S(2)}, u32[]{:S(2)}) collective-permute-start(bf16[128,256]{1,0:T(8,128)(2,1)S(1)} %copy-done.15), channel_id=1, source_target_pairs={{506,0},{7,1},{508,2},{9,3},{510,4},{11,5},{0,6},{13,7},{2,8},{15,... | collective-permute-start | bytes 196616 | tf_op jit(solution)/shard_map/ppermute | solution.py:18
  55.0 0.0 copy-done
  55.0 0.0 copy-done.3
  55.0 0.0 copy-start.4
  55.1 0.9 %copy-done.4 = bf16[1024,128]{1,0:T(8,128)(2,1)S(1)} copy-done((bf16[1024,128]{1,0:T(8,128)(2,1)S(1)}, bf16[1024,128]{1,0:T(8,128)(2,1)}, u32[]{:S(2)}) %copy-start.4) | copy-done | bytes 262168
  56.0 0.0 copy-start.5
  56.0 0.0 copy-start.11
  56.0 0.6 shard_map.123.part_ref
  56.6 0.0 collective-permute-done.3.near_ref
  56.7 3.2 %collective-permute-done.4.far_ref = bf16[128,256]{1,0:T(8,128)(2,1)S(1)} collective-permute-done((bf16[128,256]{1,0:T(8,128)(2,1)S(1)}, bf16[128,256]{1,0:T(8,128)(2,1)S(1)}, u32[]{:S(2)}, u32[]{:S(2)}) %collective-permute-start.4) | collective-permute-done | bytes 65568 | tf_op jit(solution)/shard_map/ppermute | solution.py:18
  59.9 0.0 collective-permute-done.5.cross_ref
  59.9 0.0 copy-start.13
  59.9 0.0 copy-done.5
  59.9 0.0 copy-done.11
  59.9 0.7 copy-done.13
  60.6 0.9 %shard_map.124 = (f32[128,256]{1,0:T(8,128)S(1)}, f32[256,256]{1,0:T(8,128)S(1)}, bf16[256,256]{1,0:T(8,128)(2,1)S(1)}, f32[1024,128]{1,0:T(8,128)S(1)}, bf16[128,256]{1,0:T(8,128)(2,1)S(1)}) custom-call(s32[3,256]{1,0:T(4,128)S(1)} %bitcast.7, s32[2,3]{1,0:T(2,128)S(1)} %copy-done.13, bf16[1152,256]{1,0:T(8,128)(2,1)S(1)} %get-tuple-element.14.pack_ref, ...), custom_call_target="tpu_custom_call" | custom-call | flops 230686720 | bytes 4000792 | tf_op jit(solution)/shard_map/pallas_call | solution.py:62
  61.5 0.0 copy-start.8
  61.5 0.6 copy-done.8
  62.1 0.0 all-to-all-done.1.gathered_ref
  62.1 0.0 copy-start.9
  62.1 0.8 %copy-done.9 = bf16[128,256]{1,0:T(8,128)(2,1)S(1)} copy-done((bf16[128,256]{1,0:T(8,128)(2,1)S(1)}, bf16[128,256]{1,0:T(8,128)(2,1)}, u32[]{:S(2)}) %copy-start.9) | copy-done | bytes 65560
  62.9 0.0 copy-start.1
  62.9 0.0 copy-start.2
  62.9 0.2 shard_map.125.mine_ref
  63.1 9.0 %collective-permute-start.6 = (bf16[256,256]{1,0:T(8,128)(2,1)S(1)}, bf16[256,256]{1,0:T(8,128)(2,1)S(1)}, u32[]{:S(2)}, u32[]{:S(2)}) collective-permute-start(bf16[256,256]{1,0:T(8,128)(2,1)S(1)} %shard_map.125.mine_ref), channel_id=1, source_target_pairs={{1,0},{0,1},{3,2},{2,3},{5,4},{4,5},{7,6},{6,7},{9,8},{8,9},{11,10... | collective-permute-start | bytes 393224 | tf_op jit(solution)/shard_map/ppermute | solution.py:18
  72.1 1.0 %collective-permute-done.6.got_ref = bf16[256,256]{1,0:T(8,128)(2,1)S(1)} collective-permute-done((bf16[256,256]{1,0:T(8,128)(2,1)S(1)}, bf16[256,256]{1,0:T(8,128)(2,1)S(1)}, u32[]{:S(2)}, u32[]{:S(2)}) %collective-permute-start.6) | collective-permute-done | bytes 131104 | tf_op jit(solution)/shard_map/ppermute | solution.py:18
  73.1 0.0 copy-done.1
  73.1 0.0 copy-done.2
  73.1 1.5 %shard_map.126 = bf16[1024,128]{1,0:T(8,128)(2,1)} custom-call(bf16[256,256]{1,0:T(8,128)(2,1)S(1)} %shard_map.125.mine_ref, bf16[256,256]{1,0:T(8,128)(2,1)S(1)} %collective-permute-done.6.got_ref, f32[256,256]{1,0:T(8,128)S(1)} %get-tuple-element.20.zero_ref, bf16[256,256]{1,0:T(8,128)(2,1)S(1)} %get-tuple-element.21.weight_ref, ...), custom_call_target="tpu_custom_call" | custom-call | flops 125829120 | bytes 1966080 | tf_op jit(solution)/shard_map/pallas_call | solution.py:62
  (1 shorter events, 0.0 us)
Async XLA Ops:
  0.0 11.6 %copy-start.10 = (bf16[32,3,256]{2,0,1:T(8,128)(2,1)S(1)}, bf16[32,3,256]{2,0,1:T(8,128)(2,1)}, u32[]{:S(2)}) copy-start(bf16[32,3,256]{2,0,1:T(8,128)(2,1)} %param.20) | copy-start | bytes 147460
  2.1 0.7 copy-start.6
  2.7 8.9 %copy-start.12 = (s32[64,3]{0,1:T(4,128)S(1)}, s32[64,3]{0,1:T(4,128)}, u32[]{:S(2)}) copy-start(s32[64,3]{0,1:T(4,128)} %param.23) | copy-start | bytes 2308
  2.7 13.1 %collective-permute-start = (bf16[1152,256]{1,0:T(8,128)(2,1)S(1)}, bf16[1152,256]{1,0:T(8,128)(2,1)S(1)}, u32[]{:S(2)}, u32[]{:S(2)}) collective-permute-start(bf16[1152,256]{1,0:T(8,128)(2,1)S(1)} %get-tuple-element.14.pack_ref), channel_id=1, source_target_pairs={{1,0},{0,1},{3,2},{2,3},{5,4},{4,5},{7,6},{6,7},{9,8},{8,9},{11,10... | collective-permute-start | bytes 1769480 | tf_op jit(solution)/shard_map/ppermute | solution.py:18
  12.5 19.8 %all-to-all-start = ((bf16[8,2,32,256]{3,2,1,0:T(8,128)(2,1)}), bf16[8,2,32,256]{3,2,1,0:T(8,128)(2,1)S(1)}, u32[]{:S(2)}, u32[]{:S(2)}) async-start(bf16[8,2,32,256]{3,2,1,0:T(8,128)(2,1)} %shard_map.120), calls=%async_computation | async-start | bytes 524288 | tf_op jit(solution)/shard_map/all_to_all | solution.py:336
  16.0 0.6 copy-start.14
  16.6 15.6 %collective-permute-start.1 = (bf16[128,256]{1,0:T(8,128)(2,1)S(1)}, bf16[128,256]{1,0:T(8,128)(2,1)S(1)}, u32[]{:S(2)}, u32[]{:S(2)}) collective-permute-start(bf16[128,256]{1,0:T(8,128)(2,1)S(1)} %get-tuple-element.15), channel_id=1, source_target_pairs={{496,0},{17,1},{498,2},{19,3},{500,4},{21,5},{502,6},{23,7},{504,8... | collective-permute-start | bytes 196616 | tf_op jit(solution)/shard_map/ppermute | solution.py:18
  22.6 11.1 %collective-permute-start.2 = (bf16[128,256]{1,0:T(8,128)(2,1)S(1)}, bf16[128,256]{1,0:T(8,128)(2,1)S(1)}, u32[]{:S(2)}, u32[]{:S(2)}) collective-permute-start(bf16[128,256]{1,0:T(8,128)(2,1)S(1)} %get-tuple-element.15), channel_id=1, source_target_pairs={{492,0},{29,1},{494,2},{31,3},{488,4},{25,5},{490,6},{27,7},{500,8... | collective-permute-start | bytes 196616 | tf_op jit(solution)/shard_map/ppermute | solution.py:18
  34.8 20.2 %copy-start = (bf16[1024,512]{1,0:T(8,128)(2,1)S(1)}, bf16[1024,512]{1,0:T(8,128)(2,1)}, u32[]{:S(2)}) copy-start(bf16[1024,512]{1,0:T(8,128)(2,1)} %next_ref.3) | copy-start | bytes 3145732
  34.8 20.2 %copy-start.3 = (bf16[1024,512]{1,0:T(8,128)(2,1)S(1)}, bf16[1024,512]{1,0:T(8,128)(2,1)}, u32[]{:S(2)}) copy-start(bf16[1024,512]{1,0:T(8,128)(2,1)} %self_ref.1) | copy-start | bytes 3145732
  34.8 27.3 %all-to-all-start.1 = ((bf16[4,128,256]{2,1,0:T(8,128)(2,1)}), bf16[4,128,256]{2,1,0:T(8,128)(2,1)S(1)}, u32[]{:S(2)}, u32[]{:S(2)}) async-start(bf16[4,128,256]{2,1,0:T(8,128)(2,1)} %shard_map.121), calls=%async_computation.1 | async-start | bytes 524288 | tf_op jit(solution)/shard_map/all_to_all | solution.py:377
  38.3 0.9 %copy-start.7 = (bf16[256,256]{1,0:T(8,128)(2,1)S(1)}, bf16[256,256]{1,0:T(8,128)(2,1)}, u32[]{:S(2)}) copy-start(bf16[256,256]{1,0:T(8,128)(2,1)} %copy-done.6) | copy-start | bytes 393220
  39.2 5.4 %copy-start.15 = (bf16[128,256]{1,0:T(8,128)(2,1)S(1)}, bf16[128,256]{1,0:T(8,128)(2,1)}, u32[]{:S(2)}) copy-start(bf16[128,256]{1,0:T(8,128)(2,1)} %copy-done.14) | copy-start | bytes 196612
  39.3 20.6 %collective-permute-start.5 = (bf16[640,256]{1,0:T(8,128)(2,1)S(1)}, bf16[640,256]{1,0:T(8,128)(2,1)S(1)}, u32[]{:S(2)}, u32[]{:S(2)}) collective-permute-start(bf16[640,256]{1,0:T(8,128)(2,1)S(1)} %shard_map.122), channel_id=1, source_target_pairs={{511,0},{2,1},{1,2},{4,3},{3,4},{6,5},{5,6},{8,7},{7,8},{10,9},{9,... | collective-permute-start | bytes 983048 | tf_op jit(solution)/shard_map/ppermute | solution.py:18
  44.6 12.0 %collective-permute-start.3 = (bf16[128,256]{1,0:T(8,128)(2,1)S(1)}, bf16[128,256]{1,0:T(8,128)(2,1)S(1)}, u32[]{:S(2)}, u32[]{:S(2)}) collective-permute-start(bf16[128,256]{1,0:T(8,128)(2,1)S(1)} %copy-done.15), channel_id=1, source_target_pairs={{508,0},{5,1},{510,2},{7,3},{0,4},{9,5},{2,6},{11,7},{4,8},{13,9},... | collective-permute-start | bytes 196616 | tf_op jit(solution)/shard_map/ppermute | solution.py:18
  53.1 6.8 %collective-permute-start.4 = (bf16[128,256]{1,0:T(8,128)(2,1)S(1)}, bf16[128,256]{1,0:T(8,128)(2,1)S(1)}, u32[]{:S(2)}, u32[]{:S(2)}) collective-permute-start(bf16[128,256]{1,0:T(8,128)(2,1)S(1)} %copy-done.15), channel_id=1, source_target_pairs={{506,0},{7,1},{508,2},{9,3},{510,4},{11,5},{0,6},{13,7},{2,8},{15,... | collective-permute-start | bytes 196616 | tf_op jit(solution)/shard_map/ppermute | solution.py:18
  55.0 1.0 %copy-start.4 = (bf16[1024,128]{1,0:T(8,128)(2,1)S(1)}, bf16[1024,128]{1,0:T(8,128)(2,1)}, u32[]{:S(2)}) copy-start(bf16[1024,128]{1,0:T(8,128)(2,1)} %x_ref.1) | copy-start | bytes 786436
  56.0 3.9 %copy-start.5 = (bf16[512,3,256]{2,0,1:T(8,128)(2,1)S(1)}, bf16[512,3,256]{2,0,1:T(8,128)(2,1)}, u32[]{:S(2)}) copy-start(bf16[512,3,256]{2,0,1:T(8,128)(2,1)} %param.18) | copy-start | bytes 2359300
  56.0 3.9 %copy-start.11 = (s32[256,3]{0,1:T(4,128)S(1)}, s32[256,3]{0,1:T(4,128)}, u32[]{:S(2)}) copy-start(s32[256,3]{0,1:T(4,128)} %param.22) | copy-start | bytes 9220
  59.9 0.7 copy-start.13
  61.5 0.6 copy-start.8
  62.1 0.8 %copy-start.9 = (bf16[128,256]{1,0:T(8,128)(2,1)S(1)}, bf16[128,256]{1,0:T(8,128)(2,1)}, u32[]{:S(2)}) copy-start(bf16[128,256]{1,0:T(8,128)(2,1)} %copy-done.8) | copy-start | bytes 196612
  62.9 10.2 %copy-start.1 = (bf16[1024,256]{1,0:T(8,128)(2,1)S(1)}, bf16[1024,256]{1,0:T(8,128)(2,1)}, u32[]{:S(2)}) copy-start(bf16[1024,256]{1,0:T(8,128)(2,1)} %basis_ref.1) | copy-start | bytes 1572868
  62.9 10.2 %copy-start.2 = (bf16[512,256]{1,0:T(8,128)(2,1)S(1)}, bf16[512,256]{1,0:T(8,128)(2,1)}, u32[]{:S(2)}) copy-start(bf16[512,256]{1,0:T(8,128)(2,1)} %e1_ref.1) | copy-start | bytes 786436
  63.1 10.0 %collective-permute-start.6 = (bf16[256,256]{1,0:T(8,128)(2,1)S(1)}, bf16[256,256]{1,0:T(8,128)(2,1)S(1)}, u32[]{:S(2)}, u32[]{:S(2)}) collective-permute-start(bf16[256,256]{1,0:T(8,128)(2,1)S(1)} %shard_map.125.mine_ref), channel_id=1, source_target_pairs={{1,0},{0,1},{3,2},{2,3},{5,4},{4,5},{7,6},{6,7},{9,8},{8,9},{11,10... | collective-permute-start | bytes 393224 | tf_op jit(solution)/shard_map/ppermute | solution.py:18

commit v3 on v2

--- a/solution.py
+++ b/solution.py
@@ -54,15 +54,18 @@
     return lax.dot_general(a, b, (((1,), (1,)), ((), ())), preferred_element_type=F32)
 
 
-def call(body, outs, flops, *args, far=False, scratch=(), grant=8):
+def call(body, outs, flops, *args, far=(), scratch=(), grant=8):
     spec = pl.BlockSpec(memory_space=pltpu.VMEM)
     moved = sum(a.size * a.dtype.itemsize for a in args)
-    if far:
-        args = [pltpu.with_memory_space_constraint(a, pltpu.HBM) for a in args]
+    args = [
+        pltpu.with_memory_space_constraint(a, pltpu.HBM) if n in far else a
+        for n, a in enumerate(args)
+    ]
+    hbm = pl.BlockSpec(memory_space=pltpu.HBM)
     return pl.pallas_call(
         body,
         out_shape=[jax.ShapeDtypeStruct(s, t) for s, t in outs],
-        in_specs=[pl.BlockSpec(memory_space=pltpu.HBM) if far else spec] * len(args),
+        in_specs=[hbm if n in far else spec for n in range(len(args))],
         out_specs=[spec] * len(outs),
         scratch_shapes=list(scratch),
         compiler_params=pltpu.CompilerParams(vmem_limit_bytes=grant << 20),
@@ -98,10 +101,9 @@
 
 
 def first_body(
-    points, rank, basis_hbm, x_hbm, e1_hbm, next_hbm, e2_hbm, c1_hbm, pack_ref, cross_ref,
+    points, rank, basis_hbm, x_hbm, e1_hbm, next_hbm, e2_hbm, c1_hbm, pack_ref,
     basis_ref, x_ref, e1_ref, next_ref, sems,
 ):
-    core = lax.axis_index("curve") & 1
     copies = []
     for i in range(2):
         rows = pl.ds(i * points, points)
@@ -109,9 +111,9 @@
         copies.append((basis_hbm.at[rows], basis_ref.at[rows]))
     copies.append((e1_hbm, e1_ref))
     copies.append((next_hbm.at[pl.ds(points, points)], next_ref))
-    copies.append((e2_hbm, pack_ref.at[pl.ds(640, 128)]))
+    copies.append((e2_hbm, pack_ref.at[pl.ds(896, 128)]))
     for s in range(3):
-        copies.append((c1_hbm.at[s], pack_ref.at[pl.ds(768 + 128 * s, 128)]))
+        copies.append((c1_hbm.at[s], pack_ref.at[pl.ds(1024 + 128 * s, 128)]))
     moves = [pltpu.make_async_copy(a, b, sems.at[n]) for n, (a, b) in enumerate(copies)]
     for move in moves:
         move.start()
@@ -128,14 +130,11 @@
     pack_ref[256:384] = part.astype(BF16)
     moves[5].wait()
     outgoing = nn(turned, next_ref[...]).astype(BF16)
-    first = core == 0
     for h in range(2):
-        sent = outgoing[:, 256 * h : 256 * (h + 1)]
-        low = x_ref[128 * h : 128 * (h + 1)]
-        high = x_ref[256 + 128 * h : 256 + 128 * (h + 1)]
-        ahead = jnp.concatenate([low, high], 1)
-        pack_ref[384 + 128 * h : 512 + 128 * h] = jnp.where(first, sent, ahead)
-        cross_ref[128 * h : 128 * (h + 1)] = jnp.where(first, ahead, sent)
+        pack_ref[384 + 128 * h : 512 + 128 * h] = outgoing[:, 256 * h : 256 * (h + 1)]
+        for v in range(2):
+            rows = x_ref[256 * v + 128 * h : 256 * v + 128 * (h + 1)]
+            pack_ref[640 + 128 * h : 768 + 128 * h, 128 * v : 128 * (v + 1)] = rows
     for move in moves[6:]:
         move.wait()
 
@@ -144,38 +143,31 @@
     first = (lax.axis_index("curve") & 1) == 0
     one = (pack_ref[256:384].astype(F32) + got_ref[256:384].astype(F32)).astype(BF16)
     one_ref[...] = one
-    mine = pack_ref[640:768]
-    other = got_ref[640:768]
+    mine = pack_ref[896:1024]
+    other = got_ref[896:1024]
     top = jnp.where(first, mine, other)
     bottom = jnp.where(first, other, mine)
     two_ref[...] = (nn(one[:, 0:128], top) + nn(one[:, 128:256], bottom)).astype(BF16)
 
 
-def cross_body(pack_ref, got_ref, near_ref, out_ref):
+def cross_body(pack_ref, got_ref, one_ref, out_ref):
     first = (lax.axis_index("curve") & 1) == 0
     out_ref[0:128] = jnp.where(first, pack_ref[0:128], got_ref[128:256])
     out_ref[128:256] = jnp.where(first, pack_ref[128:256], pack_ref[0:128])
     out_ref[256:384] = jnp.where(first, got_ref[0:128], pack_ref[128:256])
-    out_ref[384:640] = near_ref[...]
-
-
-def near_body(points, self_ref, next_ref, x_ref, out_ref):
-    x0 = x_ref[0:points]
-    x1 = x_ref[points : 2 * points]
-    out_ref[0:points] = nn(self_ref[0:points], x0) + nn(next_ref[0:points], x1)
-    inner = nn(x0.T, next_ref[0:points])
-    out_ref[points : 2 * points] = nn(self_ref[points : 2 * points], x1) + inner.T
+    out_ref[384:640] = jnp.where(first, pack_ref[640:896], pack_ref[384:640])
+    out_ref[640:768] = one_ref[...]
+
+
+def bundle_body(one_ref, cross_ref, out_ref):
+    out_ref[0:128] = one_ref[...]
+    out_ref[128:256] = cross_ref[640:768]
 
 
 def couple_two_body(near_ref, far_ref, weights_ref, out_ref):
-    near = near_ref[...]
-    far = far_ref[...]
-    total = None
-    for m in range(8):
-        piece = nn(near[:, 32 * m : 32 * (m + 1)], weights_ref[m, 0])
-        piece = piece + nn(far[:, 32 * m : 32 * (m + 1)], weights_ref[m, 1])
-        total = piece if total is None else total + piece
-    value = total.astype(BF16)
+    first = weights_ref[:, 0].reshape(256, 256)
+    second = weights_ref[:, 1].reshape(256, 256)
+    value = (nn(near_ref[...], first) + nn(far_ref[...], second)).astype(BF16)
     for i in range(4):
         out_ref[i] = value
 
@@ -185,20 +177,31 @@
     rank,
     table_ref,
     leaf_ref,
-    pack_ref,
     got_ref,
-    near_ref,
-    far_ref,
     cross_ref,
-    c0_ref,
-    part_ref,
-    next_ref,
-    one_ref,
+    c0_hbm,
+    self_hbm,
+    next_hbm,
+    x_hbm,
+    mask_ref,
     zero_ref,
     weight_ref,
     field_ref,
-    send_ref,
+    c0_ref,
+    self_ref,
+    next_ref,
+    x_ref,
+    sems,
 ):
+    copies = [(x_hbm, x_ref)]
+    for i in range(2):
+        rows = pl.ds(i * points, points)
+        copies.append((self_hbm.at[rows], self_ref.at[rows]))
+        copies.append((next_hbm.at[rows], next_ref.at[rows]))
+    copies.append((c0_hbm, c0_ref))
+    moves = [pltpu.make_async_copy(a, b, sems.at[n]) for n, (a, b) in enumerate(copies)]
+    for move in moves:
+        move.start()
     device = lax.axis_index("curve")
     core = device & 1
     first = core == 0
@@ -206,25 +209,51 @@
     own = device // 2
     sign = jnp.where(first, -1, 1)
     row = picked_row(table_ref[...], own)
-    near = near_ref[...].astype(F32)
-    far = far_ref[...].astype(F32)
-    total = None
     for s in range(3):
-        entry = row[s : s + 1]
-        chosen = near * offset_mask(entry, own, 2 * sign, clusters)
-        chosen = chosen + far * offset_mask(entry, own, 3 * sign, clusters)
-        chosen = chosen.astype(BF16)
-        mine = pack_ref[768 + 128 * s : 896 + 128 * s]
-        other = got_ref[768 + 128 * s : 896 + 128 * s]
-        term = nn(chosen[:, 0:128], jnp.where(first, mine, other))
-        term = term + nn(chosen[:, 128:256], jnp.where(first, other, mine))
-        total = term if total is None else total + term
-    one_ref[...] = total
+        for n in range(2):
+            mask = offset_mask(row[s : s + 1], own, (n + 2) * sign, clusters)
+            mask_ref[2 * s + n : 2 * s + n + 1] = jnp.broadcast_to(mask, (1, 256))
+
+    pieces = []
+    ahead = []
+    for h in range(2):
+        pieces.append(
+            jnp.where(
+                first,
+                cross_ref[384 + 128 * h : 512 + 128 * h],
+                got_ref[384 + 128 * h : 512 + 128 * h],
+            )
+        )
+        ahead.append(
+            jnp.where(
+                first,
+                got_ref[640 + 128 * h : 768 + 128 * h],
+                cross_ref[384 + 128 * h : 512 + 128 * h],
+            )
+        )
+    incoming = jnp.concatenate(pieces, 1).astype(F32).T
+    following = jnp.concatenate(
+        [ahead[0][:, 0:128], ahead[1][:, 0:128], ahead[0][:, 128:256], ahead[1][:, 128:256]], 0
+    )
+    moves[0].wait()
+    x0 = x_ref[0:points]
+    x1 = x_ref[points : 2 * points]
+    moves[1].wait()
+    moves[2].wait()
+    top = next_ref[0:points]
+    field_ref[0:points] = nn(self_ref[0:points], x0) + nn(top, x1) + incoming
+    inner = nn(x0.T, top).T
+    moves[3].wait()
+    moves[4].wait()
+    field_ref[points : 2 * points] = (
+        nn(self_ref[points : 2 * points], x1)
+        + nn(next_ref[points : 2 * points], following)
+        + inner
+    )
 
     leaves = clusters * 4
     cross = [cross_ref[128 * n : 128 * (n + 1)].astype(F32) for n in range(3)]
     partner = [got_ref[128 * n : 128 * (n + 1)].astype(F32) for n in range(2)]
-    send_ref[...] = jnp.where(first, cross_ref[256:384], cross_ref[0:128])
 
     def either(a, b):
         return jnp.where(first, a, b)
@@ -244,6 +273,7 @@
             (3, either(nothing, cross[2])),
         ),
     )
+    moves[5].wait()
     weight = None
     for i in range(2):
         leaf = 2 * device + i
@@ -264,35 +294,30 @@
         zero_ref[128 * i : 128 * (i + 1)] = total
     weight_ref[...] = weight.astype(BF16)
 
-    pieces = []
-    ahead = []
-    for h in range(2):
-        paired = got_ref[384 + 128 * h : 512 + 128 * h]
-        crossed = cross_ref[384 + 128 * h : 512 + 128 * h]
-        pieces.append(jnp.where(first, crossed, paired))
-        ahead.append(jnp.where(first, paired, crossed))
-    incoming = jnp.concatenate(pieces, 1).astype(F32).T
-    following = jnp.concatenate(
-        [ahead[0][:, 0:128], ahead[1][:, 0:128], ahead[0][:, 128:256], ahead[1][:, 128:256]], 0
-    )
-    field_ref[0:points] = part_ref[0:points] + incoming
-    field_ref[points : 2 * points] = part_ref[points : 2 * points] + nn(
-        next_ref[points : 2 * points], following
-    )
-
-
-def share_body(gathered_ref, one_ref, pack_ref, got_ref, send_ref, out_ref):
+
+def share_body(gathered_ref, near_ref, mask_ref, pack_ref, got_ref, cross_ref, out_ref):
     first = (lax.axis_index("curve") & 1) == 0
-    mine = pack_ref[640:768]
-    other = got_ref[640:768]
+    near = near_ref[0:128].astype(F32)
+    far = near_ref[128:256].astype(F32)
+    one = None
+    for s in range(3):
+        chosen = near * mask_ref[2 * s : 2 * s + 1] + far * mask_ref[2 * s + 1 : 2 * s + 2]
+        chosen = chosen.astype(BF16)
+        mine = pack_ref[1024 + 128 * s : 1152 + 128 * s]
+        other = got_ref[1024 + 128 * s : 1152 + 128 * s]
+        term = nn(chosen[:, 0:128], jnp.where(first, mine, other))
+        term = term + nn(chosen[:, 128:256], jnp.where(first, other, mine))
+        one = term if one is None else one + term
     total = gathered_ref[0].astype(F32)
     for i in range(1, 4):
         total = total + gathered_ref[i].astype(F32)
     total = total.astype(BF16)
+    mine = pack_ref[896:1024]
+    other = got_ref[896:1024]
     top = nt(total, jnp.where(first, mine, other))
     bottom = nt(total, jnp.where(first, other, mine))
-    out_ref[0:128] = (one_ref[...] + jnp.concatenate([top, bottom], 1)).astype(BF16)
-    out_ref[128:256] = send_ref[...]
+    out_ref[0:128] = (one + jnp.concatenate([top, bottom], 1)).astype(BF16)
+    out_ref[128:256] = jnp.where(first, cross_ref[256:384], cross_ref[0:128])
 
 
 def last_body(points, rank, mine_ref, got_ref, zero_ref, weight_ref, e1_ref, basis_ref, field_ref, out_ref):
@@ -336,9 +361,9 @@
     weights_two = lax.all_to_all(
         spread, "curve", 0, 0, axis_index_groups=cluster_groups(size)
     )
-    pack, near_cross = call(
+    (pack,) = call(
         functools.partial(first_body, points, rank),
-        [((1152, 256), BF16), ((256, 256), BF16)],
+        [((1408, 256), BF16)],
         160 << 20,
         leaf_basis,
         vectors,
@@ -346,7 +371,7 @@
         near_next,
         transfer_two,
         c1,
-        far=True,
+        far=range(6),
         scratch=[
             pltpu.VMEM((2 * points, rank), BF16),
             pltpu.VMEM((2 * points, 128), BF16),
@@ -359,44 +384,43 @@
     one, two = call(second_body, [((128, 256), BF16), ((128, 256), BF16)], 16 << 20, pack, got)
     two_far = third_cluster(two)
     two_near = far_route(two, 8)
-    (leaves,) = call(cross_body, [((640, 256), BF16)], 1 << 18, pack, got, near_cross)
+    (leaves,) = call(cross_body, [((768, 256), BF16)], 1 << 18, pack, got, one)
     crossed = chip_swap(leaves)
-    one_near = far_route(one, 2)
-    one_far = far_route(one, 3)
-    (near_part,) = call(
-        functools.partial(near_body, points),
-        [((2 * points, 128), F32)],
-        320 << 20,
+    (coupled,) = call(
+        couple_two_body, [((4, 128, 256), BF16)], 32 << 20, two_near, two_far, weights_two
+    )
+    gathered = lax.all_to_all(coupled, "curve", 0, 0, axis_index_groups=chip_groups(size))
+    (bundle,) = call(bundle_body, [((256, 256), BF16)], 1 << 18, one, crossed)
+    one_near = far_route(bundle, 2)
+    mask, far_zero, weight, field = call(
+        functools.partial(gather_body, points, rank),
+        [
+            ((8, 256), F32),
+            ((256, 256), F32),
+            ((256, 256), BF16),
+            ((2 * points, 128), F32),
+        ],
+        500 << 20,
+        table_one,
+        list_zero,
+        got,
+        crossed,
+        c0,
         near_self,
         near_next,
         vectors,
-    )
-    (coupled,) = call(
-        couple_two_body, [((4, 128, 256), BF16)], 32 << 20, two_near, two_far, weights_two
-    )
-    gathered = lax.all_to_all(coupled, "curve", 0, 0, axis_index_groups=chip_groups(size))
-    far_one, far_zero, weight, field, send = call(
-        functools.partial(gather_body, points, rank),
-        [
-            ((128, 256), F32),
-            ((256, 256), F32),
-            ((256, 256), BF16),
-            ((2 * points, 128), F32),
-            ((128, 256), BF16),
+        far=range(4, 8),
+        scratch=[
+            pltpu.VMEM(c0.shape, BF16),
+            pltpu.VMEM(near_self.shape, BF16),
+            pltpu.VMEM(near_next.shape, BF16),
+            pltpu.VMEM(vectors.shape, BF16),
+            pltpu.SemaphoreType.DMA((6,)),
         ],
-        220 << 20,
-        table_one,
-        list_zero,
-        pack,
-        got,
-        one_near,
-        one_far,
-        crossed,
-        c0,
-        near_part,
-        near_next,
-    )
-    (share,) = call(share_body, [((256, 256), BF16)], 16 << 20, gathered, far_one, pack, got, send)
+    )
+    (share,) = call(
+        share_body, [((256, 256), BF16)], 16 << 20, gathered, one_near, mask, pack, got, crossed
+    )
     last = core_swap(share)
     (out,) = call(
         functools.partial(last_body, points, rank),

time: 75.2 us -> 64.6 us (0.86)
  starting transfers between devices: 56.1 us -> 51.4 us
  local copies, waits for them, and re-layouts: 5.24 us -> 0.69 us
  waiting for transfers between devices: 5.61 us -> 2.99 us
  Pallas kernels: 7.4 us -> 8.83 us
    ppermute x7 -> x6, starting transfers between devices: 49.2 us -> 44.6 us  [route(): lax.ppermute(value, 'curve', [(source_of(i) % size, i) for i in range(siz...]
    unnamed x32 -> x12, local copies, waits for them, and re-layouts: 5.24 us -> 0.69 us
    ppermute x7 -> x6, waiting for transfers between devices: 5.6 us -> 2.98 us  [route(): lax.ppermute(value, 'curve', [(source_of(i) % size, i) for i in range(siz...]
    pallas_call x9, Pallas kernels: 7.4 us -> 8.83 us  [call(): pl.pallas_call(body, out_shape=[jax.ShapeDtypeStruct(s, t) for s, t in ou...]
  transfers between devices with their start and end apart: 9 -> 8, of which waited for: 3 -> 2; matrix products, arithmetic and copies ran while one was open for 0% -> 0% of each run, Pallas kernels for 3% -> 8%
where the time goes in v3:
time: 64.6 us; the launch traced here: 64.1 us
  starting transfers between devices  51.4 us (80%)
  Pallas kernels  8.83 us (14%)
  waiting for transfers between devices  2.99 us (5%)
  local copies, waits for them, and re-layouts  0.69 us (1%)
    ppermute x6, starting transfers between devices, route(): lax.ppermute(value, 'curve', [(source_of(i) % size, i) for i in range(siz...  44.6 us
    pallas_call x9, Pallas kernels, call(): pl.pallas_call(body, out_shape=[jax.ShapeDtypeStruct(s, t) for s, t in ou...  8.83 us
    all_to_all x1, starting transfers between devices, local_part(): lax.all_to_all(coupled, 'curve', 0, 0, axis_index_groups=chip_groups(size))  3.41 us
    all_to_all x1, starting transfers between devices, local_part(): lax.all_to_all(spread, 'curve', 0, 0, axis_index_groups=cluster_groups(si...  3.36 us
    ppermute x6, waiting for transfers between devices, route(): lax.ppermute(value, 'curve', [(source_of(i) % size, i) for i in range(siz...  2.98 us
  transfers between devices with their start and end apart: 8, of which 2 were waited for; matrix products, arithmetic and copies ran while one was open for 0% of the time, Pallas kernels for 8%

profile of v3, /device:TPU:1, one launch (start us, length us, event | category | flops | bytes accessed | tf_op | source)
XLA Modules:
  0.0 64.1 jit_solution(10148926630190703140)
XLA Ops:
  0.0 0.0 copy-start.2
  0.0 2.1 %shard_map.118.pack_ref = bf16[1408,256]{1,0:T(8,128)(2,1)S(1)} custom-call(bf16[1024,256]{1,0:T(8,128)(2,1)} %basis_ref.1, bf16[1024,128]{1,0:T(8,128)(2,1)} %x_hbm.3, bf16[512,256]{1,0:T(8,128)(2,1)} %e1_ref.1, bf16[1024,512]{1,0:T(8,128)(2,1)} %next_hbm.3, bf16[128,256]{1,0:T(8,128)(2,1)} %e2_hbm.1, bf16[3,128,256]{2,1,0:T(8,128)(2,1)} %bitcast.9), custom_call_target="tpu_custom_call" | custom-call | flops 167772160 | bytes 2359296 | tf_op jit(solution)/shard_map/pallas_call | solution.py:65
  2.1 0.0 copy-start.4
  2.1 8.7 %collective-permute-start = (bf16[1408,256]{1,0:T(8,128)(2,1)S(1)}, bf16[1408,256]{1,0:T(8,128)(2,1)S(1)}, u32[]{:S(2)}, u32[]{:S(2)}) collective-permute-start(bf16[1408,256]{1,0:T(8,128)(2,1)S(1)} %shard_map.118.pack_ref), channel_id=1, source_target_pairs={{1,0},{0,1},{3,2},{2,3},{5,4},{4,5},{7,6},{6,7},{9,8},{8,9},{11,10... | collective-permute-start | bytes 2162696 | tf_op jit(solution)/shard_map/ppermute | solution.py:18
  10.9 0.0 copy-done.2
  10.9 0.0 copy-done.4
  10.9 0.8 %shard_map.120 = bf16[8,2,32,256]{3,2,1,0:T(8,128)(2,1)} custom-call(s32[3,64]{1,0:T(4,128)S(1)} %bitcast.7, bf16[3,32,256]{2,1,0:T(8,128)(2,1)S(1)} %bitcast.5), custom_call_target="tpu_custom_call" | custom-call | flops 262144 | bytes 49920 | tf_op jit(solution)/shard_map/pallas_call | solution.py:65
  11.7 3.4 %all-to-all-start = ((bf16[8,2,32,256]{3,2,1,0:T(8,128)(2,1)}), bf16[8,2,32,256]{3,2,1,0:T(8,128)(2,1)S(1)}, u32[]{:S(2)}, u32[]{:S(2)}) async-start(bf16[8,2,32,256]{3,2,1,0:T(8,128)(2,1)} %shard_map.120), calls=%async_computation | async-start | bytes 524288 | tf_op jit(solution)/shard_map/all_to_all | solution.py:361
  15.1 0.0 collective-permute-done.got_ref
  15.1 0.2 shard_map.119
  15.3 3.5 %collective-permute-start.3 = (bf16[768,256]{1,0:T(8,128)(2,1)S(1)}, bf16[768,256]{1,0:T(8,128)(2,1)S(1)}, u32[]{:S(2)}, u32[]{:S(2)}) collective-permute-start(bf16[768,256]{1,0:T(8,128)(2,1)S(1)} %shard_map.122), channel_id=1, source_target_pairs={{511,0},{2,1},{1,2},{4,3},{3,4},{6,5},{5,6},{8,7},{7,8},{10,9},{9,... | collective-permute-start | bytes 1179656 | tf_op jit(solution)/shard_map/ppermute | solution.py:18
  18.8 12.5 %collective-permute-start.2 = (bf16[128,256]{1,0:T(8,128)(2,1)S(1)}, bf16[128,256]{1,0:T(8,128)(2,1)S(1)}, u32[]{:S(2)}, u32[]{:S(2)}) collective-permute-start(bf16[128,256]{1,0:T(8,128)(2,1)S(1)} %get-tuple-element.11), channel_id=1, source_target_pairs={{492,0},{29,1},{494,2},{31,3},{488,4},{25,5},{490,6},{27,7},{500,8... | collective-permute-start | bytes 196616 | tf_op jit(solution)/shard_map/ppermute | solution.py:18
  31.4 3.0 %collective-permute-start.1 = (bf16[128,256]{1,0:T(8,128)(2,1)S(1)}, bf16[128,256]{1,0:T(8,128)(2,1)S(1)}, u32[]{:S(2)}, u32[]{:S(2)}) collective-permute-start(bf16[128,256]{1,0:T(8,128)(2,1)S(1)} %get-tuple-element.11), channel_id=1, source_target_pairs={{496,0},{17,1},{498,2},{19,3},{500,4},{21,5},{502,6},{23,7},{504,8... | collective-permute-start | bytes 196616 | tf_op jit(solution)/shard_map/ppermute | solution.py:18
  34.3 0.0 all-to-all-done.weights_ref
  34.4 0.0 collective-permute-done.2.far_ref
  34.4 2.0 %collective-permute-done.1.near_ref = bf16[128,256]{1,0:T(8,128)(2,1)S(1)} collective-permute-done((bf16[128,256]{1,0:T(8,128)(2,1)S(1)}, bf16[128,256]{1,0:T(8,128)(2,1)S(1)}, u32[]{:S(2)}, u32[]{:S(2)}) %collective-permute-start.1) | collective-permute-done | bytes 65568 | tf_op jit(solution)/shard_map/ppermute | solution.py:18
  36.4 0.9 %shard_map.121 = bf16[4,128,256]{2,1,0:T(8,128)(2,1)} custom-call(bf16[128,256]{1,0:T(8,128)(2,1)S(1)} %collective-permute-done.1.near_ref, bf16[128,256]{1,0:T(8,128)(2,1)S(1)} %collective-permute-done.2.far_ref, bf16[8,2,32,256]{3,2,1,0:T(8,128)(2,1)S(1)} %all-to-all-done.weights_ref), custom_call_target="tpu_custom_call" | custom-call | flops 33554432 | bytes 393216 | tf_op jit(solution)/shard_map/pallas_call | solution.py:65
  37.3 3.4 %all-to-all-start.1 = ((bf16[4,128,256]{2,1,0:T(8,128)(2,1)}), bf16[4,128,256]{2,1,0:T(8,128)(2,1)S(1)}, u32[]{:S(2)}, u32[]{:S(2)}) async-start(bf16[4,128,256]{2,1,0:T(8,128)(2,1)} %shard_map.121), calls=%async_computation.1 | async-start | bytes 524288 | tf_op jit(solution)/shard_map/all_to_all | solution.py:392
  40.7 0.0 collective-permute-done.3.cross_ref
  40.7 0.0 copy-start.3
  40.7 7.9 %collective-permute-start.4 = (bf16[256,256]{1,0:T(8,128)(2,1)S(1)}, bf16[256,256]{1,0:T(8,128)(2,1)S(1)}, u32[]{:S(2)}, u32[]{:S(2)}) collective-permute-start(bf16[256,256]{1,0:T(8,128)(2,1)S(1)} %shard_map.123), channel_id=1, source_target_pairs={{508,0},{5,1},{510,2},{7,3},{0,4},{9,5},{2,6},{11,7},{4,8},{13,9},... | collective-permute-start | bytes 393224 | tf_op jit(solution)/shard_map/ppermute | solution.py:18
  48.7 0.0 copy-start.5
  48.7 0.0 copy-done.3
  48.7 0.7 %copy-done.5 = s32[2,3]{1,0:T(2,128)S(1)} copy-done((s32[2,3]{1,0:T(2,128)S(1)}, s32[2,3]{1,0:T(2,128)}, u32[]{:S(2)}) %copy-start.5) | copy-done | bytes 48
  49.3 3.0 %shard_map.124 = (f32[8,256]{1,0:T(8,128)S(1)}, f32[256,256]{1,0:T(8,128)S(1)}, bf16[256,256]{1,0:T(8,128)(2,1)S(1)}, f32[1024,128]{1,0:T(8,128)S(1)}) custom-call(s32[3,256]{1,0:T(4,128)S(1)} %bitcast.6, s32[2,3]{1,0:T(2,128)S(1)} %copy-done.5, bf16[1408,256]{1,0:T(8,128)(2,1)S(1)} %collective-permute-done.got_ref, ...), custom_call_target="tpu_custom_call" | custom-call | flops 524288000 | bytes 4262936 | tf_op jit(solution)/shard_map/pallas_call | solution.py:65
  52.4 0.0 all-to-all-done.1.gathered_ref
  52.4 0.0 collective-permute-done.4.near_ref
  52.4 0.0 copy-start
  52.4 0.0 copy-start.1
  52.4 0.3 shard_map.125.mine_ref
  52.7 8.9 %collective-permute-start.5 = (bf16[256,256]{1,0:T(8,128)(2,1)S(1)}, bf16[256,256]{1,0:T(8,128)(2,1)S(1)}, u32[]{:S(2)}, u32[]{:S(2)}) collective-permute-start(bf16[256,256]{1,0:T(8,128)(2,1)S(1)} %shard_map.125.mine_ref), channel_id=1, source_target_pairs={{1,0},{0,1},{3,2},{2,3},{5,4},{4,5},{7,6},{6,7},{9,8},{8,9},{11,10... | collective-permute-start | bytes 393224 | tf_op jit(solution)/shard_map/ppermute | solution.py:18
  61.7 1.0 %collective-permute-done.5.got_ref = bf16[256,256]{1,0:T(8,128)(2,1)S(1)} collective-permute-done((bf16[256,256]{1,0:T(8,128)(2,1)S(1)}, bf16[256,256]{1,0:T(8,128)(2,1)S(1)}, u32[]{:S(2)}, u32[]{:S(2)}) %collective-permute-start.5) | collective-permute-done | bytes 131104 | tf_op jit(solution)/shard_map/ppermute | solution.py:18
  62.6 0.0 copy-done
  62.6 0.0 copy-done.1
  62.6 1.5 %shard_map.126 = bf16[1024,128]{1,0:T(8,128)(2,1)} custom-call(bf16[256,256]{1,0:T(8,128)(2,1)S(1)} %shard_map.125.mine_ref, bf16[256,256]{1,0:T(8,128)(2,1)S(1)} %collective-permute-done.5.got_ref, f32[256,256]{1,0:T(8,128)S(1)} %get-tuple-element.14.zero_ref, bf16[256,256]{1,0:T(8,128)(2,1)S(1)} %get-tuple-element.15.weight_ref, ...), custom_call_target="tpu_custom_call" | custom-call | flops 125829120 | bytes 1966080 | tf_op jit(solution)/shard_map/pallas_call | solution.py:65
  (2 shorter events, 0.0 us)
Async XLA Ops:
  0.0 10.9 %copy-start.2 = (bf16[32,3,256]{2,0,1:T(8,128)(2,1)S(1)}, bf16[32,3,256]{2,0,1:T(8,128)(2,1)}, u32[]{:S(2)}) copy-start(bf16[32,3,256]{2,0,1:T(8,128)(2,1)} %param.20) | copy-start | bytes 147460
  2.1 8.8 %copy-start.4 = (s32[64,3]{0,1:T(4,128)S(1)}, s32[64,3]{0,1:T(4,128)}, u32[]{:S(2)}) copy-start(s32[64,3]{0,1:T(4,128)} %param.23) | copy-start | bytes 2308
  2.1 13.0 %collective-permute-start = (bf16[1408,256]{1,0:T(8,128)(2,1)S(1)}, bf16[1408,256]{1,0:T(8,128)(2,1)S(1)}, u32[]{:S(2)}, u32[]{:S(2)}) collective-permute-start(bf16[1408,256]{1,0:T(8,128)(2,1)S(1)} %shard_map.118.pack_ref), channel_id=1, source_target_pairs={{1,0},{0,1},{3,2},{2,3},{5,4},{4,5},{7,6},{6,7},{9,8},{8,9},{11,10... | collective-permute-start | bytes 2162696 | tf_op jit(solution)/shard_map/ppermute | solution.py:18
  11.7 22.6 %all-to-all-start = ((bf16[8,2,32,256]{3,2,1,0:T(8,128)(2,1)}), bf16[8,2,32,256]{3,2,1,0:T(8,128)(2,1)S(1)}, u32[]{:S(2)}, u32[]{:S(2)}) async-start(bf16[8,2,32,256]{3,2,1,0:T(8,128)(2,1)} %shard_map.120), calls=%async_computation | async-start | bytes 524288 | tf_op jit(solution)/shard_map/all_to_all | solution.py:361
  15.3 25.4 %collective-permute-start.3 = (bf16[768,256]{1,0:T(8,128)(2,1)S(1)}, bf16[768,256]{1,0:T(8,128)(2,1)S(1)}, u32[]{:S(2)}, u32[]{:S(2)}) collective-permute-start(bf16[768,256]{1,0:T(8,128)(2,1)S(1)} %shard_map.122), channel_id=1, source_target_pairs={{511,0},{2,1},{1,2},{4,3},{3,4},{6,5},{5,6},{8,7},{7,8},{10,9},{9,... | collective-permute-start | bytes 1179656 | tf_op jit(solution)/shard_map/ppermute | solution.py:18
  18.8 15.5 %collective-permute-start.2 = (bf16[128,256]{1,0:T(8,128)(2,1)S(1)}, bf16[128,256]{1,0:T(8,128)(2,1)S(1)}, u32[]{:S(2)}, u32[]{:S(2)}) collective-permute-start(bf16[128,256]{1,0:T(8,128)(2,1)S(1)} %get-tuple-element.11), channel_id=1, source_target_pairs={{492,0},{29,1},{494,2},{31,3},{488,4},{25,5},{490,6},{27,7},{500,8... | collective-permute-start | bytes 196616 | tf_op jit(solution)/shard_map/ppermute | solution.py:18
  31.4 5.0 %collective-permute-start.1 = (bf16[128,256]{1,0:T(8,128)(2,1)S(1)}, bf16[128,256]{1,0:T(8,128)(2,1)S(1)}, u32[]{:S(2)}, u32[]{:S(2)}) collective-permute-start(bf16[128,256]{1,0:T(8,128)(2,1)S(1)} %get-tuple-element.11), channel_id=1, source_target_pairs={{496,0},{17,1},{498,2},{19,3},{500,4},{21,5},{502,6},{23,7},{504,8... | collective-permute-start | bytes 196616 | tf_op jit(solution)/shard_map/ppermute | solution.py:18
  37.3 15.1 %all-to-all-start.1 = ((bf16[4,128,256]{2,1,0:T(8,128)(2,1)}), bf16[4,128,256]{2,1,0:T(8,128)(2,1)S(1)}, u32[]{:S(2)}, u32[]{:S(2)}) async-start(bf16[4,128,256]{2,1,0:T(8,128)(2,1)} %shard_map.121), calls=%async_computation.1 | async-start | bytes 524288 | tf_op jit(solution)/shard_map/all_to_all | solution.py:392
  40.7 8.0 %copy-start.3 = (s32[256,3]{0,1:T(4,128)S(1)}, s32[256,3]{0,1:T(4,128)}, u32[]{:S(2)}) copy-start(s32[256,3]{0,1:T(4,128)} %param.22) | copy-start | bytes 9220
  40.7 11.6 %collective-permute-start.4 = (bf16[256,256]{1,0:T(8,128)(2,1)S(1)}, bf16[256,256]{1,0:T(8,128)(2,1)S(1)}, u32[]{:S(2)}, u32[]{:S(2)}) collective-permute-start(bf16[256,256]{1,0:T(8,128)(2,1)S(1)} %shard_map.123), channel_id=1, source_target_pairs={{508,0},{5,1},{510,2},{7,3},{0,4},{9,5},{2,6},{11,7},{4,8},{13,9},... | collective-permute-start | bytes 393224 | tf_op jit(solution)/shard_map/ppermute | solution.py:18
  48.7 0.7 %copy-start.5 = (s32[2,3]{1,0:T(2,128)S(1)}, s32[2,3]{1,0:T(2,128)}, u32[]{:S(2)}) copy-start(s32[2,3]{1,0:T(2,128)} %leaf_ref.1) | copy-start | bytes 76
  52.4 10.3 %copy-start = (bf16[1024,256]{1,0:T(8,128)(2,1)S(1)}, bf16[1024,256]{1,0:T(8,128)(2,1)}, u32[]{:S(2)}) copy-start(bf16[1024,256]{1,0:T(8,128)(2,1)} %basis_ref.1) | copy-start | bytes 1572868
  52.4 10.3 %copy-start.1 = (bf16[512,256]{1,0:T(8,128)(2,1)S(1)}, bf16[512,256]{1,0:T(8,128)(2,1)}, u32[]{:S(2)}) copy-start(bf16[512,256]{1,0:T(8,128)(2,1)} %e1_ref.1) | copy-start | bytes 786436
  52.7 9.9 %collective-permute-start.5 = (bf16[256,256]{1,0:T(8,128)(2,1)S(1)}, bf16[256,256]{1,0:T(8,128)(2,1)S(1)}, u32[]{:S(2)}, u32[]{:S(2)}) collective-permute-start(bf16[256,256]{1,0:T(8,128)(2,1)S(1)} %shard_map.125.mine_ref), channel_id=1, source_target_pairs={{1,0},{0,1},{3,2},{2,3},{5,4},{4,5},{7,6},{6,7},{9,8},{8,9},{11,10... | collective-permute-start | bytes 393224 | tf_op jit(solution)/shard_map/ppermute | solution.py:18

commit v4 on v3

--- a/solution.py
+++ b/solution.py
@@ -54,7 +54,7 @@
     return lax.dot_general(a, b, (((1,), (1,)), ((), ())), preferred_element_type=F32)
 
 
-def call(body, outs, flops, *args, far=(), scratch=(), grant=8):
+def call(body, outs, flops, *args, far=(), far_out=(), scratch=(), grant=8):
     spec = pl.BlockSpec(memory_space=pltpu.VMEM)
     moved = sum(a.size * a.dtype.itemsize for a in args)
     args = [
@@ -66,7 +66,7 @@
         body,
         out_shape=[jax.ShapeDtypeStruct(s, t) for s, t in outs],
         in_specs=[hbm if n in far else spec for n in range(len(args))],
-        out_specs=[spec] * len(outs),
+        out_specs=[hbm if n in far_out else spec for n in range(len(outs))],
         scratch_shapes=list(scratch),
         compiler_params=pltpu.CompilerParams(vmem_limit_bytes=grant << 20),
         cost_estimate=pl.CostEstimate(flops=flops, bytes_accessed=moved, transcendentals=0),
@@ -83,26 +83,10 @@
     return jnp.where(entry == wanted, 1.0, 0.0).astype(F32)
 
 
-def spread_body(table_ref, coupling_ref, out_ref):
-    device = lax.axis_index("curve")
-    clusters = table_ref.shape[1]
-    own = device // 8
-    row = picked_row(table_ref[...], own)
-    for core, offsets in enumerate(((-2, -3), (2, 3))):
-        for n, offset in enumerate(offsets):
-            total = None
-            for s in range(3):
-                mask = offset_mask(row[s : s + 1], own, offset, clusters)
-                term = coupling_ref[s].astype(F32) * mask
-                total = term if total is None else total + term
-            value = total.astype(BF16)
-            for chip in range(4):
-                out_ref[2 * chip + core, n] = value
-
-
 def first_body(
-    points, rank, basis_hbm, x_hbm, e1_hbm, next_hbm, e2_hbm, c1_hbm, pack_ref,
-    basis_ref, x_ref, e1_ref, next_ref, sems,
+    points, rank, table_hbm, c2_hbm, basis_hbm, x_hbm, e1_hbm, next_hbm, e2_hbm, c1_hbm,
+    pack_ref, spread_hbm,
+    basis_ref, x_ref, e1_ref, next_ref, table_ref, c2_ref, spread_ref, sems, out_sems,
 ):
     copies = []
     for i in range(2):
@@ -114,8 +98,30 @@
     copies.append((e2_hbm, pack_ref.at[pl.ds(896, 128)]))
     for s in range(3):
         copies.append((c1_hbm.at[s], pack_ref.at[pl.ds(1024 + 128 * s, 128)]))
+    copies.append((table_hbm, table_ref))
+    copies.append((c2_hbm, c2_ref))
     moves = [pltpu.make_async_copy(a, b, sems.at[n]) for n, (a, b) in enumerate(copies)]
-    for move in moves:
+    for move in moves[-2:] + moves[:-2]:
+        move.start()
+    device = lax.axis_index("curve")
+    clusters = table_ref.shape[1]
+    own = device // 8
+    for move in moves[-2:]:
+        move.wait()
+    row = picked_row(table_ref[...], own)
+    for core, offsets in enumerate(((-2, -3), (2, 3))):
+        for n, offset in enumerate(offsets):
+            total = None
+            for s in range(3):
+                mask = offset_mask(row[s : s + 1], own, offset, clusters)
+                term = c2_ref[s].astype(F32) * mask
+                total = term if total is None else total + term
+            spread_ref[core, n] = total.astype(BF16)
+    sent = [
+        pltpu.make_async_copy(spread_ref.at[m % 2], spread_hbm.at[m], out_sems.at[m])
+        for m in range(8)
+    ]
+    for move in sent:
         move.start()
     coefs = []
     for i in range(2):
@@ -135,11 +141,13 @@
         for v in range(2):
             rows = x_ref[256 * v + 128 * h : 256 * v + 128 * (h + 1)]
             pack_ref[640 + 128 * h : 768 + 128 * h, 128 * v : 128 * (v + 1)] = rows
-    for move in moves[6:]:
+    for move in moves[6:-2]:
         move.wait()
-
-
-def second_body(pack_ref, got_ref, one_ref, two_ref):
+    for move in sent:
+        move.wait()
+
+
+def second_body(pack_ref, got_ref, one_ref, two_ref, out_ref):
     first = (lax.axis_index("curve") & 1) == 0
     one = (pack_ref[256:384].astype(F32) + got_ref[256:384].astype(F32)).astype(BF16)
     one_ref[...] = one
@@ -148,28 +156,26 @@
     top = jnp.where(first, mine, other)
     bottom = jnp.where(first, other, mine)
     two_ref[...] = (nn(one[:, 0:128], top) + nn(one[:, 128:256], bottom)).astype(BF16)
-
-
-def cross_body(pack_ref, got_ref, one_ref, out_ref):
-    first = (lax.axis_index("curve") & 1) == 0
     out_ref[0:128] = jnp.where(first, pack_ref[0:128], got_ref[128:256])
     out_ref[128:256] = jnp.where(first, pack_ref[128:256], pack_ref[0:128])
     out_ref[256:384] = jnp.where(first, got_ref[0:128], pack_ref[128:256])
     out_ref[384:640] = jnp.where(first, pack_ref[640:896], pack_ref[384:640])
-    out_ref[640:768] = one_ref[...]
 
 
 def bundle_body(one_ref, cross_ref, out_ref):
     out_ref[0:128] = one_ref[...]
-    out_ref[128:256] = cross_ref[640:768]
-
-
-def couple_two_body(near_ref, far_ref, weights_ref, out_ref):
+    out_ref[128:256] = cross_ref[...]
+
+
+def couple_two_body(near_ref, far_ref, weights_ref, out_hbm, value_ref, sems):
     first = weights_ref[:, 0].reshape(256, 256)
     second = weights_ref[:, 1].reshape(256, 256)
-    value = (nn(near_ref[...], first) + nn(far_ref[...], second)).astype(BF16)
-    for i in range(4):
-        out_ref[i] = value
+    value_ref[...] = (nn(near_ref[...], first) + nn(far_ref[...], second)).astype(BF16)
+    moves = [pltpu.make_async_copy(value_ref, out_hbm.at[i], sems.at[i]) for i in range(4)]
+    for move in moves:
+        move.start()
+    for move in moves:
+        move.wait()
 
 
 def gather_body(
@@ -320,10 +326,14 @@
     out_ref[128:256] = jnp.where(first, cross_ref[256:384], cross_ref[0:128])
 
 
-def last_body(points, rank, mine_ref, got_ref, zero_ref, weight_ref, e1_ref, basis_ref, field_ref, out_ref):
+def last_body(
+    points, rank, mine_ref, got_ref, zero_ref, weight_ref, e1_ref, basis_ref, field_ref, out_hbm,
+    out_ref, sems,
+):
     core = lax.axis_index("curve") & 1
     one = (mine_ref[0:128].astype(F32) + got_ref[0:128].astype(F32)).astype(BF16)
     extra = nn(got_ref[128:256], weight_ref[...])
+    moves = []
     for i in range(2):
         used = jnp.where(core == (1 - i), 1.0, 0.0)
         zero = zero_ref[128 * i : 128 * (i + 1)] + extra * used
@@ -332,6 +342,12 @@
         out_ref[i * points : (i + 1) * points] = (
             field_ref[i * points : (i + 1) * points] + field
         ).astype(BF16)
+        rows = pl.ds(i * points, points)
+        move = pltpu.make_async_copy(out_ref.at[rows], out_hbm.at[rows], sems.at[i])
+        move.start()
+        moves.append(move)
+    for move in moves:
+        move.wait()
 
 
 def local_part(
@@ -357,40 +373,59 @@
     table_one = list_one.T
     table_two = list_two.T
 
-    (spread,) = call(spread_body, [((8, 2, 32, 256), BF16)], 1 << 18, table_two, c2)
-    weights_two = lax.all_to_all(
-        spread, "curve", 0, 0, axis_index_groups=cluster_groups(size)
-    )
-    (pack,) = call(
+    pack, spread = call(
         functools.partial(first_body, points, rank),
-        [((1408, 256), BF16)],
+        [((1408, 256), BF16), ((8, 2, 32, 256), BF16)],
         160 << 20,
+        table_two,
+        c2,
         leaf_basis,
         vectors,
         transfer_one,
         near_next,
         transfer_two,
         c1,
-        far=range(6),
+        far=range(8),
+        far_out=(1,),
         scratch=[
             pltpu.VMEM((2 * points, rank), BF16),
             pltpu.VMEM((2 * points, 128), BF16),
             pltpu.VMEM((2 * rank, rank), BF16),
             pltpu.VMEM((points, points), BF16),
-            pltpu.SemaphoreType.DMA((10,)),
+            pltpu.VMEM(table_two.shape, I32),
+            pltpu.VMEM(c2.shape, BF16),
+            pltpu.VMEM((2, 2, 32, 256), BF16),
+            pltpu.SemaphoreType.DMA((12,)),
+            pltpu.SemaphoreType.DMA((8,)),
         ],
     )
     got = core_swap(pack)
-    one, two = call(second_body, [((128, 256), BF16), ((128, 256), BF16)], 16 << 20, pack, got)
+    weights_two = lax.all_to_all(
+        spread, "curve", 0, 0, axis_index_groups=cluster_groups(size)
+    )
+    one, two, leaves = call(
+        second_body,
+        [((128, 256), BF16), ((128, 256), BF16), ((640, 256), BF16)],
+        16 << 20,
+        pack,
+        got,
+    )
     two_far = third_cluster(two)
     two_near = far_route(two, 8)
-    (leaves,) = call(cross_body, [((768, 256), BF16)], 1 << 18, pack, got, one)
+    one_crossed = chip_swap(one)
     crossed = chip_swap(leaves)
     (coupled,) = call(
-        couple_two_body, [((4, 128, 256), BF16)], 32 << 20, two_near, two_far, weights_two
+        couple_two_body,
+        [((4, 128, 256), BF16)],
+        32 << 20,
+        two_near,
+        two_far,
+        weights_two,
+        far_out=(0,),
+        scratch=[pltpu.VMEM((128, 256), BF16), pltpu.SemaphoreType.DMA((4,))],
     )
     gathered = lax.all_to_all(coupled, "curve", 0, 0, axis_index_groups=chip_groups(size))
-    (bundle,) = call(bundle_body, [((256, 256), BF16)], 1 << 18, one, crossed)
+    (bundle,) = call(bundle_body, [((256, 256), BF16)], 1 << 18, one, one_crossed)
     one_near = far_route(bundle, 2)
     mask, far_zero, weight, field = call(
         functools.partial(gather_body, points, rank),
@@ -433,6 +468,8 @@
         transfer_one,
         leaf_basis,
         field,
+        far_out=(0,),
+        scratch=[pltpu.VMEM((2 * points, 128), BF16), pltpu.SemaphoreType.DMA((2,))],
     )
     return out
 

time: 64.6 us -> 74 us (1.15)
  waiting for transfers between devices: 2.99 us -> 8.93 us
  starting transfers between devices: 51.4 us -> 55.6 us
    ppermute x6 -> x7, waiting for transfers between devices: 2.98 us -> 8.92 us  [route(): lax.ppermute(value, 'curve', [(source_of(i) % size, i) for i in range(siz...]
    ppermute x6 -> x7, starting transfers between devices: 44.6 us -> 48.8 us  [route(): lax.ppermute(value, 'curve', [(source_of(i) % size, i) for i in range(siz...]
    pallas_call x9 -> x7, Pallas kernels: 8.83 us -> 8.1 us  [call(): pl.pallas_call(body, out_shape=[jax.ShapeDtypeStruct(s, t) for s, t in ou...]
  transfers between devices with their start and end apart: 8 -> 9, of which waited for: 2 -> 3; matrix products, arithmetic and copies ran while one was open for 0% -> 0% of each run, Pallas kernels for 8% -> 4%
where the time goes in v4:
time: 74 us; the launch traced here: 73.5 us
  starting transfers between devices  55.6 us (75%)
  waiting for transfers between devices  8.93 us (12%)
  Pallas kernels  8.1 us (11%)
    ppermute x7, starting transfers between devices, route(): lax.ppermute(value, 'curve', [(source_of(i) % size, i) for i in range(siz...  48.8 us
    ppermute x7, waiting for transfers between devices, route(): lax.ppermute(value, 'curve', [(source_of(i) % size, i) for i in range(siz...  8.92 us
    pallas_call x7, Pallas kernels, call(): pl.pallas_call(body, out_shape=[jax.ShapeDtypeStruct(s, t) for s, t in ou...  8.1 us
    all_to_all x1, starting transfers between devices, local_part(): lax.all_to_all(coupled, 'curve', 0, 0, axis_index_groups=chip_groups(size))  3.42 us
    all_to_all x1, starting transfers between devices, local_part(): lax.all_to_all(spread, 'curve', 0, 0, axis_index_groups=cluster_groups(si...  3.38 us
  transfers between devices with their start and end apart: 9, of which 3 were waited for; matrix products, arithmetic and copies ran while one was open for 0% of the time, Pallas kernels for 4%

profile of v4, /device:TPU:1, one launch (start us, length us, event | category | flops | bytes accessed | tf_op | source)
XLA Modules:
  0.0 73.5 jit_solution(15569144561567460277)
XLA Ops:
  0.0 2.2 %shard_map.118 = (bf16[1408,256]{1,0:T(8,128)(2,1)S(1)}, bf16[8,2,32,256]{3,2,1,0:T(8,128)(2,1)}) custom-call(s32[3,64]{1,0:T(4,128)} %bitcast.9, bf16[3,32,256]{2,1,0:T(8,128)(2,1)} %bitcast.8, bf16[1024,256]{1,0:T(8,128)(2,1)} %basis_ref.1, bf16[1024,128]{1,0:T(8,128)(2,1)} %x_hbm.3, bf16[512,256]{1,0:T(8,128)(2,1)} %e1_ref.1, bf16[1024,512]{1,0:T(8,128)(2,1)} %next_hbm.3, ...), custom_call_target="tpu_custom_call" | custom-call | flops 167772160 | bytes 2409216 | tf_op jit(solution)/shard_map/pallas_call | solution.py:65
  2.2 8.7 %collective-permute-start = (bf16[1408,256]{1,0:T(8,128)(2,1)S(1)}, bf16[1408,256]{1,0:T(8,128)(2,1)S(1)}, u32[]{:S(2)}, u32[]{:S(2)}) collective-permute-start(bf16[1408,256]{1,0:T(8,128)(2,1)S(1)} %get-tuple-element.14.pack_ref), channel_id=1, source_target_pairs={{1,0},{0,1},{3,2},{2,3},{5,4},{4,5},{7,6},{6,7},{9,8},{8,9},{11,10... | collective-permute-start | bytes 2162696 | tf_op jit(solution)/shard_map/ppermute | solution.py:18
  11.0 3.4 %all-to-all-start = ((bf16[8,2,32,256]{3,2,1,0:T(8,128)(2,1)}), bf16[8,2,32,256]{3,2,1,0:T(8,128)(2,1)S(1)}, u32[]{:S(2)}, u32[]{:S(2)}) async-start(bf16[8,2,32,256]{3,2,1,0:T(8,128)(2,1)} %get-tuple-element.16), calls=%async_computation | async-start | bytes 524288 | tf_op jit(solution)/shard_map/all_to_all | solution.py:403
  14.4 0.0 collective-permute-done.got_ref
  14.4 0.2 shard_map.119
  14.6 12.6 %collective-permute-start.2 = (bf16[128,256]{1,0:T(8,128)(2,1)S(1)}, bf16[128,256]{1,0:T(8,128)(2,1)S(1)}, u32[]{:S(2)}, u32[]{:S(2)}) collective-permute-start(bf16[128,256]{1,0:T(8,128)(2,1)S(1)} %get-tuple-element.15), channel_id=1, source_target_pairs={{492,0},{29,1},{494,2},{31,3},{488,4},{25,5},{490,6},{27,7},{500,8... | collective-permute-start | bytes 196616 | tf_op jit(solution)/shard_map/ppermute | solution.py:18
  27.2 3.0 %collective-permute-start.1 = (bf16[128,256]{1,0:T(8,128)(2,1)S(1)}, bf16[128,256]{1,0:T(8,128)(2,1)S(1)}, u32[]{:S(2)}, u32[]{:S(2)}) collective-permute-start(bf16[128,256]{1,0:T(8,128)(2,1)S(1)} %get-tuple-element.15), channel_id=1, source_target_pairs={{496,0},{17,1},{498,2},{19,3},{500,4},{21,5},{502,6},{23,7},{504,8... | collective-permute-start | bytes 196616 | tf_op jit(solution)/shard_map/ppermute | solution.py:18
  30.2 0.0 all-to-all-done.weights_ref
  30.2 0.0 collective-permute-done.2.far_ref
  30.2 2.0 %collective-permute-done.1.near_ref = bf16[128,256]{1,0:T(8,128)(2,1)S(1)} collective-permute-done((bf16[128,256]{1,0:T(8,128)(2,1)S(1)}, bf16[128,256]{1,0:T(8,128)(2,1)S(1)}, u32[]{:S(2)}, u32[]{:S(2)}) %collective-permute-start.1) | collective-permute-done | bytes 65568 | tf_op jit(solution)/shard_map/ppermute | solution.py:18
  32.2 0.9 %shard_map.120 = bf16[4,128,256]{2,1,0:T(8,128)(2,1)} custom-call(bf16[128,256]{1,0:T(8,128)(2,1)S(1)} %collective-permute-done.1.near_ref, bf16[128,256]{1,0:T(8,128)(2,1)S(1)} %collective-permute-done.2.far_ref, bf16[8,2,32,256]{3,2,1,0:T(8,128)(2,1)S(1)} %all-to-all-done.weights_ref), custom_call_target="tpu_custom_call" | custom-call | flops 33554432 | bytes 393216 | tf_op jit(solution)/shard_map/pallas_call | solution.py:65
  33.2 3.4 %all-to-all-start.1 = ((bf16[4,128,256]{2,1,0:T(8,128)(2,1)}), bf16[4,128,256]{2,1,0:T(8,128)(2,1)S(1)}, u32[]{:S(2)}, u32[]{:S(2)}) async-start(bf16[4,128,256]{2,1,0:T(8,128)(2,1)} %shard_map.120), calls=%async_computation.1 | async-start | bytes 524288 | tf_op jit(solution)/shard_map/all_to_all | solution.py:427
  36.6 3.8 %collective-permute-start.5 = (bf16[640,256]{1,0:T(8,128)(2,1)S(1)}, bf16[640,256]{1,0:T(8,128)(2,1)S(1)}, u32[]{:S(2)}, u32[]{:S(2)}) collective-permute-start(bf16[640,256]{1,0:T(8,128)(2,1)S(1)} %get-tuple-element.18), channel_id=1, source_target_pairs={{511,0},{2,1},{1,2},{4,3},{3,4},{6,5},{5,6},{8,7},{7,8},{10,9},{9,... | collective-permute-start | bytes 983048 | tf_op jit(solution)/shard_map/ppermute | solution.py:18
  40.4 1.9 %collective-permute-start.3 = (bf16[128,256]{1,0:T(8,128)(2,1)S(1)}, bf16[128,256]{1,0:T(8,128)(2,1)S(1)}, u32[]{:S(2)}, u32[]{:S(2)}) collective-permute-start(bf16[128,256]{1,0:T(8,128)(2,1)S(1)} %get-tuple-element.17.one_ref), channel_id=1, source_target_pairs={{511,0},{2,1},{1,2},{4,3},{3,4},{6,5},{5,6},{8,7},{7,8},{10,9},{9,... | collective-permute-start | bytes 196616 | tf_op jit(solution)/shard_map/ppermute | solution.py:18
  42.3 5.9 %collective-permute-done.3.cross_ref = bf16[128,256]{1,0:T(8,128)(2,1)S(1)} collective-permute-done((bf16[128,256]{1,0:T(8,128)(2,1)S(1)}, bf16[128,256]{1,0:T(8,128)(2,1)S(1)}, u32[]{:S(2)}, u32[]{:S(2)}) %collective-permute-start.3) | collective-permute-done | bytes 65568 | tf_op jit(solution)/shard_map/ppermute | solution.py:18
  48.2 0.0 copy-start.2
  48.2 5.4 %collective-permute-start.4 = (bf16[256,256]{1,0:T(8,128)(2,1)S(1)}, bf16[256,256]{1,0:T(8,128)(2,1)S(1)}, u32[]{:S(2)}, u32[]{:S(2)}) collective-permute-start(bf16[256,256]{1,0:T(8,128)(2,1)S(1)} %shard_map.121), channel_id=1, source_target_pairs={{508,0},{5,1},{510,2},{7,3},{0,4},{9,5},{2,6},{11,7},{4,8},{13,9},... | collective-permute-start | bytes 393224 | tf_op jit(solution)/shard_map/ppermute | solution.py:18
  53.7 0.0 collective-permute-done.5.cross_ref
  53.7 0.0 copy-start.3
  53.7 0.0 copy-done.2
  53.7 0.7 copy-done.3
  54.3 3.0 %shard_map.122 = (f32[8,256]{1,0:T(8,128)S(1)}, f32[256,256]{1,0:T(8,128)S(1)}, bf16[256,256]{1,0:T(8,128)(2,1)S(1)}, f32[1024,128]{1,0:T(8,128)S(1)}) custom-call(s32[3,256]{1,0:T(4,128)S(1)} %bitcast.5, s32[2,3]{1,0:T(2,128)S(1)} %copy-done.3, bf16[1408,256]{1,0:T(8,128)(2,1)S(1)} %collective-permute-done.got_ref, ...), custom_call_target="tpu_custom_call" | custom-call | flops 524288000 | bytes 4197400 | tf_op jit(solution)/shard_map/pallas_call | solution.py:65
  57.4 0.0 collective-permute-done.4.near_ref
  57.4 0.0 all-to-all-done.1.gathered_ref
  57.4 0.0 copy-start
  57.4 0.0 copy-start.1
  57.4 0.3 shard_map.123.mine_ref
  57.7 13.4 %collective-permute-start.6 = (bf16[256,256]{1,0:T(8,128)(2,1)S(1)}, bf16[256,256]{1,0:T(8,128)(2,1)S(1)}, u32[]{:S(2)}, u32[]{:S(2)}) collective-permute-start(bf16[256,256]{1,0:T(8,128)(2,1)S(1)} %shard_map.123.mine_ref), channel_id=1, source_target_pairs={{1,0},{0,1},{3,2},{2,3},{5,4},{4,5},{7,6},{6,7},{9,8},{8,9},{11,10... | collective-permute-start | bytes 393224 | tf_op jit(solution)/shard_map/ppermute | solution.py:18
  71.1 1.0 %collective-permute-done.6.got_ref = bf16[256,256]{1,0:T(8,128)(2,1)S(1)} collective-permute-done((bf16[256,256]{1,0:T(8,128)(2,1)S(1)}, bf16[256,256]{1,0:T(8,128)(2,1)S(1)}, u32[]{:S(2)}, u32[]{:S(2)}) %collective-permute-start.6) | collective-permute-done | bytes 131104 | tf_op jit(solution)/shard_map/ppermute | solution.py:18
  72.1 0.0 copy-done
  72.1 0.0 copy-done.1
  72.1 1.4 %shard_map.124 = bf16[1024,128]{1,0:T(8,128)(2,1)} custom-call(bf16[256,256]{1,0:T(8,128)(2,1)S(1)} %shard_map.123.mine_ref, bf16[256,256]{1,0:T(8,128)(2,1)S(1)} %collective-permute-done.6.got_ref, f32[256,256]{1,0:T(8,128)S(1)} %get-tuple-element.20.zero_ref, bf16[256,256]{1,0:T(8,128)(2,1)S(1)} %get-tuple-element.21.weight_ref, ...), custom_call_target="tpu_custom_call" | custom-call | flops 125829120 | bytes 1966080 | tf_op jit(solution)/shard_map/pallas_call | solution.py:65
  (1 shorter events, 0.0 us)
Async XLA Ops:
  2.2 12.1 %collective-permute-start = (bf16[1408,256]{1,0:T(8,128)(2,1)S(1)}, bf16[1408,256]{1,0:T(8,128)(2,1)S(1)}, u32[]{:S(2)}, u32[]{:S(2)}) collective-permute-start(bf16[1408,256]{1,0:T(8,128)(2,1)S(1)} %get-tuple-element.14.pack_ref), channel_id=1, source_target_pairs={{1,0},{0,1},{3,2},{2,3},{5,4},{4,5},{7,6},{6,7},{9,8},{8,9},{11,10... | collective-permute-start | bytes 2162696 | tf_op jit(solution)/shard_map/ppermute | solution.py:18
  11.0 19.2 %all-to-all-start = ((bf16[8,2,32,256]{3,2,1,0:T(8,128)(2,1)}), bf16[8,2,32,256]{3,2,1,0:T(8,128)(2,1)S(1)}, u32[]{:S(2)}, u32[]{:S(2)}) async-start(bf16[8,2,32,256]{3,2,1,0:T(8,128)(2,1)} %get-tuple-element.16), calls=%async_computation | async-start | bytes 524288 | tf_op jit(solution)/shard_map/all_to_all | solution.py:403
  14.6 15.6 %collective-permute-start.2 = (bf16[128,256]{1,0:T(8,128)(2,1)S(1)}, bf16[128,256]{1,0:T(8,128)(2,1)S(1)}, u32[]{:S(2)}, u32[]{:S(2)}) collective-permute-start(bf16[128,256]{1,0:T(8,128)(2,1)S(1)} %get-tuple-element.15), channel_id=1, source_target_pairs={{492,0},{29,1},{494,2},{31,3},{488,4},{25,5},{490,6},{27,7},{500,8... | collective-permute-start | bytes 196616 | tf_op jit(solution)/shard_map/ppermute | solution.py:18
  27.2 5.0 %collective-permute-start.1 = (bf16[128,256]{1,0:T(8,128)(2,1)S(1)}, bf16[128,256]{1,0:T(8,128)(2,1)S(1)}, u32[]{:S(2)}, u32[]{:S(2)}) collective-permute-start(bf16[128,256]{1,0:T(8,128)(2,1)S(1)} %get-tuple-element.15), channel_id=1, source_target_pairs={{496,0},{17,1},{498,2},{19,3},{500,4},{21,5},{502,6},{23,7},{504,8... | collective-permute-start | bytes 196616 | tf_op jit(solution)/shard_map/ppermute | solution.py:18
  33.2 24.2 %all-to-all-start.1 = ((bf16[4,128,256]{2,1,0:T(8,128)(2,1)}), bf16[4,128,256]{2,1,0:T(8,128)(2,1)S(1)}, u32[]{:S(2)}, u32[]{:S(2)}) async-start(bf16[4,128,256]{2,1,0:T(8,128)(2,1)} %shard_map.120), calls=%async_computation.1 | async-start | bytes 524288 | tf_op jit(solution)/shard_map/all_to_all | solution.py:427
  36.6 17.1 %collective-permute-start.5 = (bf16[640,256]{1,0:T(8,128)(2,1)S(1)}, bf16[640,256]{1,0:T(8,128)(2,1)S(1)}, u32[]{:S(2)}, u32[]{:S(2)}) collective-permute-start(bf16[640,256]{1,0:T(8,128)(2,1)S(1)} %get-tuple-element.18), channel_id=1, source_target_pairs={{511,0},{2,1},{1,2},{4,3},{3,4},{6,5},{5,6},{8,7},{7,8},{10,9},{9,... | collective-permute-start | bytes 983048 | tf_op jit(solution)/shard_map/ppermute | solution.py:18
  40.4 7.9 %collective-permute-start.3 = (bf16[128,256]{1,0:T(8,128)(2,1)S(1)}, bf16[128,256]{1,0:T(8,128)(2,1)S(1)}, u32[]{:S(2)}, u32[]{:S(2)}) collective-permute-start(bf16[128,256]{1,0:T(8,128)(2,1)S(1)} %get-tuple-element.17.one_ref), channel_id=1, source_target_pairs={{511,0},{2,1},{1,2},{4,3},{3,4},{6,5},{5,6},{8,7},{7,8},{10,9},{9,... | collective-permute-start | bytes 196616 | tf_op jit(solution)/shard_map/ppermute | solution.py:18
  48.2 5.4 %copy-start.2 = (s32[256,3]{0,1:T(4,128)S(1)}, s32[256,3]{0,1:T(4,128)}, u32[]{:S(2)}) copy-start(s32[256,3]{0,1:T(4,128)} %param.22) | copy-start | bytes 9220
  48.2 9.1 %collective-permute-start.4 = (bf16[256,256]{1,0:T(8,128)(2,1)S(1)}, bf16[256,256]{1,0:T(8,128)(2,1)S(1)}, u32[]{:S(2)}, u32[]{:S(2)}) collective-permute-start(bf16[256,256]{1,0:T(8,128)(2,1)S(1)} %shard_map.121), channel_id=1, source_target_pairs={{508,0},{5,1},{510,2},{7,3},{0,4},{9,5},{2,6},{11,7},{4,8},{13,9},... | collective-permute-start | bytes 393224 | tf_op jit(solution)/shard_map/ppermute | solution.py:18
  53.7 0.7 copy-start.3
  57.4 14.7 %copy-start = (bf16[1024,256]{1,0:T(8,128)(2,1)S(1)}, bf16[1024,256]{1,0:T(8,128)(2,1)}, u32[]{:S(2)}) copy-start(bf16[1024,256]{1,0:T(8,128)(2,1)} %basis_ref.1) | copy-start | bytes 1572868
  57.4 14.7 %copy-start.1 = (bf16[512,256]{1,0:T(8,128)(2,1)S(1)}, bf16[512,256]{1,0:T(8,128)(2,1)}, u32[]{:S(2)}) copy-start(bf16[512,256]{1,0:T(8,128)(2,1)} %e1_ref.1) | copy-start | bytes 786436
  57.7 14.3 %collective-permute-start.6 = (bf16[256,256]{1,0:T(8,128)(2,1)S(1)}, bf16[256,256]{1,0:T(8,128)(2,1)S(1)}, u32[]{:S(2)}, u32[]{:S(2)}) collective-permute-start(bf16[256,256]{1,0:T(8,128)(2,1)S(1)} %shard_map.123.mine_ref), channel_id=1, source_target_pairs={{1,0},{0,1},{3,2},{2,3},{5,4},{4,5},{7,6},{6,7},{9,8},{8,9},{11,10... | collective-permute-start | bytes 393224 | tf_op jit(solution)/shard_map/ppermute | solution.py:18

commit v5 on v4

--- a/solution.py
+++ b/solution.py
@@ -147,24 +147,24 @@
         move.wait()
 
 
-def second_body(pack_ref, got_ref, one_ref, two_ref, out_ref):
+def second_body(pack_ref, got_ref, two_ref, edge_ref, out_ref):
     first = (lax.axis_index("curve") & 1) == 0
     one = (pack_ref[256:384].astype(F32) + got_ref[256:384].astype(F32)).astype(BF16)
-    one_ref[...] = one
+    edge_ref[0:128] = one
+    edge_ref[128:256] = jnp.where(first, pack_ref[0:128], pack_ref[128:256])
     mine = pack_ref[896:1024]
     other = got_ref[896:1024]
     top = jnp.where(first, mine, other)
     bottom = jnp.where(first, other, mine)
     two_ref[...] = (nn(one[:, 0:128], top) + nn(one[:, 128:256], bottom)).astype(BF16)
-    out_ref[0:128] = jnp.where(first, pack_ref[0:128], got_ref[128:256])
-    out_ref[128:256] = jnp.where(first, pack_ref[128:256], pack_ref[0:128])
-    out_ref[256:384] = jnp.where(first, got_ref[0:128], pack_ref[128:256])
-    out_ref[384:640] = jnp.where(first, pack_ref[640:896], pack_ref[384:640])
-
-
-def bundle_body(one_ref, cross_ref, out_ref):
-    out_ref[0:128] = one_ref[...]
-    out_ref[128:256] = cross_ref[...]
+    out_ref[0:128] = jnp.where(first, pack_ref[128:256], got_ref[128:256])
+    out_ref[128:256] = jnp.where(first, got_ref[0:128], pack_ref[0:128])
+    out_ref[256:512] = jnp.where(first, pack_ref[640:896], pack_ref[384:640])
+
+
+def bundle_body(edge_ref, crossed_ref, out_ref):
+    out_ref[0:128] = edge_ref[0:128]
+    out_ref[128:256] = crossed_ref[0:128]
 
 
 def couple_two_body(near_ref, far_ref, weights_ref, out_hbm, value_ref, sems):
@@ -178,19 +178,16 @@
         move.wait()
 
 
-def gather_body(
+def near_body(
     points,
     rank,
     table_ref,
     leaf_ref,
-    got_ref,
-    cross_ref,
     c0_hbm,
     self_hbm,
     next_hbm,
     x_hbm,
     mask_ref,
-    zero_ref,
     weight_ref,
     field_ref,
     c0_ref,
@@ -203,68 +200,84 @@
     for i in range(2):
         rows = pl.ds(i * points, points)
         copies.append((self_hbm.at[rows], self_ref.at[rows]))
-        copies.append((next_hbm.at[rows], next_ref.at[rows]))
+    copies.append((next_hbm.at[pl.ds(0, points)], next_ref))
     copies.append((c0_hbm, c0_ref))
     moves = [pltpu.make_async_copy(a, b, sems.at[n]) for n, (a, b) in enumerate(copies)]
     for move in moves:
         move.start()
     device = lax.axis_index("curve")
     core = device & 1
-    first = core == 0
     clusters = table_ref.shape[1]
     own = device // 2
-    sign = jnp.where(first, -1, 1)
+    sign = jnp.where(core == 0, -1, 1)
     row = picked_row(table_ref[...], own)
     for s in range(3):
         for n in range(2):
             mask = offset_mask(row[s : s + 1], own, (n + 2) * sign, clusters)
             mask_ref[2 * s + n : 2 * s + n + 1] = jnp.broadcast_to(mask, (1, 256))
-
-    pieces = []
-    ahead = []
-    for h in range(2):
-        pieces.append(
-            jnp.where(
-                first,
-                cross_ref[384 + 128 * h : 512 + 128 * h],
-                got_ref[384 + 128 * h : 512 + 128 * h],
-            )
-        )
-        ahead.append(
-            jnp.where(
-                first,
-                got_ref[640 + 128 * h : 768 + 128 * h],
-                cross_ref[384 + 128 * h : 512 + 128 * h],
-            )
-        )
-    incoming = jnp.concatenate(pieces, 1).astype(F32).T
-    following = jnp.concatenate(
-        [ahead[0][:, 0:128], ahead[1][:, 0:128], ahead[0][:, 128:256], ahead[1][:, 128:256]], 0
-    )
     moves[0].wait()
     x0 = x_ref[0:points]
     x1 = x_ref[points : 2 * points]
     moves[1].wait()
+    moves[3].wait()
+    top = next_ref[...]
+    field_ref[0:points] = nn(self_ref[0:points], x0) + nn(top, x1)
+    inner = nn(x0.T, top).T
     moves[2].wait()
-    top = next_ref[0:points]
-    field_ref[0:points] = nn(self_ref[0:points], x0) + nn(top, x1) + incoming
-    inner = nn(x0.T, top).T
-    moves[3].wait()
+    field_ref[points : 2 * points] = nn(self_ref[points : 2 * points], x1) + inner
+    leaves = clusters * 4
     moves[4].wait()
-    field_ref[points : 2 * points] = (
-        nn(self_ref[points : 2 * points], x1)
-        + nn(next_ref[points : 2 * points], following)
-        + inner
-    )
-
-    leaves = clusters * 4
-    cross = [cross_ref[128 * n : 128 * (n + 1)].astype(F32) for n in range(3)]
-    partner = [got_ref[128 * n : 128 * (n + 1)].astype(F32) for n in range(2)]
+    weight = None
+    for i in range(2):
+        leaf = 2 * device + i
+        for s in range(3):
+            entry = leaf_ref[i : i + 1, s : s + 1]
+            edge = offset_mask(entry, leaf, 3 if i else -3, leaves)
+            edge = edge * jnp.where(core == (1 - i), 1.0, 0.0)
+            term = c0_ref[s, i * rank : (i + 1) * rank].astype(F32) * edge
+            weight = term if weight is None else weight + term
+    weight_ref[...] = weight.astype(BF16)
+
+
+def gather_body(
+    points,
+    rank,
+    leaf_ref,
+    got_ref,
+    edge_ref,
+    cross_ref,
+    c0_ref,
+    next_ref,
+    part_ref,
+    zero_ref,
+    field_ref,
+):
+    device = lax.axis_index("curve")
+    first = (device & 1) == 0
+    leaves = 2 * lax.axis_size("curve")
 
     def either(a, b):
         return jnp.where(first, a, b)
 
-    nothing = jnp.zeros_like(cross[0])
+    pieces = []
+    ahead = []
+    for h in range(2):
+        crossed = cross_ref[256 + 128 * h : 384 + 128 * h]
+        pieces.append(either(crossed, got_ref[384 + 128 * h : 512 + 128 * h]))
+        ahead.append(either(got_ref[640 + 128 * h : 768 + 128 * h], crossed))
+    incoming = jnp.concatenate(pieces, 1).astype(F32).T
+    following = jnp.concatenate(
+        [ahead[0][:, 0:128], ahead[1][:, 0:128], ahead[0][:, 128:256], ahead[1][:, 128:256]], 0
+    )
+    field_ref[0:points] = part_ref[0:points] + incoming
+    field_ref[points : 2 * points] = part_ref[points : 2 * points] + nn(
+        next_ref[points : 2 * points], following
+    )
+    edge = edge_ref[128:256].astype(F32)
+    rest = [cross_ref[128 * n : 128 * (n + 1)].astype(F32) for n in range(2)]
+    partner = [got_ref[128 * n : 128 * (n + 1)].astype(F32) for n in range(2)]
+    cross = (either(rest[0], edge), either(rest[1], rest[0]), either(edge, rest[1]))
+    nothing = jnp.zeros_like(edge)
     tables = (
         (
             (-3, either(cross[0], nothing)),
@@ -279,8 +292,6 @@
             (3, either(nothing, cross[2])),
         ),
     )
-    moves[5].wait()
-    weight = None
     for i in range(2):
         leaf = 2 * device + i
         total = None
@@ -290,18 +301,12 @@
             for offset, value in tables[i]:
                 term = value * offset_mask(entry, leaf, offset, leaves)
                 chosen = term if chosen is None else chosen + term
-            block = c0_ref[s, i * rank : (i + 1) * rank]
-            term = nn(chosen.astype(BF16), block)
+            term = nn(chosen.astype(BF16), c0_ref[s, i * rank : (i + 1) * rank])
             total = term if total is None else total + term
-            edge = offset_mask(entry, leaf, 3 if i else -3, leaves)
-            edge = edge * jnp.where(core == (1 - i), 1.0, 0.0)
-            term = block.astype(F32) * edge
-            weight = term if weight is None else weight + term
         zero_ref[128 * i : 128 * (i + 1)] = total
-    weight_ref[...] = weight.astype(BF16)
-
-
-def share_body(gathered_ref, near_ref, mask_ref, pack_ref, got_ref, cross_ref, out_ref):
+
+
+def share_body(gathered_ref, near_ref, mask_ref, pack_ref, got_ref, edge_ref, out_ref):
     first = (lax.axis_index("curve") & 1) == 0
     near = near_ref[0:128].astype(F32)
     far = near_ref[128:256].astype(F32)
@@ -323,7 +328,7 @@
     top = nt(total, jnp.where(first, mine, other))
     bottom = nt(total, jnp.where(first, other, mine))
     out_ref[0:128] = (one + jnp.concatenate([top, bottom], 1)).astype(BF16)
-    out_ref[128:256] = jnp.where(first, cross_ref[256:384], cross_ref[0:128])
+    out_ref[128:256] = edge_ref[128:256]
 
 
 def last_body(
@@ -403,16 +408,16 @@
     weights_two = lax.all_to_all(
         spread, "curve", 0, 0, axis_index_groups=cluster_groups(size)
     )
-    one, two, leaves = call(
+    two, edge, leaves = call(
         second_body,
-        [((128, 256), BF16), ((128, 256), BF16), ((640, 256), BF16)],
+        [((128, 256), BF16), ((256, 256), BF16), ((512, 256), BF16)],
         16 << 20,
         pack,
         got,
     )
     two_far = third_cluster(two)
     two_near = far_route(two, 8)
-    one_crossed = chip_swap(one)
+    edge_crossed = chip_swap(edge)
     crossed = chip_swap(leaves)
     (coupled,) = call(
         couple_two_body,
@@ -425,38 +430,51 @@
         scratch=[pltpu.VMEM((128, 256), BF16), pltpu.SemaphoreType.DMA((4,))],
     )
     gathered = lax.all_to_all(coupled, "curve", 0, 0, axis_index_groups=chip_groups(size))
-    (bundle,) = call(bundle_body, [((256, 256), BF16)], 1 << 18, one, one_crossed)
+    (bundle,) = call(bundle_body, [((256, 256), BF16)], 1 << 18, edge, edge_crossed)
     one_near = far_route(bundle, 2)
-    mask, far_zero, weight, field = call(
-        functools.partial(gather_body, points, rank),
-        [
-            ((8, 256), F32),
-            ((256, 256), F32),
-            ((256, 256), BF16),
-            ((2 * points, 128), F32),
-        ],
-        500 << 20,
+    mask, weight, part = call(
+        functools.partial(near_body, points, rank),
+        [((8, 256), F32), ((256, 256), BF16), ((2 * points, 128), F32)],
+        300 << 20,
         table_one,
         list_zero,
-        got,
-        crossed,
         c0,
         near_self,
         near_next,
         vectors,
-        far=range(4, 8),
+        far=range(2, 6),
         scratch=[
             pltpu.VMEM(c0.shape, BF16),
             pltpu.VMEM(near_self.shape, BF16),
-            pltpu.VMEM(near_next.shape, BF16),
+            pltpu.VMEM((points, points), BF16),
             pltpu.VMEM(vectors.shape, BF16),
-            pltpu.SemaphoreType.DMA((6,)),
+            pltpu.SemaphoreType.DMA((5,)),
         ],
     )
     (share,) = call(
-        share_body, [((256, 256), BF16)], 16 << 20, gathered, one_near, mask, pack, got, crossed
+        share_body,
+        [((256, 256), BF16)],
+        16 << 20,
+        gathered,
+        one_near,
+        mask,
+        pack,
+        got,
+        edge_crossed,
     )
     last = core_swap(share)
+    far_zero, field = call(
+        functools.partial(gather_body, points, rank),
+        [((256, 256), F32), ((2 * points, 128), F32)],
+        150 << 20,
+        list_zero,
+        got,
+        edge_crossed,
+        crossed,
+        c0,
+        near_next,
+        part,
+    )
     (out,) = call(
         functools.partial(last_body, points, rank),
         [((2 * points, 128), BF16)],

time: 74 us -> 69.6 us (0.941)
  waiting for transfers between devices: 8.93 us -> 3.76 us
    ppermute x7, waiting for transfers between devices: 8.92 us -> 3.76 us  [route(): lax.ppermute(value, 'curve', [(source_of(i) % size, i) for i in range(siz...]
    pallas_call x7 -> x8, Pallas kernels: 8.1 us -> 8.46 us  [call(): pl.pallas_call(body, out_shape=[jax.ShapeDtypeStruct(s, t) for s, t in ou...]
  transfers between devices with their start and end apart: 9 -> 9, of which waited for: 3 -> 3; matrix products, arithmetic and copies ran while one was open for 0% -> 0% of each run, Pallas kernels for 4% -> 6%
where the time goes in v5:
time: 69.6 us; the launch traced here: 69 us
  starting transfers between devices  55.7 us (80%)
  Pallas kernels  8.46 us (12%)
  waiting for transfers between devices  3.76 us (5%)
  local copies, waits for them, and re-layouts  0.86 us (1%)
    ppermute x7, starting transfers between devices, route(): lax.ppermute(value, 'curve', [(source_of(i) % size, i) for i in range(siz...  48.9 us
    pallas_call x8, Pallas kernels, call(): pl.pallas_call(body, out_shape=[jax.ShapeDtypeStruct(s, t) for s, t in ou...  8.46 us
    ppermute x7, waiting for transfers between devices, route(): lax.ppermute(value, 'curve', [(source_of(i) % size, i) for i in range(siz...  3.76 us
    all_to_all x1, starting transfers between devices, local_part(): lax.all_to_all(coupled, 'curve', 0, 0, axis_index_groups=chip_groups(size))  3.42 us
    all_to_all x1, starting transfers between devices, local_part(): lax.all_to_all(spread, 'curve', 0, 0, axis_index_groups=cluster_groups(si...  3.38 us
  transfers between devices with their start and end apart: 9, of which 3 were waited for; matrix products, arithmetic and copies ran while one was open for 0% of the time, Pallas kernels for 6%

profile of v5, /device:TPU:1, one launch (start us, length us, event | category | flops | bytes accessed | tf_op | source)
XLA Modules:
  0.0 69.0 jit_solution(11268713578465814355)
XLA Ops:
  0.0 2.2 %shard_map.118 = (bf16[1408,256]{1,0:T(8,128)(2,1)S(1)}, bf16[8,2,32,256]{3,2,1,0:T(8,128)(2,1)}) custom-call(s32[3,64]{1,0:T(4,128)} %bitcast.10, bf16[3,32,256]{2,1,0:T(8,128)(2,1)} %bitcast.9, bf16[1024,256]{1,0:T(8,128)(2,1)} %basis_ref.1, bf16[1024,128]{1,0:T(8,128)(2,1)} %x_hbm.3, bf16[512,256]{1,0:T(8,128)(2,1)} %e1_ref.1, ...), custom_call_target="tpu_custom_call" | custom-call | flops 167772160 | bytes 2409216 | tf_op jit(solution)/shard_map/pallas_call | solution.py:65
  2.2 8.7 %collective-permute-start = (bf16[1408,256]{1,0:T(8,128)(2,1)S(1)}, bf16[1408,256]{1,0:T(8,128)(2,1)S(1)}, u32[]{:S(2)}, u32[]{:S(2)}) collective-permute-start(bf16[1408,256]{1,0:T(8,128)(2,1)S(1)} %get-tuple-element.15.pack_ref), channel_id=1, source_target_pairs={{1,0},{0,1},{3,2},{2,3},{5,4},{4,5},{7,6},{6,7},{9,8},{8,9},{11,10... | collective-permute-start | bytes 2162696 | tf_op jit(solution)/shard_map/ppermute | solution.py:18
  11.0 3.4 %all-to-all-start = ((bf16[8,2,32,256]{3,2,1,0:T(8,128)(2,1)}), bf16[8,2,32,256]{3,2,1,0:T(8,128)(2,1)S(1)}, u32[]{:S(2)}, u32[]{:S(2)}) async-start(bf16[8,2,32,256]{3,2,1,0:T(8,128)(2,1)} %get-tuple-element.17), calls=%async_computation | async-start | bytes 524288 | tf_op jit(solution)/shard_map/all_to_all | solution.py:408
  14.4 0.0 collective-permute-done.got_ref
  14.4 0.2 shard_map.119
  14.6 5.9 %collective-permute-start.1 = (bf16[128,256]{1,0:T(8,128)(2,1)S(1)}, bf16[128,256]{1,0:T(8,128)(2,1)S(1)}, u32[]{:S(2)}, u32[]{:S(2)}) collective-permute-start(bf16[128,256]{1,0:T(8,128)(2,1)S(1)} %get-tuple-element.16), channel_id=1, source_target_pairs={{496,0},{17,1},{498,2},{19,3},{500,4},{21,5},{502,6},{23,7},{504,8... | collective-permute-start | bytes 196616 | tf_op jit(solution)/shard_map/ppermute | solution.py:18
  20.5 9.7 %collective-permute-start.2 = (bf16[128,256]{1,0:T(8,128)(2,1)S(1)}, bf16[128,256]{1,0:T(8,128)(2,1)S(1)}, u32[]{:S(2)}, u32[]{:S(2)}) collective-permute-start(bf16[128,256]{1,0:T(8,128)(2,1)S(1)} %get-tuple-element.16), channel_id=1, source_target_pairs={{492,0},{29,1},{494,2},{31,3},{488,4},{25,5},{490,6},{27,7},{500,8... | collective-permute-start | bytes 196616 | tf_op jit(solution)/shard_map/ppermute | solution.py:18
  30.2 0.0 all-to-all-done.weights_ref
  30.2 0.0 collective-permute-done.1.near_ref
  30.2 1.4 %collective-permute-done.2.far_ref = bf16[128,256]{1,0:T(8,128)(2,1)S(1)} collective-permute-done((bf16[128,256]{1,0:T(8,128)(2,1)S(1)}, bf16[128,256]{1,0:T(8,128)(2,1)S(1)}, u32[]{:S(2)}, u32[]{:S(2)}) %collective-permute-start.2) | collective-permute-done | bytes 65568 | tf_op jit(solution)/shard_map/ppermute | solution.py:18
  31.6 0.9 %shard_map.120 = bf16[4,128,256]{2,1,0:T(8,128)(2,1)} custom-call(bf16[128,256]{1,0:T(8,128)(2,1)S(1)} %collective-permute-done.1.near_ref, bf16[128,256]{1,0:T(8,128)(2,1)S(1)} %collective-permute-done.2.far_ref, bf16[8,2,32,256]{3,2,1,0:T(8,128)(2,1)S(1)} %all-to-all-done.weights_ref), custom_call_target="tpu_custom_call" | custom-call | flops 33554432 | bytes 393216 | tf_op jit(solution)/shard_map/pallas_call | solution.py:65
  32.5 3.4 %all-to-all-start.1 = ((bf16[4,128,256]{2,1,0:T(8,128)(2,1)}), bf16[4,128,256]{2,1,0:T(8,128)(2,1)S(1)}, u32[]{:S(2)}, u32[]{:S(2)}) async-start(bf16[4,128,256]{2,1,0:T(8,128)(2,1)} %shard_map.120), calls=%async_computation.1 | async-start | bytes 524288 | tf_op jit(solution)/shard_map/all_to_all | solution.py:432
  36.0 5.3 %collective-permute-start.3 = (bf16[256,256]{1,0:T(8,128)(2,1)S(1)}, bf16[256,256]{1,0:T(8,128)(2,1)S(1)}, u32[]{:S(2)}, u32[]{:S(2)}) collective-permute-start(bf16[256,256]{1,0:T(8,128)(2,1)S(1)} %get-tuple-element.18.edge_ref), channel_id=1, source_target_pairs={{511,0},{2,1},{1,2},{4,3},{3,4},{6,5},{5,6},{8,7},{7,8},{10,9},{9,... | collective-permute-start | bytes 393224 | tf_op jit(solution)/shard_map/ppermute | solution.py:18
  41.3 1.9 %collective-permute-start.6 = (bf16[512,256]{1,0:T(8,128)(2,1)S(1)}, bf16[512,256]{1,0:T(8,128)(2,1)S(1)}, u32[]{:S(2)}, u32[]{:S(2)}) collective-permute-start(bf16[512,256]{1,0:T(8,128)(2,1)S(1)} %get-tuple-element.20), channel_id=1, source_target_pairs={{511,0},{2,1},{1,2},{4,3},{3,4},{6,5},{5,6},{8,7},{7,8},{10,9},{9,... | collective-permute-start | bytes 786440 | tf_op jit(solution)/shard_map/ppermute | solution.py:18
  43.2 2.0 %collective-permute-done.3.crossed_ref.edge_ref = bf16[256,256]{1,0:T(8,128)(2,1)S(1)} collective-permute-done((bf16[256,256]{1,0:T(8,128)(2,1)S(1)}, bf16[256,256]{1,0:T(8,128)(2,1)S(1)}, u32[]{:S(2)}, u32[]{:S(2)}) %collective-permute-start.3) | collective-permute-done | bytes 131104 | tf_op jit(solution)/shard_map/ppermute | solution.py:18
  45.2 0.0 copy-start.5
  45.2 8.9 %collective-permute-start.4 = (bf16[256,256]{1,0:T(8,128)(2,1)S(1)}, bf16[256,256]{1,0:T(8,128)(2,1)S(1)}, u32[]{:S(2)}, u32[]{:S(2)}) collective-permute-start(bf16[256,256]{1,0:T(8,128)(2,1)S(1)} %shard_map.121), channel_id=1, source_target_pairs={{508,0},{5,1},{510,2},{7,3},{0,4},{9,5},{2,6},{11,7},{4,8},{13,9},... | collective-permute-start | bytes 393224 | tf_op jit(solution)/shard_map/ppermute | solution.py:18
  54.1 0.0 copy-start.4
  54.1 0.0 copy-done.5
  54.2 0.7 copy-done.4
  54.8 2.8 %shard_map.122 = (f32[8,256]{1,0:T(8,128)S(1)}, bf16[256,256]{1,0:T(8,128)(2,1)S(1)}, f32[1024,128]{1,0:T(8,128)S(1)}) custom-call(s32[3,256]{1,0:T(4,128)S(1)} %bitcast.7, s32[2,3]{1,0:T(2,128)S(1)} %copy-done.4, bf16[3,512,256]{2,1,0:T(8,128)(2,1)} %bitcast.5, bf16[1024,512]{1,0:T(8,128)(2,1)} %self_hbm.1, bf16[1024,512]{1,0:T(8,128)(2,1)} %next_ref.1, ...), custom_call_target="tpu_custom_call" | custom-call | flops 314572800 | bytes 3148824 | tf_op jit(solution)/shard_map/pallas_call | solution.py:65
  57.6 0.0 collective-permute-done.4.near_ref
  57.7 0.0 all-to-all-done.1.gathered_ref
  57.7 0.0 copy-start
  57.7 0.0 copy-start.1
  57.7 0.3 shard_map.123.mine_ref
  58.0 8.4 %collective-permute-start.5 = (bf16[256,256]{1,0:T(8,128)(2,1)S(1)}, bf16[256,256]{1,0:T(8,128)(2,1)S(1)}, u32[]{:S(2)}, u32[]{:S(2)}) collective-permute-start(bf16[256,256]{1,0:T(8,128)(2,1)S(1)} %shard_map.123.mine_ref), channel_id=1, source_target_pairs={{1,0},{0,1},{3,2},{2,3},{5,4},{4,5},{7,6},{6,7},{9,8},{8,9},{11,10... | collective-permute-start | bytes 393224 | tf_op jit(solution)/shard_map/ppermute | solution.py:18
  66.4 0.0 collective-permute-done.6.cross_ref
  66.5 0.0 copy-done
  66.5 0.0 copy-done.1
  66.5 0.0 copy-start.2
  66.5 0.0 copy-start.3
  66.5 0.6 shard_map.124
  67.1 0.3 collective-permute-done.5.got_ref
  67.4 0.1 copy-done.2
  67.5 0.1 copy-done.3
  67.6 1.4 %shard_map.125 = bf16[1024,128]{1,0:T(8,128)(2,1)} custom-call(bf16[256,256]{1,0:T(8,128)(2,1)S(1)} %shard_map.123.mine_ref, bf16[256,256]{1,0:T(8,128)(2,1)S(1)} %collective-permute-done.5.got_ref, f32[256,256]{1,0:T(8,128)S(1)} %get-tuple-element.22.zero_ref, bf16[256,256]{1,0:T(8,128)(2,1)S(1)} %get-tuple-element.23.weight_ref, ...), custom_call_target="tpu_custom_call" | custom-call | flops 125829120 | bytes 1966080 | tf_op jit(solution)/shard_map/pallas_call | solution.py:65
  (1 shorter events, 0.0 us)
Async XLA Ops:
  2.2 12.1 %collective-permute-start = (bf16[1408,256]{1,0:T(8,128)(2,1)S(1)}, bf16[1408,256]{1,0:T(8,128)(2,1)S(1)}, u32[]{:S(2)}, u32[]{:S(2)}) collective-permute-start(bf16[1408,256]{1,0:T(8,128)(2,1)S(1)} %get-tuple-element.15.pack_ref), channel_id=1, source_target_pairs={{1,0},{0,1},{3,2},{2,3},{5,4},{4,5},{7,6},{6,7},{9,8},{8,9},{11,10... | collective-permute-start | bytes 2162696 | tf_op jit(solution)/shard_map/ppermute | solution.py:18
  11.0 19.2 %all-to-all-start = ((bf16[8,2,32,256]{3,2,1,0:T(8,128)(2,1)}), bf16[8,2,32,256]{3,2,1,0:T(8,128)(2,1)S(1)}, u32[]{:S(2)}, u32[]{:S(2)}) async-start(bf16[8,2,32,256]{3,2,1,0:T(8,128)(2,1)} %get-tuple-element.17), calls=%async_computation | async-start | bytes 524288 | tf_op jit(solution)/shard_map/all_to_all | solution.py:408
  14.6 15.7 %collective-permute-start.1 = (bf16[128,256]{1,0:T(8,128)(2,1)S(1)}, bf16[128,256]{1,0:T(8,128)(2,1)S(1)}, u32[]{:S(2)}, u32[]{:S(2)}) collective-permute-start(bf16[128,256]{1,0:T(8,128)(2,1)S(1)} %get-tuple-element.16), channel_id=1, source_target_pairs={{496,0},{17,1},{498,2},{19,3},{500,4},{21,5},{502,6},{23,7},{504,8... | collective-permute-start | bytes 196616 | tf_op jit(solution)/shard_map/ppermute | solution.py:18
  20.5 11.1 %collective-permute-start.2 = (bf16[128,256]{1,0:T(8,128)(2,1)S(1)}, bf16[128,256]{1,0:T(8,128)(2,1)S(1)}, u32[]{:S(2)}, u32[]{:S(2)}) collective-permute-start(bf16[128,256]{1,0:T(8,128)(2,1)S(1)} %get-tuple-element.16), channel_id=1, source_target_pairs={{492,0},{29,1},{494,2},{31,3},{488,4},{25,5},{490,6},{27,7},{500,8... | collective-permute-start | bytes 196616 | tf_op jit(solution)/shard_map/ppermute | solution.py:18
  32.5 25.1 %all-to-all-start.1 = ((bf16[4,128,256]{2,1,0:T(8,128)(2,1)}), bf16[4,128,256]{2,1,0:T(8,128)(2,1)S(1)}, u32[]{:S(2)}, u32[]{:S(2)}) async-start(bf16[4,128,256]{2,1,0:T(8,128)(2,1)} %shard_map.120), calls=%async_computation.1 | async-start | bytes 524288 | tf_op jit(solution)/shard_map/all_to_all | solution.py:432
  36.0 9.2 %collective-permute-start.3 = (bf16[256,256]{1,0:T(8,128)(2,1)S(1)}, bf16[256,256]{1,0:T(8,128)(2,1)S(1)}, u32[]{:S(2)}, u32[]{:S(2)}) collective-permute-start(bf16[256,256]{1,0:T(8,128)(2,1)S(1)} %get-tuple-element.18.edge_ref), channel_id=1, source_target_pairs={{511,0},{2,1},{1,2},{4,3},{3,4},{6,5},{5,6},{8,7},{7,8},{10,9},{9,... | collective-permute-start | bytes 393224 | tf_op jit(solution)/shard_map/ppermute | solution.py:18
  41.3 25.2 %collective-permute-start.6 = (bf16[512,256]{1,0:T(8,128)(2,1)S(1)}, bf16[512,256]{1,0:T(8,128)(2,1)S(1)}, u32[]{:S(2)}, u32[]{:S(2)}) collective-permute-start(bf16[512,256]{1,0:T(8,128)(2,1)S(1)} %get-tuple-element.20), channel_id=1, source_target_pairs={{511,0},{2,1},{1,2},{4,3},{3,4},{6,5},{5,6},{8,7},{7,8},{10,9},{9,... | collective-permute-start | bytes 786440 | tf_op jit(solution)/shard_map/ppermute | solution.py:18
  45.2 8.9 %copy-start.5 = (s32[256,3]{0,1:T(4,128)S(1)}, s32[256,3]{0,1:T(4,128)}, u32[]{:S(2)}) copy-start(s32[256,3]{0,1:T(4,128)} %param.22) | copy-start | bytes 9220
  45.2 12.4 %collective-permute-start.4 = (bf16[256,256]{1,0:T(8,128)(2,1)S(1)}, bf16[256,256]{1,0:T(8,128)(2,1)S(1)}, u32[]{:S(2)}, u32[]{:S(2)}) collective-permute-start(bf16[256,256]{1,0:T(8,128)(2,1)S(1)} %shard_map.121), channel_id=1, source_target_pairs={{508,0},{5,1},{510,2},{7,3},{0,4},{9,5},{2,6},{11,7},{4,8},{13,9},... | collective-permute-start | bytes 393224 | tf_op jit(solution)/shard_map/ppermute | solution.py:18
  54.1 0.7 copy-start.4
  57.7 8.8 %copy-start = (bf16[1024,512]{1,0:T(8,128)(2,1)S(1)}, bf16[1024,512]{1,0:T(8,128)(2,1)}, u32[]{:S(2)}) copy-start(bf16[1024,512]{1,0:T(8,128)(2,1)} %next_ref.1) | copy-start | bytes 3145732
  57.7 8.8 %copy-start.1 = (bf16[512,3,256]{2,0,1:T(8,128)(2,1)S(1)}, bf16[512,3,256]{2,0,1:T(8,128)(2,1)}, u32[]{:S(2)}) copy-start(bf16[512,3,256]{2,0,1:T(8,128)(2,1)} %param.18) | copy-start | bytes 2359300
  58.0 9.4 %collective-permute-start.5 = (bf16[256,256]{1,0:T(8,128)(2,1)S(1)}, bf16[256,256]{1,0:T(8,128)(2,1)S(1)}, u32[]{:S(2)}, u32[]{:S(2)}) collective-permute-start(bf16[256,256]{1,0:T(8,128)(2,1)S(1)} %shard_map.123.mine_ref), channel_id=1, source_target_pairs={{1,0},{0,1},{3,2},{2,3},{5,4},{4,5},{7,6},{6,7},{9,8},{8,9},{11,10... | collective-permute-start | bytes 393224 | tf_op jit(solution)/shard_map/ppermute | solution.py:18
  66.5 1.0 %copy-start.2 = (bf16[1024,256]{1,0:T(8,128)(2,1)S(1)}, bf16[1024,256]{1,0:T(8,128)(2,1)}, u32[]{:S(2)}) copy-start(bf16[1024,256]{1,0:T(8,128)(2,1)} %basis_ref.1) | copy-start | bytes 1572868
  66.5 1.1 %copy-start.3 = (bf16[512,256]{1,0:T(8,128)(2,1)S(1)}, bf16[512,256]{1,0:T(8,128)(2,1)}, u32[]{:S(2)}) copy-start(bf16[512,256]{1,0:T(8,128)(2,1)} %e1_ref.1) | copy-start | bytes 786436

commit v6 on v5

--- a/solution.py
+++ b/solution.py
@@ -181,8 +181,8 @@
 def near_body(
     points,
     rank,
-    table_ref,
-    leaf_ref,
+    table_hbm,
+    leaf_hbm,
     c0_hbm,
     self_hbm,
     next_hbm,
@@ -190,6 +190,8 @@
     mask_ref,
     weight_ref,
     field_ref,
+    leaf_ref,
+    table_ref,
     c0_ref,
     self_ref,
     next_ref,
@@ -202,13 +204,17 @@
         copies.append((self_hbm.at[rows], self_ref.at[rows]))
     copies.append((next_hbm.at[pl.ds(0, points)], next_ref))
     copies.append((c0_hbm, c0_ref))
+    copies.append((table_hbm, table_ref))
+    copies.append((leaf_hbm, leaf_ref))
     moves = [pltpu.make_async_copy(a, b, sems.at[n]) for n, (a, b) in enumerate(copies)]
-    for move in moves:
+    for move in moves[-2:] + moves[:-2]:
         move.start()
     device = lax.axis_index("curve")
     core = device & 1
     clusters = table_ref.shape[1]
     own = device // 2
+    moves[5].wait()
+    moves[6].wait()
     sign = jnp.where(core == 0, -1, 1)
     row = picked_row(table_ref[...], own)
     for s in range(3):
@@ -432,9 +438,9 @@
     gathered = lax.all_to_all(coupled, "curve", 0, 0, axis_index_groups=chip_groups(size))
     (bundle,) = call(bundle_body, [((256, 256), BF16)], 1 << 18, edge, edge_crossed)
     one_near = far_route(bundle, 2)
-    mask, weight, part = call(
+    mask, weight, part, leaf_list = call(
         functools.partial(near_body, points, rank),
-        [((8, 256), F32), ((256, 256), BF16), ((2 * points, 128), F32)],
+        [((8, 256), F32), ((256, 256), BF16), ((2 * points, 128), F32), (list_zero.shape, I32)],
         300 << 20,
         table_one,
         list_zero,
@@ -442,13 +448,14 @@
         near_self,
         near_next,
         vectors,
-        far=range(2, 6),
+        far=range(6),
         scratch=[
+            pltpu.VMEM(table_one.shape, I32),
             pltpu.VMEM(c0.shape, BF16),
             pltpu.VMEM(near_self.shape, BF16),
             pltpu.VMEM((points, points), BF16),
             pltpu.VMEM(vectors.shape, BF16),
-            pltpu.SemaphoreType.DMA((5,)),
+            pltpu.SemaphoreType.DMA((7,)),
         ],
     )
     (share,) = call(
@@ -467,7 +474,7 @@
         functools.partial(gather_body, points, rank),
         [((256, 256), F32), ((2 * points, 128), F32)],
         150 << 20,
-        list_zero,
+        leaf_list,
         got,
         edge_crossed,
         crossed,

time: 69.6 us -> 69.5 us (level)
  no operation moved by 1% of the time
where the time goes in v6:
time: 69.5 us; the launch traced here: 69 us
  starting transfers between devices  56.3 us (81%)
  Pallas kernels  8.52 us (12%)
  waiting for transfers between devices  3.76 us (5%)
    ppermute x7, starting transfers between devices, route(): lax.ppermute(value, 'curve', [(source_of(i) % size, i) for i in range(siz...  49.5 us
    pallas_call x8, Pallas kernels, call(): pl.pallas_call(body, out_shape=[jax.ShapeDtypeStruct(s, t) for s, t in ou...  8.52 us
    ppermute x7, waiting for transfers between devices, route(): lax.ppermute(value, 'curve', [(source_of(i) % size, i) for i in range(siz...  3.76 us
    all_to_all x1, starting transfers between devices, local_part(): lax.all_to_all(coupled, 'curve', 0, 0, axis_index_groups=chip_groups(size))  3.42 us
    all_to_all x1, starting transfers between devices, local_part(): lax.all_to_all(spread, 'curve', 0, 0, axis_index_groups=cluster_groups(si...  3.38 us
  transfers between devices with their start and end apart: 9, of which 3 were waited for; matrix products, arithmetic and copies ran while one was open for 0% of the time, Pallas kernels for 6%

profile of v6, /device:TPU:1, one launch (start us, length us, event | category | flops | bytes accessed | tf_op | source)
XLA Modules:
  0.0 69.0 jit_solution(7185726055144423609)
XLA Ops:
  0.0 2.2 %shard_map.118 = (bf16[1408,256]{1,0:T(8,128)(2,1)S(1)}, bf16[8,2,32,256]{3,2,1,0:T(8,128)(2,1)}) custom-call(s32[3,64]{1,0:T(4,128)} %bitcast.10, bf16[3,32,256]{2,1,0:T(8,128)(2,1)} %bitcast.8, bf16[1024,256]{1,0:T(8,128)(2,1)} %basis_ref.1, bf16[1024,128]{1,0:T(8,128)(2,1)} %x_hbm.3, bf16[512,256]{1,0:T(8,128)(2,1)} %e1_ref.1, ...), custom_call_target="tpu_custom_call" | custom-call | flops 167772160 | bytes 2409216 | tf_op jit(solution)/shard_map/pallas_call | solution.py:65
  2.2 8.7 %collective-permute-start = (bf16[1408,256]{1,0:T(8,128)(2,1)S(1)}, bf16[1408,256]{1,0:T(8,128)(2,1)S(1)}, u32[]{:S(2)}, u32[]{:S(2)}) collective-permute-start(bf16[1408,256]{1,0:T(8,128)(2,1)S(1)} %get-tuple-element.16.pack_ref), channel_id=1, source_target_pairs={{1,0},{0,1},{3,2},{2,3},{5,4},{4,5},{7,6},{6,7},{9,8},{8,9},{11,10... | collective-permute-start | bytes 2162696 | tf_op jit(solution)/shard_map/ppermute | solution.py:18
  11.0 3.4 %all-to-all-start = ((bf16[8,2,32,256]{3,2,1,0:T(8,128)(2,1)}), bf16[8,2,32,256]{3,2,1,0:T(8,128)(2,1)S(1)}, u32[]{:S(2)}, u32[]{:S(2)}) async-start(bf16[8,2,32,256]{3,2,1,0:T(8,128)(2,1)} %get-tuple-element.18), calls=%async_computation | async-start | bytes 524288 | tf_op jit(solution)/shard_map/all_to_all | solution.py:414
  14.4 0.0 collective-permute-done.got_ref
  14.4 0.2 shard_map.119
  14.6 5.9 %collective-permute-start.1 = (bf16[128,256]{1,0:T(8,128)(2,1)S(1)}, bf16[128,256]{1,0:T(8,128)(2,1)S(1)}, u32[]{:S(2)}, u32[]{:S(2)}) collective-permute-start(bf16[128,256]{1,0:T(8,128)(2,1)S(1)} %get-tuple-element.17), channel_id=1, source_target_pairs={{496,0},{17,1},{498,2},{19,3},{500,4},{21,5},{502,6},{23,7},{504,8... | collective-permute-start | bytes 196616 | tf_op jit(solution)/shard_map/ppermute | solution.py:18
  20.5 9.7 %collective-permute-start.2 = (bf16[128,256]{1,0:T(8,128)(2,1)S(1)}, bf16[128,256]{1,0:T(8,128)(2,1)S(1)}, u32[]{:S(2)}, u32[]{:S(2)}) collective-permute-start(bf16[128,256]{1,0:T(8,128)(2,1)S(1)} %get-tuple-element.17), channel_id=1, source_target_pairs={{492,0},{29,1},{494,2},{31,3},{488,4},{25,5},{490,6},{27,7},{500,8... | collective-permute-start | bytes 196616 | tf_op jit(solution)/shard_map/ppermute | solution.py:18
  30.2 0.0 all-to-all-done.weights_ref
  30.2 0.0 collective-permute-done.1.near_ref
  30.2 1.4 %collective-permute-done.2.far_ref = bf16[128,256]{1,0:T(8,128)(2,1)S(1)} collective-permute-done((bf16[128,256]{1,0:T(8,128)(2,1)S(1)}, bf16[128,256]{1,0:T(8,128)(2,1)S(1)}, u32[]{:S(2)}, u32[]{:S(2)}) %collective-permute-start.2) | collective-permute-done | bytes 65568 | tf_op jit(solution)/shard_map/ppermute | solution.py:18
  31.6 0.9 %shard_map.120 = bf16[4,128,256]{2,1,0:T(8,128)(2,1)} custom-call(bf16[128,256]{1,0:T(8,128)(2,1)S(1)} %collective-permute-done.1.near_ref, bf16[128,256]{1,0:T(8,128)(2,1)S(1)} %collective-permute-done.2.far_ref, bf16[8,2,32,256]{3,2,1,0:T(8,128)(2,1)S(1)} %all-to-all-done.weights_ref), custom_call_target="tpu_custom_call" | custom-call | flops 33554432 | bytes 393216 | tf_op jit(solution)/shard_map/pallas_call | solution.py:65
  32.5 3.4 %all-to-all-start.1 = ((bf16[4,128,256]{2,1,0:T(8,128)(2,1)}), bf16[4,128,256]{2,1,0:T(8,128)(2,1)S(1)}, u32[]{:S(2)}, u32[]{:S(2)}) async-start(bf16[4,128,256]{2,1,0:T(8,128)(2,1)} %shard_map.120), calls=%async_computation.1 | async-start | bytes 524288 | tf_op jit(solution)/shard_map/all_to_all | solution.py:438
  36.0 5.3 %collective-permute-start.3 = (bf16[256,256]{1,0:T(8,128)(2,1)S(1)}, bf16[256,256]{1,0:T(8,128)(2,1)S(1)}, u32[]{:S(2)}, u32[]{:S(2)}) collective-permute-start(bf16[256,256]{1,0:T(8,128)(2,1)S(1)} %get-tuple-element.19.edge_ref), channel_id=1, source_target_pairs={{511,0},{2,1},{1,2},{4,3},{3,4},{6,5},{5,6},{8,7},{7,8},{10,9},{9,... | collective-permute-start | bytes 393224 | tf_op jit(solution)/shard_map/ppermute | solution.py:18
  41.3 1.9 %collective-permute-start.6 = (bf16[512,256]{1,0:T(8,128)(2,1)S(1)}, bf16[512,256]{1,0:T(8,128)(2,1)S(1)}, u32[]{:S(2)}, u32[]{:S(2)}) collective-permute-start(bf16[512,256]{1,0:T(8,128)(2,1)S(1)} %get-tuple-element.22), channel_id=1, source_target_pairs={{511,0},{2,1},{1,2},{4,3},{3,4},{6,5},{5,6},{8,7},{7,8},{10,9},{9,... | collective-permute-start | bytes 786440 | tf_op jit(solution)/shard_map/ppermute | solution.py:18
  43.2 2.0 %collective-permute-done.3.crossed_ref.edge_ref = bf16[256,256]{1,0:T(8,128)(2,1)S(1)} collective-permute-done((bf16[256,256]{1,0:T(8,128)(2,1)S(1)}, bf16[256,256]{1,0:T(8,128)(2,1)S(1)}, u32[]{:S(2)}, u32[]{:S(2)}) %collective-permute-start.3) | collective-permute-done | bytes 131104 | tf_op jit(solution)/shard_map/ppermute | solution.py:18
  45.2 8.9 %collective-permute-start.4 = (bf16[256,256]{1,0:T(8,128)(2,1)S(1)}, bf16[256,256]{1,0:T(8,128)(2,1)S(1)}, u32[]{:S(2)}, u32[]{:S(2)}) collective-permute-start(bf16[256,256]{1,0:T(8,128)(2,1)S(1)} %shard_map.121), channel_id=1, source_target_pairs={{508,0},{5,1},{510,2},{7,3},{0,4},{9,5},{2,6},{11,7},{4,8},{13,9},... | collective-permute-start | bytes 393224 | tf_op jit(solution)/shard_map/ppermute | solution.py:18
  54.1 2.9 %shard_map.122 = (f32[8,256]{1,0:T(8,128)S(1)}, bf16[256,256]{1,0:T(8,128)(2,1)S(1)}, f32[1024,128]{1,0:T(8,128)S(1)}, s32[2,3]{1,0:T(2,128)S(1)}) custom-call(s32[3,256]{1,0:T(4,128)} %bitcast.9, s32[2,3]{1,0:T(2,128)} %leaf_hbm.1, bf16[3,512,256]{2,1,0:T(8,128)(2,1)} %bitcast.5, bf16[1024,512]{1,0:T(8,128)(2,1)} %self_hbm.1, bf16[1024,512]{1,0:T(8,128)(2,1)} %next_ref.1, ...), custom_call_target="tpu_custom_call" | custom-call | flops 314572800 | bytes 3148824 | tf_op jit(solution)/shard_map/pallas_call | solution.py:65
  57.0 0.0 collective-permute-done.4.near_ref
  57.0 0.0 all-to-all-done.1.gathered_ref
  57.0 0.0 copy-start
  57.0 0.0 copy-start.1
  57.1 0.3 shard_map.123.mine_ref
  57.4 9.1 %collective-permute-start.5 = (bf16[256,256]{1,0:T(8,128)(2,1)S(1)}, bf16[256,256]{1,0:T(8,128)(2,1)S(1)}, u32[]{:S(2)}, u32[]{:S(2)}) collective-permute-start(bf16[256,256]{1,0:T(8,128)(2,1)S(1)} %shard_map.123.mine_ref), channel_id=1, source_target_pairs={{1,0},{0,1},{3,2},{2,3},{5,4},{4,5},{7,6},{6,7},{9,8},{8,9},{11,10... | collective-permute-start | bytes 393224 | tf_op jit(solution)/shard_map/ppermute | solution.py:18
  66.4 0.0 collective-permute-done.6.cross_ref
  66.4 0.0 copy-done
  66.5 0.0 copy-done.1
  66.5 0.0 copy-start.2
  66.5 0.0 copy-start.3
  66.5 0.6 shard_map.124
  67.1 0.3 collective-permute-done.5.got_ref
  67.4 0.1 copy-done.2
  67.5 0.1 copy-done.3
  67.6 1.4 %shard_map.125 = bf16[1024,128]{1,0:T(8,128)(2,1)} custom-call(bf16[256,256]{1,0:T(8,128)(2,1)S(1)} %shard_map.123.mine_ref, bf16[256,256]{1,0:T(8,128)(2,1)S(1)} %collective-permute-done.5.got_ref, f32[256,256]{1,0:T(8,128)S(1)} %get-tuple-element.24.zero_ref, bf16[256,256]{1,0:T(8,128)(2,1)S(1)} %get-tuple-element.25.weight_ref, ...), custom_call_target="tpu_custom_call" | custom-call | flops 125829120 | bytes 1966080 | tf_op jit(solution)/shard_map/pallas_call | solution.py:65
  (1 shorter events, 0.0 us)
Async XLA Ops:
  2.2 12.1 %collective-permute-start = (bf16[1408,256]{1,0:T(8,128)(2,1)S(1)}, bf16[1408,256]{1,0:T(8,128)(2,1)S(1)}, u32[]{:S(2)}, u32[]{:S(2)}) collective-permute-start(bf16[1408,256]{1,0:T(8,128)(2,1)S(1)} %get-tuple-element.16.pack_ref), channel_id=1, source_target_pairs={{1,0},{0,1},{3,2},{2,3},{5,4},{4,5},{7,6},{6,7},{9,8},{8,9},{11,10... | collective-permute-start | bytes 2162696 | tf_op jit(solution)/shard_map/ppermute | solution.py:18
  11.0 19.2 %all-to-all-start = ((bf16[8,2,32,256]{3,2,1,0:T(8,128)(2,1)}), bf16[8,2,32,256]{3,2,1,0:T(8,128)(2,1)S(1)}, u32[]{:S(2)}, u32[]{:S(2)}) async-start(bf16[8,2,32,256]{3,2,1,0:T(8,128)(2,1)} %get-tuple-element.18), calls=%async_computation | async-start | bytes 524288 | tf_op jit(solution)/shard_map/all_to_all | solution.py:414
  14.6 15.7 %collective-permute-start.1 = (bf16[128,256]{1,0:T(8,128)(2,1)S(1)}, bf16[128,256]{1,0:T(8,128)(2,1)S(1)}, u32[]{:S(2)}, u32[]{:S(2)}) collective-permute-start(bf16[128,256]{1,0:T(8,128)(2,1)S(1)} %get-tuple-element.17), channel_id=1, source_target_pairs={{496,0},{17,1},{498,2},{19,3},{500,4},{21,5},{502,6},{23,7},{504,8... | collective-permute-start | bytes 196616 | tf_op jit(solution)/shard_map/ppermute | solution.py:18
  20.5 11.1 %collective-permute-start.2 = (bf16[128,256]{1,0:T(8,128)(2,1)S(1)}, bf16[128,256]{1,0:T(8,128)(2,1)S(1)}, u32[]{:S(2)}, u32[]{:S(2)}) collective-permute-start(bf16[128,256]{1,0:T(8,128)(2,1)S(1)} %get-tuple-element.17), channel_id=1, source_target_pairs={{492,0},{29,1},{494,2},{31,3},{488,4},{25,5},{490,6},{27,7},{500,8... | collective-permute-start | bytes 196616 | tf_op jit(solution)/shard_map/ppermute | solution.py:18
  32.5 24.5 %all-to-all-start.1 = ((bf16[4,128,256]{2,1,0:T(8,128)(2,1)}), bf16[4,128,256]{2,1,0:T(8,128)(2,1)S(1)}, u32[]{:S(2)}, u32[]{:S(2)}) async-start(bf16[4,128,256]{2,1,0:T(8,128)(2,1)} %shard_map.120), calls=%async_computation.1 | async-start | bytes 524288 | tf_op jit(solution)/shard_map/all_to_all | solution.py:438
  36.0 9.2 %collective-permute-start.3 = (bf16[256,256]{1,0:T(8,128)(2,1)S(1)}, bf16[256,256]{1,0:T(8,128)(2,1)S(1)}, u32[]{:S(2)}, u32[]{:S(2)}) collective-permute-start(bf16[256,256]{1,0:T(8,128)(2,1)S(1)} %get-tuple-element.19.edge_ref), channel_id=1, source_target_pairs={{511,0},{2,1},{1,2},{4,3},{3,4},{6,5},{5,6},{8,7},{7,8},{10,9},{9,... | collective-permute-start | bytes 393224 | tf_op jit(solution)/shard_map/ppermute | solution.py:18
  41.3 25.2 %collective-permute-start.6 = (bf16[512,256]{1,0:T(8,128)(2,1)S(1)}, bf16[512,256]{1,0:T(8,128)(2,1)S(1)}, u32[]{:S(2)}, u32[]{:S(2)}) collective-permute-start(bf16[512,256]{1,0:T(8,128)(2,1)S(1)} %get-tuple-element.22), channel_id=1, source_target_pairs={{511,0},{2,1},{1,2},{4,3},{3,4},{6,5},{5,6},{8,7},{7,8},{10,9},{9,... | collective-permute-start | bytes 786440 | tf_op jit(solution)/shard_map/ppermute | solution.py:18
  45.2 11.8 %collective-permute-start.4 = (bf16[256,256]{1,0:T(8,128)(2,1)S(1)}, bf16[256,256]{1,0:T(8,128)(2,1)S(1)}, u32[]{:S(2)}, u32[]{:S(2)}) collective-permute-start(bf16[256,256]{1,0:T(8,128)(2,1)S(1)} %shard_map.121), channel_id=1, source_target_pairs={{508,0},{5,1},{510,2},{7,3},{0,4},{9,5},{2,6},{11,7},{4,8},{13,9},... | collective-permute-start | bytes 393224 | tf_op jit(solution)/shard_map/ppermute | solution.py:18
  57.0 9.4 %copy-start = (bf16[1024,512]{1,0:T(8,128)(2,1)S(1)}, bf16[1024,512]{1,0:T(8,128)(2,1)}, u32[]{:S(2)}) copy-start(bf16[1024,512]{1,0:T(8,128)(2,1)} %next_ref.1) | copy-start | bytes 3145732
  57.0 9.4 %copy-start.1 = (bf16[512,3,256]{2,0,1:T(8,128)(2,1)S(1)}, bf16[512,3,256]{2,0,1:T(8,128)(2,1)}, u32[]{:S(2)}) copy-start(bf16[512,3,256]{2,0,1:T(8,128)(2,1)} %param.18) | copy-start | bytes 2359300
  57.4 10.0 %collective-permute-start.5 = (bf16[256,256]{1,0:T(8,128)(2,1)S(1)}, bf16[256,256]{1,0:T(8,128)(2,1)S(1)}, u32[]{:S(2)}, u32[]{:S(2)}) collective-permute-start(bf16[256,256]{1,0:T(8,128)(2,1)S(1)} %shard_map.123.mine_ref), channel_id=1, source_target_pairs={{1,0},{0,1},{3,2},{2,3},{5,4},{4,5},{7,6},{6,7},{9,8},{8,9},{11,10... | collective-permute-start | bytes 393224 | tf_op jit(solution)/shard_map/ppermute | solution.py:18
  66.5 1.0 %copy-start.2 = (bf16[1024,256]{1,0:T(8,128)(2,1)S(1)}, bf16[1024,256]{1,0:T(8,128)(2,1)}, u32[]{:S(2)}) copy-start(bf16[1024,256]{1,0:T(8,128)(2,1)} %basis_ref.1) | copy-start | bytes 1572868
  66.5 1.1 %copy-start.3 = (bf16[512,256]{1,0:T(8,128)(2,1)S(1)}, bf16[512,256]{1,0:T(8,128)(2,1)}, u32[]{:S(2)}) copy-start(bf16[512,256]{1,0:T(8,128)(2,1)} %e1_ref.1) | copy-start | bytes 786436
